TPU v7x, 256 devices: a whole 4x4x8 slice. The times are simulated.
256 devices in a mesh: section: 8 (over x, z_lo), mp: 32 (over y, z_hi, core).
Axes of the slice: x: 4, y: 4, z: 8 (z_hi: 4, z_lo: 2; z = z_hi * 2 + z_lo), core: 2. Of those that a mesh axis runs over, the one named last changes fastest.
Arguments:
- enc_final: bfloat16 [8, 128, 4096], P('section', None, 'mp'), may hold values from -64 to 64
- enc_len: int32 [8], replicated, may hold values from 32 to 128, as said below
- kv_weight: bfloat16 [8, 4096, 2, 4096], P('section', None, None, 'mp'), may hold values from -1 to 1
- queries: bfloat16 [8, 8, 512, 4096], P('section', None, None, 'mp'), may hold values from -4096 to 4096
- d_context: bfloat16 [8, 8, 512, 4096], P('section', None, None, 'mp'), may hold values from -6 to 6
Outputs:
- context: bfloat16 [8, 8, 512, 4096], P('section', None, None, 'mp')
- query_grad: bfloat16 [8, 8, 512, 4096], P('section', None, None, 'mp')
- kv_weight_grad: bfloat16 [8, 4096, 2, 4096], P('section', None, None, 'mp')
- enc_grad: bfloat16 [8, 128, 4096], P('section', None, 'mp')
Inputs may be any that keep to these rules, and one draw needn't show every extreme that they name: `enc_len`: some microbatch has exactly 128 valid positions.
All inputs are finite; a program needn't handle non-finite values.
Results may differ from a plain program's by a relative error of at most 0.02.
Values may be sent and summed in bfloat16 or wider, within the bound.
No kernel may reach another device: no remote copies, remote signals or barrier semaphores. Data moves between devices by JAX's collectives and lax.ppermute only.
A program may use at most 128 MiB of HBM per device.

v0:
```python
import functools

import jax
import jax.numpy as jnp
from jax import lax
from jax.experimental import pallas as pl
from jax.experimental.pallas import tpu as pltpu
from jax.sharding import PartitionSpec as P

HD = 64
AXES = ("section", "mp")
BF = jnp.bfloat16
F32 = jnp.float32


def coords(i):
    section, mp = divmod(i, 32)
    x, zl = divmod(section, 2)
    y, zh, c = mp // 8, (mp // 2) % 4, mp % 2
    return x, y, 2 * zh + zl, c


def index(x, y, z, c):
    return ((x % 4) * 2 + z % 2) * 32 + (y % 4) * 8 + ((z % 8) // 2) * 2 + c


def shift(value, dx=0, dy=0, dz=0, dc=0):
    pairs = []
    for i in range(256):
        x, y, z, c = coords(i)
        pairs.append((i, index(x + dx, y + dy, z + dz, c ^ dc)))
    return lax.ppermute(value, AXES, pairs)


def cross(value, k, along):
    pairs = []
    for i in range(256):
        x, y, z, c = coords(i)
        dx, dy = (k, 0) if c == along else (0, k)
        pairs.append((i, index(x + dx, y + dy, z, c)))
    return lax.ppermute(value, AXES, pairs)


def nt(a, b):
    return lax.dot_general(a, b, (((1,), (1,)), ((), ())), preferred_element_type=F32)


def nn(a, b):
    return lax.dot_general(a, b, (((1,), (0,)), ((), ())), preferred_element_type=F32)


def tn(a, b):
    return lax.dot_general(a, b, (((0,), (0,)), ((), ())), preferred_element_type=F32)


def fetch(src, dst, sems):
    copies = [pltpu.make_async_copy(s, d, sems.at[i]) for i, (s, d) in enumerate(zip(src, dst))]
    for copy in copies:
        copy.start()
    return copies


def states_block(stack, dy, zh, z, c):
    rows = []
    for dx in range(4):
        outer, inner = c * dy + (1 - c) * dx, c * dx + (1 - c) * dy
        for zl in range(2):
            dz = (z + 8 - (2 * zh + zl)) & 7
            rows.append(stack[outer, inner, dz])
    return jnp.concatenate(rows, axis=0)


def fetch_weight(w, dst, start, slot, sem):
    return pltpu.make_async_copy(
        w.at[pl.ds(start, 4)], dst.at[pl.ds(start, 4)], sem.at[slot]
    )


def project_kernel(which, last, pos, *refs):
    n = len(which)
    x, y, z, c = pos[0], pos[1], pos[2], pos[3]
    pieces, refs = refs[:n], refs[n:]
    w_own, w_par, refs = refs[0], refs[1], refs[2:]
    if last:
        before, keep, send, stack, wo, wp, acc, sems, wsems = refs
    else:
        acc, stack, wo, wp, sems, wsems = refs

    def rows(copy_of):
        return [(y + 4 - dy) & 3 for dy in copy_of]

    def weights(copy_of):
        copies = []
        for i, yy in enumerate(rows(copy_of)):
            copies.append(
                (
                    fetch_weight(w_own, wo, yy * 4, 2 * i, wsems),
                    fetch_weight(w_par, wp, yy * 4, 2 * i + 1, wsems),
                )
            )
        for pair in copies:
            for copy in pair:
                copy.start()
        return copies

    copies = fetch(pieces, [stack.at[i] for i in range(n)], sems)
    if last:
        acc[...] = before[...]

    def block(copy_of, first, height, dxs, source):
        started = weights(copy_of)
        for copy in copies:
            copy.wait()
        sums = None
        for i, dy in enumerate(copy_of):
            yy = (y + 4 - dy) & 3
            lhs = jnp.concatenate(
                [
                    jnp.concatenate(
                        [
                            source(dx, dy)[(z + 8 - (2 * zh + zl)) & 7]
                            for dx in dxs
                            for zl in range(2)
                        ],
                        axis=0,
                    )
                    for zh in range(4)
                ],
                axis=1,
            )
            for copy in started[i]:
                copy.wait()
            own = nn(lhs, wo[pl.ds(yy * 4, 4)].reshape(1024, 256))
            par = nn(lhs, wp[pl.ds(yy * 4, 4)].reshape(1024, 256))
            sums = (own, par) if sums is None else (sums[0] + own, sums[1] + par)
        own, par = sums
        if last:
            own += acc[first : first + height, :256]
            par += acc[first : first + height, 256:]
        acc[first : first + height, :256] = own
        acc[first : first + height, 256:] = par

    @pl.when(c == 0)
    def _():
        first = which[0] * 128
        if not last:
            acc[...] = jnp.zeros_like(acc)
        block(range(4), first, n * 128, which, lambda dx, dy: stack.at[which.index(dx), dy])

    @pl.when(c == 1)
    def _():
        block(which, 0, 512, range(4), lambda dx, dy: stack.at[which.index(dy), dx])

    if last:
        for dx in range(4):
            for zl in range(2):
                m = ((x + 4 - dx) & 3) * 2 + zl
                row = (dx * 2 + zl) * 64
                keep[m] = acc[row : row + 64, :256].astype(BF)
                send[m] = acc[row : row + 64, 256:].astype(BF)


def attend_kernel(pos, lens, q_ref, d_ref, keep_ref, recv_ref, ctx_ref, qg_ref, own_ref, part_ref):
    c = pos[3]
    q = q_ref[0, 0]
    d = d_ref[0, 0]
    kv = jnp.concatenate([keep_ref[0], recv_ref[0]], axis=0)
    k, v = kv[:, :128], kv[:, 128:]
    left = lax.broadcasted_iota(jnp.int32, (128, 128), 1) < HD
    top = lax.broadcasted_iota(jnp.int32, (128, 128), 0) < HD
    zero = jnp.zeros((128, 128), BF)

    def stack_heads(t):
        return jnp.concatenate([jnp.where(left, t, zero), jnp.where(left, zero, t)], axis=0)

    def stack_heads_t(t):
        tt = t.T
        return jnp.concatenate([jnp.where(top, tt, zero), jnp.where(top, zero, tt)], axis=1)

    k_rows, v_rows = stack_heads(k), stack_heads(v)
    k_cols, v_cols = stack_heads_t(k), stack_heads_t(v)
    factor = HD ** (-0.5)
    source = (lax.broadcasted_iota(jnp.int32, (128, 512), 0) + 64 * c) & 127
    valid = source < lens[pl.program_id(0)]
    scores = nt(k_rows, q)
    prob_grad = nt(v_rows, d)
    probs, score_grads = [], []
    for h in range(2):
        s = jnp.where(valid, scores[h * 128 : h * 128 + 128] * factor, -1e30)
        e = jnp.exp(s - jnp.max(s, axis=0, keepdims=True))
        p = e * (1.0 / jnp.sum(e, axis=0, keepdims=True))
        g = prob_grad[h * 128 : h * 128 + 128]
        score_grads.append((p * (g - jnp.sum(g * p, axis=0, keepdims=True)) * factor).astype(BF))
        probs.append(p.astype(BF))
    prob = jnp.concatenate(probs, axis=0)
    score_grad = jnp.concatenate(score_grads, axis=0)
    ctx_ref[0, 0] = nn(v_cols, prob).astype(BF).T
    qg_ref[0, 0] = nn(k_cols, score_grad).astype(BF).T
    vg = nn(prob, d)
    kg = nn(score_grad, q)
    kg = jnp.where(left, kg[:128], kg[128:]).astype(BF)
    vg = jnp.where(left, vg[:128], vg[128:]).astype(BF)
    own_ref[0, :, :128] = kg[:64]
    own_ref[0, :, 128:] = vg[:64]
    part_ref[0, :, :128] = kg[64:]
    part_ref[0, :, 128:] = vg[64:]


def spread_kernel(which, after, pos, g_own, g_par, w_own, w_par, *refs):
    n = len(which)
    refs = refs[after:]
    outs, (wo, wp, wsems) = refs[:n], refs[n:]
    x, y, z, c = pos[0], pos[1], pos[2], pos[3]

    def block(dys, dxs, target):
        started = []
        for i, dy in enumerate(dys):
            yy = (y + dy) & 3
            pair = (
                fetch_weight(w_own, wo, yy * 4, 2 * i, wsems),
                fetch_weight(w_par, wp, yy * 4, 2 * i + 1, wsems),
            )
            for copy in pair:
                copy.start()
            started.append(pair)
        order = [(dx, zl, ((x + dx) & 3) * 2 + zl) for dx in dxs for zl in range(2)]
        own = jnp.concatenate([g_own[m] for _, _, m in order], axis=0)
        par = jnp.concatenate([g_par[m] for _, _, m in order], axis=0)
        for i, dy in enumerate(dys):
            yy = (y + dy) & 3
            for copy in started[i]:
                copy.wait()
            t = nt(own, wo[pl.ds(yy * 4, 4)].reshape(1024, 256))
            t = (t + nt(par, wp[pl.ds(yy * 4, 4)].reshape(1024, 256))).astype(BF)
            for j, (dx, zl, _) in enumerate(order):
                for zh in range(4):
                    target(dx, dy)[(2 * zh + zl + 8 - z) & 7] = t[
                        j * 64 : j * 64 + 64, zh * 256 : zh * 256 + 256
                    ]

    @pl.when(c == 0)
    def _():
        block(range(4), which, lambda dx, dy: outs[which.index(dx)].at[dy])

    @pl.when(c == 1)
    def _():
        block(which, range(4), lambda dx, dy: outs[which.index(dy)].at[dx])


def weight_kernel(pos, p0, p1, p2, p3, g_own, g_par, _, own_ref, par_ref, stack, sems):
    x, y, z, c = pos[0], pos[1], pos[2], pos[3]
    copies = fetch([p0, p1, p2, p3], [stack.at[i] for i in range(4)], sems)
    order = [((x + 4 - dx) & 3) * 2 + zl for dx in range(4) for zl in range(2)]
    own = jnp.concatenate([g_own[m] for m in order], axis=0)
    par = jnp.concatenate([g_par[m] for m in order], axis=0)
    for copy in copies:
        copy.wait()

    def step(i, _):
        dy = i // 4
        zh = i & 3
        lhs = states_block(stack, dy, zh, z, c)
        f = ((y + 4 - dy) & 3) * 4 + zh
        own_ref[f] = tn(lhs, own)
        par_ref[f] = tn(lhs, par).astype(BF)
        return 0

    lax.fori_loop(0, 16, step, 0)


SMEM = pl.BlockSpec(memory_space=pltpu.SMEM)
VMEM = pl.BlockSpec(memory_space=pltpu.VMEM)
HBM = pl.BlockSpec(memory_space=pl.ANY)


def stack_of(n):
    return pltpu.VMEM((n, 4, 8, 64, 256), BF)


WEIGHT = pltpu.VMEM((16, 256, 256), BF)


def whole(kernel, ins, outs, out_specs, scratch):
    return pl.pallas_call(
        kernel,
        in_specs=[SMEM] + ins,
        out_specs=out_specs,
        out_shape=[jax.ShapeDtypeStruct(s, d) for s, d in outs],
        scratch_shapes=scratch,
        compiler_params=pltpu.CompilerParams(vmem_limit_bytes=56 * 2**20),
    )


def sems(n):
    return pltpu.SemaphoreType.DMA((n,))


def spread(which, pos, own, par, w_own, w_par, after):
    return whole(
        functools.partial(spread_kernel, which, len(after)),
        [VMEM] * 2 + [HBM] * (2 + len(after)),
        [((4, 8, 64, 256), BF)] * len(which),
        [VMEM] * len(which),
        [WEIGHT, WEIGHT, sems(8)],
    )(pos, own, par, w_own, w_par, *after)


def attend(pos, lens, queries, d_context, keep, recv):
    wide = pl.BlockSpec((1, 1, 512, 128), lambda m, p, n: (0, m, 0, 0))
    kv = pl.BlockSpec((1, 64, 256), lambda m, p, n: (m, 0, 0))
    return pl.pallas_call(
        attend_kernel,
        grid_spec=pltpu.PrefetchScalarGridSpec(
            num_scalar_prefetch=2,
            grid=(8,),
            in_specs=[wide, wide, kv, kv],
            out_specs=[wide, wide, kv, kv],
        ),
        out_shape=[jax.ShapeDtypeStruct((1, 8, 512, 128), BF)] * 2
        + [jax.ShapeDtypeStruct((8, 64, 256), BF)] * 2,
        name="attend",
    )(pos, lens, queries, d_context, keep, recv)


def total(parts):
    return functools.reduce(lambda p, q: p + q, [p.astype(F32) for p in parts]).astype(BF)


def shards(enc_final, enc_len, kv_weight, queries, d_context):
    section, mp = lax.axis_index("section"), lax.axis_index("mp")
    c = mp % 2
    pos = jnp.stack([section // 2, mp // 8, ((mp // 2) % 4) * 2 + section % 2, c]).astype(jnp.int32)
    first = c == 0

    lower, upper = enc_final[0, :64], enc_final[0, 64:]
    mine = jnp.where(first, lower, upper)
    other = shift(jnp.where(first, upper, lower), dc=1)
    states = jnp.where(first, jnp.concatenate([mine, other], 1), jnp.concatenate([other, mine], 1))

    w_own = kv_weight.reshape(16, 256, 256)
    w_par = shift(w_own, dc=1)

    far = (2, 1, 3)
    line = jnp.stack([states] + [shift(states, dz=k) for k in range(1, 8)])
    got = {0: line}
    for k in far:
        got[k] = cross(line, k, 1)
    plane = jnp.stack([got[k] for k in range(4)])
    got = {0: plane}
    for k in far:
        got[k] = cross(plane, k, 0)
    pieces = [got[k] for k in range(4)]

    half = ((8, 64, 256), BF)
    (acc,) = whole(
        functools.partial(project_kernel, (0,), False),
        [HBM] * 3,
        [((512, 512), F32)],
        [VMEM],
        [stack_of(1), WEIGHT, WEIGHT, sems(1), sems(8)],
    )(pos, plane, w_own, w_par)
    keep, send = whole(
        functools.partial(project_kernel, (1, 2, 3), True),
        [HBM] * 5 + [VMEM],
        [half, half],
        [VMEM] * 2,
        [stack_of(3), WEIGHT, WEIGHT, pltpu.VMEM((512, 512), F32), sems(3), sems(8)],
    )(pos, *pieces[1:], w_own, w_par, acc)
    recv = shift(send, dc=1)
    context, query_grad, grad_keep, grad_send = attend(pos, enc_len, queries, d_context, keep, recv)
    grad_recv = shift(grad_send, dc=1)

    (part_2,) = spread((2,), pos, grad_keep, grad_recv, w_own, w_par, ())
    got_2 = cross(part_2, 2, 0)
    part_1, part_3 = spread((1, 3), pos, grad_keep, grad_recv, w_own, w_par, (part_2,))
    got_1 = cross(part_1, 1, 0)
    got_3 = cross(part_3, 3, 0)
    (part_0,) = spread((0,), pos, grad_keep, grad_recv, w_own, w_par, (part_1,))
    got = [part_0, got_1, got_2, got_3]

    grad_own, grad_par = whole(
        weight_kernel,
        [HBM] * 4 + [VMEM] * 2 + [HBM],
        [((16, 256, 256), F32), ((16, 256, 256), BF)],
        [VMEM] * 2,
        [stack_of(4), sems(4)],
    )(pos, *pieces, grad_keep, grad_recv, part_0)
    grad_other = shift(grad_par, dc=1)
    weight_grad = (grad_own + grad_other.astype(F32)).astype(BF).reshape(1, 4096, 2, 128)

    parts = [total([p[k] for p in got]) for k in range(4)]
    got = [parts[0]] + [cross(parts[k], k, 1) for k in far]
    got[0], weight_grad = lax.optimization_barrier((got[0], weight_grad))
    line = [total([p[k] for p in got]) for k in range(8)]
    rows = total([line[0]] + [shift(line[k], dz=k) for k in range(1, 8)])
    own = jnp.where(first, rows[:, :128], rows[:, 128:])
    other = shift(jnp.where(first, rows[:, 128:], rows[:, :128]), dc=1)
    enc_grad = jnp.where(first, jnp.concatenate([own, other], 0), jnp.concatenate([other, own], 0))
    return context, query_grad, weight_grad, enc_grad[None]


def solution(mesh):
    return jax.shard_map(
        shards,
        mesh=mesh,
        in_specs=(
            P("section", None, "mp"),
            P(),
            P("section", None, None, "mp"),
            P("section", None, None, "mp"),
            P("section", None, None, "mp"),
        ),
        out_specs=(
            P("section", None, None, "mp"),
            P("section", None, None, "mp"),
            P("section", None, None, "mp"),
            P("section", None, "mp"),
        ),
        check_vma=False,
    )
```

profile of v0, /device:TPU:1, one launch (start us, length us, event | category | flops | bytes accessed | tf_op | source)
XLA Modules:
  0.0 208.5 jit_solution(7528428685036573537)
XLA Ops:
  1.4 3.2 %collective-permute-start = (bf16[64,128]{1,0:T(8,128)(2,1)S(1)}, bf16[64,128]{1,0:T(8,128)(2,1)S(1)}, u32[]{:S(2)}, u32[]{:S(2)}) collective-permute-start(bf16[64,128]{1,0:T(8,128)(2,1)S(1)} %get-tuple-element.42), channel_id=1, source_target_pairs={{0,1},{1,0},{2,3},{3,2},{4,5},{5,4},{6,7},{7,6},{8,9},{9,8},{10,11... | collective-permute-start | bytes 49160 | tf_op jit(solution)/shard_map/ppermute | solution.py:32
  4.6 3.2 %reshape.218.refs_1_.refs_3_.w_own = bf16[16,256,256]{2,1,0:T(8,128)(2,1)S(1)} reshape(bf16[1,4096,2,128]{3,2,1,0:T(2,128)(2,1)} %param.7) | data formatting | bytes 4194304 | tf_op jit(solution)/shard_map/reshape | solution.py:340
  7.9 3.9 %collective-permute-start.7 = (bf16[64,256]{1,0:T(8,128)(2,1)S(1)}, bf16[64,256]{1,0:T(8,128)(2,1)S(1)}, u32[]{:S(2)}, u32[]{:S(2)}) collective-permute-start(bf16[64,256]{1,0:T(8,128)(2,1)S(1)} %maximum_select_fusion.1), channel_id=1, source_target_pairs={{0,38},{1,39},{2,32},{3,33},{4,34},{5,35},{6,36},{7,37},{8,46},{9,... | collective-permute-start | bytes 98312 | tf_op jit(solution)/shard_map/ppermute | solution.py:32
  18.6 3.7 %collective-permute-done.2 = bf16[64,256]{1,0:T(8,128)(2,1)S(1)} collective-permute-done((bf16[64,256]{1,0:T(8,128)(2,1)S(1)}, bf16[64,256]{1,0:T(8,128)(2,1)S(1)}, u32[]{:S(2)}, u32[]{:S(2)}) %collective-permute-start.2) | collective-permute-done | bytes 32800 | tf_op jit(solution)/shard_map/ppermute | solution.py:32
  23.4 5.1 %collective-permute-done.3 = bf16[64,256]{1,0:T(8,128)(2,1)S(1)} collective-permute-done((bf16[64,256]{1,0:T(8,128)(2,1)S(1)}, bf16[64,256]{1,0:T(8,128)(2,1)S(1)}, u32[]{:S(2)}, u32[]{:S(2)}) %collective-permute-start.3) | collective-permute-done | bytes 32800 | tf_op jit(solution)/shard_map/ppermute | solution.py:32
  28.4 4.3 %collective-permute-start.4 = (bf16[64,256]{1,0:T(8,128)(2,1)S(1)}, bf16[64,256]{1,0:T(8,128)(2,1)S(1)}, u32[]{:S(2)}, u32[]{:S(2)}) collective-permute-start(bf16[64,256]{1,0:T(8,128)(2,1)S(1)} %maximum_select_fusion.1), channel_id=1, source_target_pairs={{0,4},{1,5},{2,6},{3,7},{4,0},{5,1},{6,2},{7,3},{8,12},{9,13},{10,... | collective-permute-start | bytes 98312 | tf_op jit(solution)/shard_map/ppermute | solution.py:32
  38.9 5.0 %collective-permute-done.10 = bf16[8,64,256]{2,1,0:T(8,128)(2,1)S(1)} collective-permute-done((bf16[8,64,256]{2,1,0:T(8,128)(2,1)S(1)}, bf16[8,64,256]{2,1,0:T(8,128)(2,1)S(1)}, u32[]{:S(2)}, u32[]{:S(2)}) %collective-permute-start.10) | collective-permute-done | bytes 262176 | tf_op jit(solution)/shard_map/ppermute | solution.py:41
  47.4 3.1 %collective-permute-start.13 = (bf16[4,8,64,256]{3,2,1,0:T(8,128)(2,1)S(1)}, bf16[4,8,64,256]{3,2,1,0:T(8,128)(2,1)}, u32[]{:S(2)}, u32[]{:S(2)}) collective-permute-start(bf16[4,8,64,256]{3,2,1,0:T(8,128)(2,1)S(1)} %pad_maximum_fusion.refs_0_.p0), channel_id=1, source_target_pairs={{0,192},{1,25},{2,194},{3,27},{4,196},{5,29},{6,198},{7,31},{8,200... | collective-permute-start | bytes 3145736 | tf_op jit(solution)/shard_map/ppermute | solution.py:41
  52.1 4.0 %shard_map.84.refs_5_ = f32[512,512]{1,0:T(8,128)} custom-call(s32[4]{0:T(128)} %pad_add_fusion.pos, bf16[4,8,64,256]{3,2,1,0:T(8,128)(2,1)} %copy-done.1, bf16[16,256,256]{2,1,0:T(8,128)(2,1)} %copy-done, bf16[16,256,256]{2,1,0:T(8,128)(2,1)} %collective-permute-done.14.refs_2_.refs_4_.w_par), custom_call_target="tpu_custom_call" | custom-call | tf_op jit(solution)/shard_map/pallas_call | solution.py:355
  56.0 17.5 %collective-permute-done.13.refs_2_.p3 = bf16[4,8,64,256]{3,2,1,0:T(8,128)(2,1)} collective-permute-done((bf16[4,8,64,256]{3,2,1,0:T(8,128)(2,1)S(1)}, bf16[4,8,64,256]{3,2,1,0:T(8,128)(2,1)}, u32[]{:S(2)}, u32[]{:S(2)}) %collective-permute-start.13) | collective-permute-done | bytes 1048608 | tf_op jit(solution)/shard_map/ppermute | solution.py:41
  73.5 3.6 %collective-permute-done.11.refs_0_.p1 = bf16[4,8,64,256]{3,2,1,0:T(8,128)(2,1)} collective-permute-done((bf16[4,8,64,256]{3,2,1,0:T(8,128)(2,1)S(1)}, bf16[4,8,64,256]{3,2,1,0:T(8,128)(2,1)}, u32[]{:S(2)}, u32[]{:S(2)}) %collective-permute-start.11) | collective-permute-done | bytes 1048608 | tf_op jit(solution)/shard_map/ppermute | solution.py:41
  77.1 6.5 %shard_map.85 = (bf16[8,64,256]{2,1,0:T(8,128)(2,1)}, bf16[8,64,256]{2,1,0:T(8,128)(2,1)}) custom-call(s32[4]{0:T(128)} %pad_add_fusion.pos, bf16[4,8,64,256]{3,2,1,0:T(8,128)(2,1)} %collective-permute-done.11.refs_0_.p1, bf16[4,8,64,256]{3,2,1,0:T(8,128)(2,1)} %collective-permute-done.12.refs_1_.p2, ...), custom_call_target="tpu_custom_call" | custom-call | tf_op jit(solution)/shard_map/pallas_call | solution.py:362
  83.7 21.1 %collective-permute-start.15 = (bf16[8,64,256]{2,1,0:T(8,128)(2,1)}, bf16[8,64,256]{2,1,0:T(8,128)(2,1)S(1)}, u32[]{:S(2)}, u32[]{:S(2)}) collective-permute-start(bf16[8,64,256]{2,1,0:T(8,128)(2,1)} %get-tuple-element.17), channel_id=1, source_target_pairs={{0,1},{1,0},{2,3},{3,2},{4,5},{5,4},{6,7},{7,6},{8,9},{9,8},{10,11... | collective-permute-start | bytes 786440 | tf_op jit(solution)/shard_map/ppermute | solution.py:32
  106.8 9.5 %attend.1 = (bf16[1,8,512,128]{3,2,1,0:T(8,128)(2,1)}, bf16[1,8,512,128]{3,2,1,0:T(8,128)(2,1)}, bf16[8,64,256]{2,1,0:T(8,128)(2,1)}, bf16[8,64,256]{2,1,0:T(8,128)(2,1)}) custom-call(s32[4]{0:T(128)} %pad_add_fusion.pos, s32[8]{0:T(128)} %lens.1, bf16[1,8,512,128]{3,2,1,0:T(8,128)(2,1)} %q_ref.1, bf16[1,8,512,128]{3,2,1,0:T(8,128)(2,1)} %d_ref.1, ...), custom_call_target="tpu_custom_call" | custom-call | tf_op jit(solution)/shard_map/attend/pallas_call | solution.py:311
  118.9 4.0 %shard_map.86.refs_0_ = bf16[4,8,64,256]{3,2,1,0:T(8,128)(2,1)} custom-call(s32[4]{0:T(128)} %pad_add_fusion.pos, bf16[8,64,256]{2,1,0:T(8,128)(2,1)} %get-tuple-element.20.g_own, bf16[8,64,256]{2,1,0:T(8,128)(2,1)} %copy-done.3, bf16[16,256,256]{2,1,0:T(8,128)(2,1)} %copy-done, bf16[16,256,256]{2,1,0:T(8,128)(2,1)} %collective-permute-done.14.refs_2_.refs_4_.w_par), custom_call_target="tpu_custom_call" | custom-call | tf_op jit(solution)/shard_map/pallas_call | solution.py:299
  122.9 5.1 %shard_map.87 = (bf16[4,8,64,256]{3,2,1,0:T(8,128)(2,1)}, bf16[4,8,64,256]{3,2,1,0:T(8,128)(2,1)}) custom-call(s32[4]{0:T(128)} %pad_add_fusion.pos, bf16[8,64,256]{2,1,0:T(8,128)(2,1)} %get-tuple-element.20.g_own, bf16[8,64,256]{2,1,0:T(8,128)(2,1)} %copy-done.3, bf16[16,256,256]{2,1,0:T(8,128)(2,1)} %copy-done, ...), custom_call_target="tpu_custom_call" | custom-call | tf_op jit(solution)/shard_map/pallas_call | solution.py:299
  128.1 4.1 %shard_map.88._ = bf16[4,8,64,256]{3,2,1,0:T(8,128)(2,1)} custom-call(s32[4]{0:T(128)} %pad_add_fusion.pos, bf16[8,64,256]{2,1,0:T(8,128)(2,1)} %get-tuple-element.20.g_own, bf16[8,64,256]{2,1,0:T(8,128)(2,1)} %copy-done.3, bf16[16,256,256]{2,1,0:T(8,128)(2,1)} %copy-done, bf16[16,256,256]{2,1,0:T(8,128)(2,1)} %collective-permute-done.14.refs_2_.refs_4_.w_par, ...), custom_call_target="tpu_custom_call" | custom-call | tf_op jit(solution)/shard_map/pallas_call | solution.py:299
  132.2 11.7 %shard_map.89 = (f32[16,256,256]{2,1,0:T(8,128)}, bf16[16,256,256]{2,1,0:T(8,128)(2,1)}) custom-call(s32[4]{0:T(128)} %pad_add_fusion.pos, bf16[4,8,64,256]{3,2,1,0:T(8,128)(2,1)} %copy-done.1, bf16[4,8,64,256]{3,2,1,0:T(8,128)(2,1)} %collective-permute-done.11.refs_0_.p1, bf16[4,8,64,256]{3,2,1,0:T(8,128)(2,1)} %collective-permute-done.12.refs_1_.p2, ...), custom_call_target="tpu_custom_call" | custom-call | tf_op jit(solution)/shard_map/pallas_call | solution.py:381
  143.8 3.2 %collective-permute-start.20 = (bf16[16,256,256]{2,1,0:T(8,128)(2,1)}, bf16[16,256,256]{2,1,0:T(8,128)(2,1)S(1)}, u32[]{:S(2)}, u32[]{:S(2)}) collective-permute-start(bf16[16,256,256]{2,1,0:T(8,128)(2,1)} %get-tuple-element.25), channel_id=1, source_target_pairs={{0,1},{1,0},{2,3},{3,2},{4,5},{5,4},{6,7},{7,6},{8,9},{9,8},{10,11... | collective-permute-start | bytes 6291464 | tf_op jit(solution)/shard_map/ppermute | solution.py:32
  148.6 13.9 %collective-permute-done.18 = bf16[4,8,64,256]{3,2,1,0:T(8,128)(2,1)S(1)} collective-permute-done((bf16[4,8,64,256]{3,2,1,0:T(8,128)(2,1)S(1)}, bf16[4,8,64,256]{3,2,1,0:T(8,128)(2,1)S(1)}, u32[]{:S(2)}, u32[]{:S(2)}) %collective-permute-start.18) | collective-permute-done | bytes 1048608 | tf_op jit(solution)/shard_map/ppermute | solution.py:41
  162.5 8.1 %collective-permute-done.19 = bf16[4,8,64,256]{3,2,1,0:T(8,128)(2,1)S(1)} collective-permute-done((bf16[4,8,64,256]{3,2,1,0:T(8,128)(2,1)S(1)}, bf16[4,8,64,256]{3,2,1,0:T(8,128)(2,1)S(1)}, u32[]{:S(2)}, u32[]{:S(2)}) %collective-permute-start.19) | collective-permute-done | bytes 1048608 | tf_op jit(solution)/shard_map/ppermute | solution.py:41
  186.3 3.8 %collective-permute-start.27 = (bf16[64,256]{1,0:T(8,128)(2,1)S(1)}, bf16[64,256]{1,0:T(8,128)(2,1)S(1)}, u32[]{:S(2)}, u32[]{:S(2)}) collective-permute-start(bf16[64,256]{1,0:T(8,128)(2,1)S(1)} %get-tuple-element.37), channel_id=1, source_target_pairs={{0,4},{1,5},{2,6},{3,7},{4,0},{5,1},{6,2},{7,3},{8,12},{9,13},{10,... | collective-permute-start | bytes 98312 | tf_op jit(solution)/shard_map/ppermute | solution.py:32
  196.1 4.5 %collective-permute-start.28 = (bf16[64,256]{1,0:T(8,128)(2,1)S(1)}, bf16[64,256]{1,0:T(8,128)(2,1)S(1)}, u32[]{:S(2)}, u32[]{:S(2)}) collective-permute-start(bf16[64,256]{1,0:T(8,128)(2,1)S(1)} %get-tuple-element.35), channel_id=1, source_target_pairs={{0,36},{1,37},{2,38},{3,39},{4,32},{5,33},{6,34},{7,35},{8,44},{9,... | collective-permute-start | bytes 98312 | tf_op jit(solution)/shard_map/ppermute | solution.py:32
  202.4 4.7 %collective-permute-start.31 = (bf16[64,128]{1,0:T(8,128)(2,1)S(1)}, bf16[64,128]{1,0:T(8,128)(2,1)S(1)}, u32[]{:S(2)}, u32[]{:S(2)}) collective-permute-start(bf16[64,128]{1,0:T(8,128)(2,1)S(1)} %get-tuple-element.40), channel_id=1, source_target_pairs={{0,1},{1,0},{2,3},{3,2},{4,5},{5,4},{6,7},{7,6},{8,9},{9,8},{10,11... | collective-permute-start | bytes 49160 | tf_op jit(solution)/shard_map/ppermute | solution.py:32
  (86 shorter events, 50.9 us)
Async XLA Ops:
  7.8 44.3 %collective-permute-start.14 = (bf16[16,256,256]{2,1,0:T(8,128)(2,1)S(1)}, bf16[16,256,256]{2,1,0:T(8,128)(2,1)}, u32[]{:S(2)}, u32[]{:S(2)}) collective-permute-start(bf16[16,256,256]{2,1,0:T(8,128)(2,1)S(1)} %reshape.218.refs_1_.refs_3_.w_own), channel_id=1, source_target_pairs={{0,1},{1,0},{2,3},{3,2},{4,5},{5,4},{6,7},{7,6},{8,9},{9,8},{10,11... | collective-permute-start | bytes 6291464 | tf_op jit(solution)/shard_map/ppermute | solution.py:32
  7.9 27.3 %collective-permute-start.7 = (bf16[64,256]{1,0:T(8,128)(2,1)S(1)}, bf16[64,256]{1,0:T(8,128)(2,1)S(1)}, u32[]{:S(2)}, u32[]{:S(2)}) collective-permute-start(bf16[64,256]{1,0:T(8,128)(2,1)S(1)} %maximum_select_fusion.1), channel_id=1, source_target_pairs={{0,38},{1,39},{2,32},{3,33},{4,34},{5,35},{6,36},{7,37},{8,46},{9,... | collective-permute-start | bytes 98312 | tf_op jit(solution)/shard_map/ppermute | solution.py:32
  11.8 23.3 %collective-permute-start.6 = (bf16[64,256]{1,0:T(8,128)(2,1)S(1)}, bf16[64,256]{1,0:T(8,128)(2,1)S(1)}, u32[]{:S(2)}, u32[]{:S(2)}) collective-permute-start(bf16[64,256]{1,0:T(8,128)(2,1)S(1)} %maximum_select_fusion.1), channel_id=1, source_target_pairs={{0,6},{1,7},{2,0},{3,1},{4,2},{5,3},{6,4},{7,5},{8,14},{9,15},{10,... | collective-permute-start | bytes 98312 | tf_op jit(solution)/shard_map/ppermute | solution.py:32
  13.0 22.1 %collective-permute-start.5 = (bf16[64,256]{1,0:T(8,128)(2,1)S(1)}, bf16[64,256]{1,0:T(8,128)(2,1)S(1)}, u32[]{:S(2)}, u32[]{:S(2)}) collective-permute-start(bf16[64,256]{1,0:T(8,128)(2,1)S(1)} %maximum_select_fusion.1), channel_id=1, source_target_pairs={{0,36},{1,37},{2,38},{3,39},{4,32},{5,33},{6,34},{7,35},{8,44},{9,... | collective-permute-start | bytes 98312 | tf_op jit(solution)/shard_map/ppermute | solution.py:32
  28.4 6.7 %collective-permute-start.4 = (bf16[64,256]{1,0:T(8,128)(2,1)S(1)}, bf16[64,256]{1,0:T(8,128)(2,1)S(1)}, u32[]{:S(2)}, u32[]{:S(2)}) collective-permute-start(bf16[64,256]{1,0:T(8,128)(2,1)S(1)} %maximum_select_fusion.1), channel_id=1, source_target_pairs={{0,4},{1,5},{2,6},{3,7},{4,0},{5,1},{6,2},{7,3},{8,12},{9,13},{10,... | collective-permute-start | bytes 98312 | tf_op jit(solution)/shard_map/ppermute | solution.py:32
  35.2 8.7 %collective-permute-start.10 = (bf16[8,64,256]{2,1,0:T(8,128)(2,1)S(1)}, bf16[8,64,256]{2,1,0:T(8,128)(2,1)S(1)}, u32[]{:S(2)}, u32[]{:S(2)}) collective-permute-start(bf16[8,64,256]{2,1,0:T(8,128)(2,1)S(1)} %bitcast_dynamic-update-slice_fusion), channel_id=1, source_target_pairs={{0,24},{1,193},{2,26},{3,195},{4,28},{5,197},{6,30},{7,199},{8,0},... | collective-permute-start | bytes 786440 | tf_op jit(solution)/shard_map/ppermute | solution.py:41
  37.7 6.8 %collective-permute-start.9 = (bf16[8,64,256]{2,1,0:T(8,128)(2,1)S(1)}, bf16[8,64,256]{2,1,0:T(8,128)(2,1)S(1)}, u32[]{:S(2)}, u32[]{:S(2)}) collective-permute-start(bf16[8,64,256]{2,1,0:T(8,128)(2,1)S(1)} %bitcast_dynamic-update-slice_fusion), channel_id=1, source_target_pairs={{0,16},{1,129},{2,18},{3,131},{4,20},{5,133},{6,22},{7,135},{8,24}... | collective-permute-start | bytes 786440 | tf_op jit(solution)/shard_map/ppermute | solution.py:41
  38.2 9.0 %collective-permute-start.8 = (bf16[8,64,256]{2,1,0:T(8,128)(2,1)S(1)}, bf16[8,64,256]{2,1,0:T(8,128)(2,1)S(1)}, u32[]{:S(2)}, u32[]{:S(2)}) collective-permute-start(bf16[8,64,256]{2,1,0:T(8,128)(2,1)S(1)} %bitcast_dynamic-update-slice_fusion), channel_id=1, source_target_pairs={{0,8},{1,65},{2,10},{3,67},{4,12},{5,69},{6,14},{7,71},{8,16},{9,7... | collective-permute-start | bytes 786440 | tf_op jit(solution)/shard_map/ppermute | solution.py:41
  47.4 26.1 %collective-permute-start.13 = (bf16[4,8,64,256]{3,2,1,0:T(8,128)(2,1)S(1)}, bf16[4,8,64,256]{3,2,1,0:T(8,128)(2,1)}, u32[]{:S(2)}, u32[]{:S(2)}) collective-permute-start(bf16[4,8,64,256]{3,2,1,0:T(8,128)(2,1)S(1)} %pad_maximum_fusion.refs_0_.p0), channel_id=1, source_target_pairs={{0,192},{1,25},{2,194},{3,27},{4,196},{5,29},{6,198},{7,31},{8,200... | collective-permute-start | bytes 3145736 | tf_op jit(solution)/shard_map/ppermute | solution.py:41
  50.5 23.0 %collective-permute-start.12 = (bf16[4,8,64,256]{3,2,1,0:T(8,128)(2,1)S(1)}, bf16[4,8,64,256]{3,2,1,0:T(8,128)(2,1)}, u32[]{:S(2)}, u32[]{:S(2)}) collective-permute-start(bf16[4,8,64,256]{3,2,1,0:T(8,128)(2,1)S(1)} %pad_maximum_fusion.refs_0_.p0), channel_id=1, source_target_pairs={{0,128},{1,17},{2,130},{3,19},{4,132},{5,21},{6,134},{7,23},{8,136... | collective-permute-start | bytes 3145736 | tf_op jit(solution)/shard_map/ppermute | solution.py:41
  50.6 26.5 %collective-permute-start.11 = (bf16[4,8,64,256]{3,2,1,0:T(8,128)(2,1)S(1)}, bf16[4,8,64,256]{3,2,1,0:T(8,128)(2,1)}, u32[]{:S(2)}, u32[]{:S(2)}) collective-permute-start(bf16[4,8,64,256]{3,2,1,0:T(8,128)(2,1)S(1)} %pad_maximum_fusion.refs_0_.p0), channel_id=1, source_target_pairs={{0,64},{1,9},{2,66},{3,11},{4,68},{5,13},{6,70},{7,15},{8,72},{9,1... | collective-permute-start | bytes 3145736 | tf_op jit(solution)/shard_map/ppermute | solution.py:41
  83.7 22.4 %collective-permute-start.15 = (bf16[8,64,256]{2,1,0:T(8,128)(2,1)}, bf16[8,64,256]{2,1,0:T(8,128)(2,1)S(1)}, u32[]{:S(2)}, u32[]{:S(2)}) collective-permute-start(bf16[8,64,256]{2,1,0:T(8,128)(2,1)} %get-tuple-element.17), channel_id=1, source_target_pairs={{0,1},{1,0},{2,3},{3,2},{4,5},{5,4},{6,7},{7,6},{8,9},{9,8},{10,11... | collective-permute-start | bytes 786440 | tf_op jit(solution)/shard_map/ppermute | solution.py:32
  143.8 32.4 %collective-permute-start.20 = (bf16[16,256,256]{2,1,0:T(8,128)(2,1)}, bf16[16,256,256]{2,1,0:T(8,128)(2,1)S(1)}, u32[]{:S(2)}, u32[]{:S(2)}) collective-permute-start(bf16[16,256,256]{2,1,0:T(8,128)(2,1)} %get-tuple-element.25), channel_id=1, source_target_pairs={{0,1},{1,0},{2,3},{3,2},{4,5},{5,4},{6,7},{7,6},{8,9},{9,8},{10,11... | collective-permute-start | bytes 6291464 | tf_op jit(solution)/shard_map/ppermute | solution.py:32
  147.0 15.5 %collective-permute-start.18 = (bf16[4,8,64,256]{3,2,1,0:T(8,128)(2,1)S(1)}, bf16[4,8,64,256]{3,2,1,0:T(8,128)(2,1)S(1)}, u32[]{:S(2)}, u32[]{:S(2)}) collective-permute-start(bf16[4,8,64,256]{3,2,1,0:T(8,128)(2,1)S(1)} %copy-done.5), channel_id=1, source_target_pairs={{0,128},{1,17},{2,130},{3,19},{4,132},{5,21},{6,134},{7,23},{8,136... | collective-permute-start | bytes 3145736 | tf_op jit(solution)/shard_map/ppermute | solution.py:41
  147.1 23.6 %collective-permute-start.19 = (bf16[4,8,64,256]{3,2,1,0:T(8,128)(2,1)S(1)}, bf16[4,8,64,256]{3,2,1,0:T(8,128)(2,1)S(1)}, u32[]{:S(2)}, u32[]{:S(2)}) collective-permute-start(bf16[4,8,64,256]{3,2,1,0:T(8,128)(2,1)S(1)} %copy-done.8), channel_id=1, source_target_pairs={{0,192},{1,25},{2,194},{3,27},{4,196},{5,29},{6,198},{7,31},{8,200... | collective-permute-start | bytes 3145736 | tf_op jit(solution)/shard_map/ppermute | solution.py:41
  147.2 26.6 %collective-permute-start.17 = (bf16[4,8,64,256]{3,2,1,0:T(8,128)(2,1)S(1)}, bf16[4,8,64,256]{3,2,1,0:T(8,128)(2,1)S(1)}, u32[]{:S(2)}, u32[]{:S(2)}) collective-permute-start(bf16[4,8,64,256]{3,2,1,0:T(8,128)(2,1)S(1)} %copy-done.6), channel_id=1, source_target_pairs={{0,64},{1,9},{2,66},{3,11},{4,68},{5,13},{6,70},{7,15},{8,72},{9,1... | collective-permute-start | bytes 3145736 | tf_op jit(solution)/shard_map/ppermute | solution.py:41
  174.4 7.2 %collective-permute-start.21 = (bf16[8,64,256]{2,1,0:T(8,128)(2,1)S(1)}, bf16[8,64,256]{2,1,0:T(8,128)(2,1)S(1)}, u32[]{:S(2)}, u32[]{:S(2)}) collective-permute-start(bf16[8,64,256]{2,1,0:T(8,128)(2,1)S(1)} %get-tuple-element.28), channel_id=1, source_target_pairs={{0,16},{1,129},{2,18},{3,131},{4,20},{5,133},{6,22},{7,135},{8,24}... | collective-permute-start | bytes 786440 | tf_op jit(solution)/shard_map/ppermute | solution.py:41
  174.7 7.7 %collective-permute-start.23 = (bf16[8,64,256]{2,1,0:T(8,128)(2,1)S(1)}, bf16[8,64,256]{2,1,0:T(8,128)(2,1)}, u32[]{:S(2)}, u32[]{:S(2)}) collective-permute-start(bf16[8,64,256]{2,1,0:T(8,128)(2,1)S(1)} %get-tuple-element.29), channel_id=1, source_target_pairs={{0,24},{1,193},{2,26},{3,195},{4,28},{5,197},{6,30},{7,199},{8,0},... | collective-permute-start | bytes 786440 | tf_op jit(solution)/shard_map/ppermute | solution.py:41
  175.7 8.8 %collective-permute-start.22 = (bf16[8,64,256]{2,1,0:T(8,128)(2,1)S(1)}, bf16[8,64,256]{2,1,0:T(8,128)(2,1)}, u32[]{:S(2)}, u32[]{:S(2)}) collective-permute-start(bf16[8,64,256]{2,1,0:T(8,128)(2,1)S(1)} %get-tuple-element.30), channel_id=1, source_target_pairs={{0,8},{1,65},{2,10},{3,67},{4,12},{5,69},{6,14},{7,71},{8,16},{9,7... | collective-permute-start | bytes 786440 | tf_op jit(solution)/shard_map/ppermute | solution.py:41
  185.4 9.2 %collective-permute-start.25 = (bf16[64,256]{1,0:T(8,128)(2,1)S(1)}, bf16[64,256]{1,0:T(8,128)(2,1)S(1)}, u32[]{:S(2)}, u32[]{:S(2)}) collective-permute-start(bf16[64,256]{1,0:T(8,128)(2,1)S(1)} %get-tuple-element.36), channel_id=1, source_target_pairs={{0,2},{1,3},{2,4},{3,5},{4,6},{5,7},{6,0},{7,1},{8,10},{9,11},{10,... | collective-permute-start | bytes 98312 | tf_op jit(solution)/shard_map/ppermute | solution.py:32
  186.3 9.8 %collective-permute-start.27 = (bf16[64,256]{1,0:T(8,128)(2,1)S(1)}, bf16[64,256]{1,0:T(8,128)(2,1)S(1)}, u32[]{:S(2)}, u32[]{:S(2)}) collective-permute-start(bf16[64,256]{1,0:T(8,128)(2,1)S(1)} %get-tuple-element.37), channel_id=1, source_target_pairs={{0,4},{1,5},{2,6},{3,7},{4,0},{5,1},{6,2},{7,3},{8,12},{9,13},{10,... | collective-permute-start | bytes 98312 | tf_op jit(solution)/shard_map/ppermute | solution.py:32
  190.1 10.4 %collective-permute-start.26 = (bf16[64,256]{1,0:T(8,128)(2,1)S(1)}, bf16[64,256]{1,0:T(8,128)(2,1)S(1)}, u32[]{:S(2)}, u32[]{:S(2)}) collective-permute-start(bf16[64,256]{1,0:T(8,128)(2,1)S(1)} %get-tuple-element.38), channel_id=1, source_target_pairs={{0,34},{1,35},{2,36},{3,37},{4,38},{5,39},{6,32},{7,33},{8,42},{9,... | collective-permute-start | bytes 98312 | tf_op jit(solution)/shard_map/ppermute | solution.py:32
  191.5 9.0 %collective-permute-start.24 = (bf16[64,256]{1,0:T(8,128)(2,1)S(1)}, bf16[64,256]{1,0:T(8,128)(2,1)S(1)}, u32[]{:S(2)}, u32[]{:S(2)}) collective-permute-start(bf16[64,256]{1,0:T(8,128)(2,1)S(1)} %get-tuple-element.32), channel_id=1, source_target_pairs={{0,32},{1,33},{2,34},{3,35},{4,36},{5,37},{6,38},{7,39},{8,40},{9,... | collective-permute-start | bytes 98312 | tf_op jit(solution)/shard_map/ppermute | solution.py:32
  193.0 7.6 %collective-permute-start.30 = (bf16[64,256]{1,0:T(8,128)(2,1)S(1)}, bf16[64,256]{1,0:T(8,128)(2,1)S(1)}, u32[]{:S(2)}, u32[]{:S(2)}) collective-permute-start(bf16[64,256]{1,0:T(8,128)(2,1)S(1)} %get-tuple-element.33), channel_id=1, source_target_pairs={{0,38},{1,39},{2,32},{3,33},{4,34},{5,35},{6,36},{7,37},{8,46},{9,... | collective-permute-start | bytes 98312 | tf_op jit(solution)/shard_map/ppermute | solution.py:32
  (17 other events, 206.0 us)
where the time goes:
time: 209 us
  waiting for transfers between devices  78.6 us (38%)
  starting transfers between devices  71.2 us (34%)
  Pallas kernels  44.9 us (21%)
  local copies, waits for them, and re-layouts  6.63 us (3%)
  other arithmetic  6.23 us (3%)
    ppermute x20, starting transfers between devices, shift(): return lax.ppermute(value, AXES, pairs)  60.2 us
    ppermute x12, waiting for transfers between devices, cross(): return lax.ppermute(value, AXES, pairs)  60.1 us
    ppermute x20, waiting for transfers between devices, shift(): return lax.ppermute(value, AXES, pairs)  18.5 us
    pallas_call x3, Pallas kernels, spread(): whole(functools.partial(spread_kernel, which, len(after)), [VMEM] * 2 + [...  13.2 us
    pallas_call x1, Pallas kernels, shards(): whole(weight_kernel, [HBM] * 4 + [VMEM] * 2 + [HBM], [((16, 256, 256), F3...  11.7 us
    ppermute x12, starting transfers between devices, cross(): return lax.ppermute(value, AXES, pairs)  11 us
    pallas_call x1, Pallas kernels, attend(): pl.pallas_call(attend_kernel, grid_spec=pltpu.PrefetchScalarGridSpec(num_...  9.52 us
    pallas_call x1, Pallas kernels, shards(): whole(functools.partial(project_kernel, (1, 2, 3), True), [HBM] * 5 + [VM...  6.55 us
  transfers between devices with their start and end apart: 32, of which 19 were waited for; matrix products, arithmetic and copies ran while one was open for 4% of the time, Pallas kernels for 2%

commit v1 on v0

v1 whole, which is shorter than its diff:
```python
import functools
import math

import jax
import jax.numpy as jnp
from jax import lax
from jax.experimental import pallas as pl
from jax.experimental.pallas import tpu as pltpu
from jax.sharding import PartitionSpec as P

HD = 64
ATTEND = 2
AXES = ("section", "mp")
BF = jnp.bfloat16
F32 = jnp.float32


def coords(i):
    section, mp = divmod(i, 32)
    x, zl = divmod(section, 2)
    y, zh, c = mp // 8, (mp // 2) % 4, mp % 2
    return x, y, 2 * zh + zl, c


def index(x, y, z, c):
    return ((x % 4) * 2 + z % 2) * 32 + (y % 4) * 8 + ((z % 8) // 2) * 2 + c


def shift(value, dx=0, dy=0, dz=0, dc=0):
    pairs = []
    for i in range(256):
        x, y, z, c = coords(i)
        pairs.append((i, index(x + dx, y + dy, z + dz, c ^ dc)))
    return lax.ppermute(value, AXES, pairs)


def cross(value, k, along):
    pairs = []
    for i in range(256):
        x, y, z, c = coords(i)
        dx, dy = (k, 0) if c == along else (0, k)
        pairs.append((i, index(x + dx, y + dy, z, c)))
    return lax.ppermute(value, AXES, pairs)


def nt(a, b):
    return lax.dot_general(a, b, (((1,), (1,)), ((), ())), preferred_element_type=F32)


def nn(a, b):
    return lax.dot_general(a, b, (((1,), (0,)), ((), ())), preferred_element_type=F32)


def project_kernel(which, last, pos, *refs):
    n = len(which)
    x, y, z, c = pos[0], pos[1], pos[2], pos[3]
    pieces, refs = refs[:n], refs[n:]
    wo, wp, refs = refs[0], refs[1], refs[2:]
    if last:
        before, keep, send, acc = refs
    else:
        (acc,) = refs

    def block(dys, first, height, dxs, source):
        own, par = None, None
        for dy in dys:
            yy = (y + 4 - dy) & 3
            columns = []
            for zh in range(4):
                rows = [
                    source(dx, dy)[(z + 8 - (2 * zh + zl)) & 7] for dx in dxs for zl in range(2)
                ]
                columns.append(jnp.concatenate(rows, axis=0))
            lhs = jnp.concatenate(columns, axis=1)
            own_term = nn(lhs, wo[pl.ds(yy * 4, 4)].reshape(1024, 256))
            par_term = nn(lhs, wp[pl.ds(yy * 4, 4)].reshape(1024, 256))
            own = own_term if own is None else own + own_term
            par = par_term if par is None else par + par_term
        if last:
            own += before[first : first + height, :256]
            par += before[first : first + height, 256:]
        acc[first : first + height, :256] = own
        acc[first : first + height, 256:] = par

    @pl.when(c == 0)
    def _():
        first = which[0] * 128
        if last:
            acc[:first] = before[:first]
        else:
            acc[...] = jnp.zeros_like(acc)
        block(range(4), first, n * 128, which, lambda dx, dy: pieces[which.index(dx)].at[dy])

    @pl.when(c == 1)
    def _():
        block(which, 0, 512, range(4), lambda dx, dy: pieces[which.index(dy)].at[dx])

    if last:
        for dx in range(4):
            for zl in range(2):
                m = ((x + 4 - dx) & 3) * 2 + zl
                row = (dx * 2 + zl) * 64
                keep[m] = acc[row : row + 64, :256].astype(BF)
                send[m] = acc[row : row + 64, 256:].astype(BF)


def attend_kernel(pos, lens, q_ref, d_ref, keep_ref, recv_ref, ctx_ref, qg_ref, own_ref, part_ref):
    left = lax.broadcasted_iota(jnp.int32, (128, 128), 1) < HD
    top = lax.broadcasted_iota(jnp.int32, (128, 128), 0) < HD
    zero = jnp.zeros((128, 128), BF)
    source = (lax.broadcasted_iota(jnp.int32, (128, 512), 0) + 64 * pos[3]) & 127
    factor = HD ** (-0.5)

    def stack_heads(t):
        return jnp.concatenate([jnp.where(left, t, zero), jnp.where(left, zero, t)], axis=0)

    def stack_heads_t(t):
        tt = t.T
        return jnp.concatenate([jnp.where(top, tt, zero), jnp.where(top, zero, tt)], axis=1)

    products = []
    for j in range(ATTEND):
        kv = jnp.concatenate([keep_ref[j], recv_ref[j]], axis=0)
        k, v = kv[:, :128], kv[:, 128:]
        products.append((k, v, nt(stack_heads(k), q_ref[0, j]), nt(stack_heads(v), d_ref[0, j])))
    for j, (k, v, scores, prob_grad) in enumerate(products):
        valid = source < lens[pl.program_id(0) * ATTEND + j]
        probs, score_grads = [], []
        for h in range(2):
            s = jnp.where(valid, scores[h * 128 : h * 128 + 128], -1e30)
            e = jnp.exp2((s - jnp.max(s, axis=0, keepdims=True)) * (factor * math.log2(math.e)))
            p = e * (1.0 / jnp.sum(e, axis=0, keepdims=True))
            g = prob_grad[h * 128 : h * 128 + 128]
            score_grads.append((p * (g - jnp.sum(g * p, axis=0, keepdims=True))).astype(BF))
            probs.append(p.astype(BF))
        prob = jnp.concatenate(probs, axis=0)
        score_grad = jnp.concatenate(score_grads, axis=0)
        ctx_ref[0, j] = nn(stack_heads_t(v), prob).astype(BF).T
        qg_ref[0, j] = nn(stack_heads_t(k * jnp.asarray(factor, BF)), score_grad).astype(BF).T
        vg = nn(prob, d_ref[0, j])
        kg = nn(score_grad, q_ref[0, j]) * factor
        kg = jnp.where(left, kg[:128], kg[128:]).astype(BF)
        vg = jnp.where(left, vg[:128], vg[128:]).astype(BF)
        own_ref[j, :, :128] = kg[:64]
        own_ref[j, :, 128:] = vg[:64]
        part_ref[j, :, :128] = kg[64:]
        part_ref[j, :, 128:] = vg[64:]


def spread_kernel(which, after, pos, g_own, g_par, wo, wp, *refs):
    outs = refs[after:]
    x, y, z, c = pos[0], pos[1], pos[2], pos[3]

    def block(dys, dxs, target):
        order = [(dx, zl, ((x + dx) & 3) * 2 + zl) for dx in dxs for zl in range(2)]
        own = jnp.concatenate([g_own[m] for _, _, m in order], axis=0)
        par = jnp.concatenate([g_par[m] for _, _, m in order], axis=0)
        for dy in dys:
            yy = (y + dy) & 3
            t = nt(own, wo[pl.ds(yy * 4, 4)].reshape(1024, 256))
            t = (t + nt(par, wp[pl.ds(yy * 4, 4)].reshape(1024, 256))).astype(BF)
            for j, (dx, zl, _) in enumerate(order):
                for zh in range(4):
                    target(dx, dy)[(2 * zh + zl + 8 - z) & 7] = t[
                        j * 64 : j * 64 + 64, zh * 256 : zh * 256 + 256
                    ]

    @pl.when(c == 0)
    def _():
        block(range(4), which, lambda dx, dy: outs[which.index(dx)].at[dy])

    @pl.when(c == 1)
    def _():
        block(which, range(4), lambda dx, dy: outs[which.index(dy)].at[dx])


def weight_kernel(pos, p0, p1, p2, p3, g_own, g_par, _, own_ref, par_ref):
    x, y, z, c = pos[0], pos[1], pos[2], pos[3]
    pieces = [p0, p1, p2, p3]
    order = [((x + 4 - dx) & 3) * 2 + zl for dx in range(4) for zl in range(2)]
    own = jnp.concatenate([g_own[m] for m in order], axis=0)
    par = jnp.concatenate([g_par[m] for m in order], axis=0)
    grads = jnp.concatenate([own, par], axis=1).T

    def product(block_of):
        for dy in range(4):
            yy = (y + 4 - dy) & 3

            def step(zh, _):
                rows = [
                    block_of(dx, dy)[(z + 8 - (2 * zh + zl)) & 7]
                    for dx in range(4)
                    for zl in range(2)
                ]
                out = nn(grads, jnp.concatenate(rows, axis=0)).astype(BF).T
                own_ref[yy * 4 + zh] = out[:, :256]
                par_ref[yy * 4 + zh] = out[:, 256:]
                return 0

            lax.fori_loop(0, 4, step, 0)

    @pl.when(c == 0)
    def _():
        product(lambda dx, dy: pieces[dx].at[dy])

    @pl.when(c == 1)
    def _():
        product(lambda dx, dy: pieces[dy].at[dx])


SMEM = pl.BlockSpec(memory_space=pltpu.SMEM)
VMEM = pl.BlockSpec(memory_space=pltpu.VMEM)
HBM = pl.BlockSpec(memory_space=pl.ANY)


def whole(kernel, ins, outs, out_specs, scratch):
    return pl.pallas_call(
        kernel,
        in_specs=[SMEM] + ins,
        out_specs=out_specs,
        out_shape=[jax.ShapeDtypeStruct(s, d) for s, d in outs],
        scratch_shapes=scratch,
        compiler_params=pltpu.CompilerParams(vmem_limit_bytes=20 * 2**20),
    )


def spread(which, pos, own, par, w_own, w_par, after):
    return whole(
        functools.partial(spread_kernel, which, len(after)),
        [VMEM] * 4 + [HBM] * len(after),
        [((4, 8, 64, 256), BF)] * len(which),
        [VMEM] * len(which),
        [],
    )(pos, own, par, w_own, w_par, *after)


def attend(pos, lens, queries, d_context, keep, recv):
    wide = pl.BlockSpec((1, ATTEND, 512, 128), lambda m, p, n: (0, m, 0, 0))
    kv = pl.BlockSpec((ATTEND, 64, 256), lambda m, p, n: (m, 0, 0))
    return pl.pallas_call(
        attend_kernel,
        grid_spec=pltpu.PrefetchScalarGridSpec(
            num_scalar_prefetch=2,
            grid=(8 // ATTEND,),
            in_specs=[wide, wide, kv, kv],
            out_specs=[wide, wide, kv, kv],
        ),
        out_shape=[jax.ShapeDtypeStruct((1, 8, 512, 128), BF)] * 2
        + [jax.ShapeDtypeStruct((8, 64, 256), BF)] * 2,
        compiler_params=pltpu.CompilerParams(vmem_limit_bytes=24 * 2**20),
        name="attend",
    )(pos, lens, queries, d_context, keep, recv)


def total(parts):
    return functools.reduce(lambda p, q: p + q, [p.astype(F32) for p in parts]).astype(BF)


def shards(enc_final, enc_len, kv_weight, queries, d_context):
    section, mp = lax.axis_index("section"), lax.axis_index("mp")
    c = mp % 2
    pos = jnp.stack([section // 2, mp // 8, ((mp // 2) % 4) * 2 + section % 2, c]).astype(jnp.int32)
    first = c == 0

    lower, upper = enc_final[0, :64], enc_final[0, 64:]
    mine = jnp.where(first, lower, upper)
    other = shift(jnp.where(first, upper, lower), dc=1)
    states = jnp.where(first, jnp.concatenate([mine, other], 1), jnp.concatenate([other, mine], 1))

    w_own = kv_weight.reshape(16, 256, 256)
    w_par = shift(w_own, dc=1)

    far = (2, 1, 3)
    line = jnp.stack([states] + [shift(states, dz=k) for k in range(1, 8)])
    got = {0: line}
    for k in far:
        got[k] = cross(line, k, 1)
    plane = jnp.stack([got[k] for k in range(4)])
    got = {0: plane}
    for k in far:
        got[k] = cross(plane, k, 0)
    pieces = [got[k] for k in range(4)]

    half = ((8, 64, 256), BF)
    (acc,) = whole(
        functools.partial(project_kernel, (0,), False), [VMEM] * 3, [((512, 512), F32)], [VMEM], []
    )(pos, plane, w_own, w_par)
    keep, send = whole(
        functools.partial(project_kernel, (1, 2, 3), True),
        [VMEM] * 6,
        [half, half],
        [VMEM] * 2,
        [pltpu.VMEM((512, 512), F32)],
    )(pos, *pieces[1:], w_own, w_par, acc)
    recv = shift(send, dc=1)
    context, query_grad, grad_keep, grad_send = attend(pos, enc_len, queries, d_context, keep, recv)
    grad_recv = shift(grad_send, dc=1)

    part_1, part_2, part_3 = spread((1, 2, 3), pos, grad_keep, grad_recv, w_own, w_par, ())
    got_1 = cross(part_1, 1, 0)
    got_2 = cross(part_2, 2, 0)
    got_3 = cross(part_3, 3, 0)
    (part_0,) = spread((0,), pos, grad_keep, grad_recv, w_own, w_par, (part_1,))
    got = [part_0, got_1, got_2, got_3]

    grad_own, grad_par = whole(
        weight_kernel, [VMEM] * 6 + [HBM], [((16, 256, 256), BF)] * 2, [VMEM] * 2, []
    )(pos, *pieces, grad_keep, grad_recv, part_0)
    grad_other = shift(grad_par, dc=1)
    weight_grad = total([grad_own, grad_other]).reshape(1, 4096, 2, 128)

    parts = [total([p[k] for p in got]) for k in range(4)]
    got = [parts[0]] + [cross(parts[k], k, 1) for k in far]
    got[0], weight_grad = lax.optimization_barrier((got[0], weight_grad))
    line = [total([p[k] for p in got]) for k in range(8)]
    rows = total([line[0]] + [shift(line[k], dz=k) for k in range(1, 8)])
    own = jnp.where(first, rows[:, :128], rows[:, 128:])
    other = shift(jnp.where(first, rows[:, 128:], rows[:, :128]), dc=1)
    enc_grad = jnp.where(first, jnp.concatenate([own, other], 0), jnp.concatenate([other, own], 0))
    return context, query_grad, weight_grad, enc_grad[None]


def solution(mesh):
    return jax.shard_map(
        shards,
        mesh=mesh,
        in_specs=(
            P("section", None, "mp"),
            P(),
            P("section", None, None, "mp"),
            P("section", None, None, "mp"),
            P("section", None, None, "mp"),
        ),
        out_specs=(
            P("section", None, None, "mp"),
            P("section", None, None, "mp"),
            P("section", None, None, "mp"),
            P("section", None, "mp"),
        ),
        check_vma=False,
    )
```

time: 209 us -> 188 us (0.90)
  the two profiles are of different devices: /device:TPU:1 before, /device:TPU:33 now
where the time goes in v1:
time: 188 us; the launch traced here: 187 us
  waiting for transfers between devices  75.7 us (40%)
  starting transfers between devices  73.4 us (39%)
  Pallas kernels  26.3 us (14%)
  other arithmetic  5.66 us (3%)
  local copies, waits for them, and re-layouts  5.22 us (3%)
    ppermute x20, starting transfers between devices, shift(): return lax.ppermute(value, AXES, pairs)  62.5 us
    ppermute x12, waiting for transfers between devices, cross(): return lax.ppermute(value, AXES, pairs)  62.3 us
    ppermute x20, waiting for transfers between devices, shift(): return lax.ppermute(value, AXES, pairs)  13.4 us
    ppermute x12, starting transfers between devices, cross(): return lax.ppermute(value, AXES, pairs)  10.9 us
    pallas_call x1, Pallas kernels, shards(): whole(weight_kernel, [VMEM] * 6 + [HBM], [((16, 256, 256), BF)] * 2, [VME...  7.72 us
    pallas_call x1, Pallas kernels, attend(): pl.pallas_call(attend_kernel, grid_spec=pltpu.PrefetchScalarGridSpec(num_...  5.84 us
    pallas_call x2, Pallas kernels, spread(): whole(functools.partial(spread_kernel, which, len(after)), [VMEM] * 4 + [...  5.8 us
    pallas_call x1, Pallas kernels, shards(): whole(functools.partial(project_kernel, (1, 2, 3), True), [VMEM] * 6, [ha...  4.41 us
  transfers between devices with their start and end apart: 32, of which 19 were waited for; matrix products, arithmetic and copies ran while one was open for 4% of the time, Pallas kernels for 1%

profile of v1, /device:TPU:33, one launch (start us, length us, event | category | flops | bytes accessed | tf_op | source)
XLA Modules:
  0.0 187.1 jit_solution(951929068386448678)
XLA Ops:
  2.1 3.2 %reshape.218.refs_1_.refs_3_.wo = bf16[16,256,256]{2,1,0:T(8,128)(2,1)S(1)} reshape(bf16[1,4096,2,128]{3,2,1,0:T(2,128)(2,1)} %param.7) | data formatting | bytes 4194304 | tf_op jit(solution)/shard_map/reshape | solution.py:270
  7.0 4.3 %collective-permute-start.6 = (bf16[64,256]{1,0:T(8,128)(2,1)S(1)}, bf16[64,256]{1,0:T(8,128)(2,1)S(1)}, u32[]{:S(2)}, u32[]{:S(2)}) collective-permute-start(bf16[64,256]{1,0:T(8,128)(2,1)S(1)} %maximum_select_fusion.1), channel_id=1, source_target_pairs={{0,6},{1,7},{2,0},{3,1},{4,2},{5,3},{6,4},{7,5},{8,14},{9,15},{10,... | collective-permute-start | bytes 98312 | tf_op jit(solution)/shard_map/ppermute | solution.py:34
  17.2 2.7 %collective-permute-done.2 = bf16[64,256]{1,0:T(8,128)(2,1)S(1)} collective-permute-done((bf16[64,256]{1,0:T(8,128)(2,1)S(1)}, bf16[64,256]{1,0:T(8,128)(2,1)S(1)}, u32[]{:S(2)}, u32[]{:S(2)}) %collective-permute-start.2) | collective-permute-done | bytes 32800 | tf_op jit(solution)/shard_map/ppermute | solution.py:34
  19.9 4.7 %collective-permute-start.3 = (bf16[64,256]{1,0:T(8,128)(2,1)S(1)}, bf16[64,256]{1,0:T(8,128)(2,1)S(1)}, u32[]{:S(2)}, u32[]{:S(2)}) collective-permute-start(bf16[64,256]{1,0:T(8,128)(2,1)S(1)} %maximum_select_fusion.1), channel_id=1, source_target_pairs={{0,34},{1,35},{2,36},{3,37},{4,38},{5,39},{6,32},{7,33},{8,42},{9,... | collective-permute-start | bytes 98312 | tf_op jit(solution)/shard_map/ppermute | solution.py:34
  25.8 4.1 %collective-permute-start.4 = (bf16[64,256]{1,0:T(8,128)(2,1)S(1)}, bf16[64,256]{1,0:T(8,128)(2,1)S(1)}, u32[]{:S(2)}, u32[]{:S(2)}) collective-permute-start(bf16[64,256]{1,0:T(8,128)(2,1)S(1)} %maximum_select_fusion.1), channel_id=1, source_target_pairs={{0,4},{1,5},{2,6},{3,7},{4,0},{5,1},{6,2},{7,3},{8,12},{9,13},{10,... | collective-permute-start | bytes 98312 | tf_op jit(solution)/shard_map/ppermute | solution.py:34
  29.9 2.6 %collective-permute-done.4 = bf16[64,256]{1,0:T(8,128)(2,1)S(1)} collective-permute-done((bf16[64,256]{1,0:T(8,128)(2,1)S(1)}, bf16[64,256]{1,0:T(8,128)(2,1)S(1)}, u32[]{:S(2)}, u32[]{:S(2)}) %collective-permute-start.4) | collective-permute-done | bytes 32800 | tf_op jit(solution)/shard_map/ppermute | solution.py:34
  36.3 5.0 %collective-permute-done.10 = bf16[8,64,256]{2,1,0:T(8,128)(2,1)S(1)} collective-permute-done((bf16[8,64,256]{2,1,0:T(8,128)(2,1)S(1)}, bf16[8,64,256]{2,1,0:T(8,128)(2,1)S(1)}, u32[]{:S(2)}, u32[]{:S(2)}) %collective-permute-start.10) | collective-permute-done | bytes 262176 | tf_op jit(solution)/shard_map/ppermute | solution.py:43
  42.0 2.7 %collective-permute-done.8 = bf16[8,64,256]{2,1,0:T(8,128)(2,1)S(1)} collective-permute-done((bf16[8,64,256]{2,1,0:T(8,128)(2,1)S(1)}, bf16[8,64,256]{2,1,0:T(8,128)(2,1)S(1)}, u32[]{:S(2)}, u32[]{:S(2)}) %collective-permute-start.8) | collective-permute-done | bytes 262176 | tf_op jit(solution)/shard_map/ppermute | solution.py:43
  44.8 3.1 %collective-permute-start.13 = (bf16[4,8,64,256]{3,2,1,0:T(8,128)(2,1)S(1)}, bf16[4,8,64,256]{3,2,1,0:T(8,128)(2,1)}, u32[]{:S(2)}, u32[]{:S(2)}) collective-permute-start(bf16[4,8,64,256]{3,2,1,0:T(8,128)(2,1)S(1)} %pad_maximum_fusion.refs_0_.p0), channel_id=1, source_target_pairs={{0,192},{1,25},{2,194},{3,27},{4,196},{5,29},{6,198},{7,31},{8,200... | collective-permute-start | bytes 3145736 | tf_op jit(solution)/shard_map/ppermute | solution.py:43
  51.4 19.5 %collective-permute-done.13.refs_2_.p3 = bf16[4,8,64,256]{3,2,1,0:T(8,128)(2,1)} collective-permute-done((bf16[4,8,64,256]{3,2,1,0:T(8,128)(2,1)S(1)}, bf16[4,8,64,256]{3,2,1,0:T(8,128)(2,1)}, u32[]{:S(2)}, u32[]{:S(2)}) %collective-permute-start.13) | collective-permute-done | bytes 1048608 | tf_op jit(solution)/shard_map/ppermute | solution.py:43
  70.9 3.6 %collective-permute-done.11.refs_0_.p1 = bf16[4,8,64,256]{3,2,1,0:T(8,128)(2,1)} collective-permute-done((bf16[4,8,64,256]{3,2,1,0:T(8,128)(2,1)S(1)}, bf16[4,8,64,256]{3,2,1,0:T(8,128)(2,1)}, u32[]{:S(2)}, u32[]{:S(2)}) %collective-permute-start.11) | collective-permute-done | bytes 1048608 | tf_op jit(solution)/shard_map/ppermute | solution.py:43
  74.5 4.4 %shard_map.85 = (bf16[8,64,256]{2,1,0:T(8,128)(2,1)S(1)}, bf16[8,64,256]{2,1,0:T(8,128)(2,1)S(1)}) custom-call(s32[4]{0:T(128)S(1)} %pad_add_fusion.pos, bf16[4,8,64,256]{3,2,1,0:T(8,128)(2,1)} %collective-permute-done.11.refs_0_.p1, bf16[4,8,64,256]{3,2,1,0:T(8,128)(2,1)} %collective-permute-done.12.refs_1_.p2, ...), custom_call_target="tpu_custom_call" | custom-call | tf_op jit(solution)/shard_map/pallas_call | solution.py:288
  79.0 20.9 %collective-permute-start.15 = (bf16[8,64,256]{2,1,0:T(8,128)(2,1)S(1)}, bf16[8,64,256]{2,1,0:T(8,128)(2,1)S(1)}, u32[]{:S(2)}, u32[]{:S(2)}) collective-permute-start(bf16[8,64,256]{2,1,0:T(8,128)(2,1)S(1)} %get-tuple-element.18), channel_id=1, source_target_pairs={{0,1},{1,0},{2,3},{3,2},{4,5},{5,4},{6,7},{7,6},{8,9},{9,8},{10,11... | collective-permute-start | bytes 786440 | tf_op jit(solution)/shard_map/ppermute | solution.py:34
  101.0 5.8 %attend.1 = (bf16[1,8,512,128]{3,2,1,0:T(8,128)(2,1)}, bf16[1,8,512,128]{3,2,1,0:T(8,128)(2,1)}, bf16[8,64,256]{2,1,0:T(8,128)(2,1)S(1)}, bf16[8,64,256]{2,1,0:T(8,128)(2,1)S(1)}) custom-call(s32[4]{0:T(128)S(1)} %pad_add_fusion.pos, s32[8]{0:T(128)S(1)} %copy-done.2, bf16[1,8,512,128]{3,2,1,0:T(8,128)(2,1)S(1)} %copy-done, ...), custom_call_target="tpu_custom_call" | custom-call | tf_op jit(solution)/shard_map/attend/pallas_call | solution.py:240
  108.4 3.4 %shard_map.86 = (bf16[4,8,64,256]{3,2,1,0:T(8,128)(2,1)S(1)}, bf16[4,8,64,256]{3,2,1,0:T(8,128)(2,1)S(1)}, bf16[4,8,64,256]{3,2,1,0:T(8,128)(2,1)S(1)}) custom-call(s32[4]{0:T(128)S(1)} %pad_add_fusion.pos, bf16[8,64,256]{2,1,0:T(8,128)(2,1)S(1)} %get-tuple-element.21.g_own, bf16[8,64,256]{2,1,0:T(8,128)(2,1)S(1)} %collective-permute-done.16.g_par, ...), custom_call_target="tpu_custom_call" | custom-call | tf_op jit(solution)/shard_map/pallas_call | solution.py:228
  114.2 7.7 %shard_map.88 = (bf16[16,256,256]{2,1,0:T(8,128)(2,1)S(1)}, bf16[16,256,256]{2,1,0:T(8,128)(2,1)S(1)}) custom-call(s32[4]{0:T(128)S(1)} %pad_add_fusion.pos, bf16[4,8,64,256]{3,2,1,0:T(8,128)(2,1)S(1)} %pad_maximum_fusion.refs_0_.p0, bf16[4,8,64,256]{3,2,1,0:T(8,128)(2,1)} %collective-permute-done.11.refs_0_.p1, ...), custom_call_target="tpu_custom_call" | custom-call | tf_op jit(solution)/shard_map/pallas_call | solution.py:306
  124.6 14.0 %collective-permute-done.18 = bf16[4,8,64,256]{3,2,1,0:T(8,128)(2,1)S(1)} collective-permute-done((bf16[4,8,64,256]{3,2,1,0:T(8,128)(2,1)S(1)}, bf16[4,8,64,256]{3,2,1,0:T(8,128)(2,1)S(1)}, u32[]{:S(2)}, u32[]{:S(2)}) %collective-permute-start.18) | collective-permute-done | bytes 1048608 | tf_op jit(solution)/shard_map/ppermute | solution.py:43
  138.6 8.0 %collective-permute-done.19 = bf16[4,8,64,256]{3,2,1,0:T(8,128)(2,1)S(1)} collective-permute-done((bf16[4,8,64,256]{3,2,1,0:T(8,128)(2,1)S(1)}, bf16[4,8,64,256]{3,2,1,0:T(8,128)(2,1)S(1)}, u32[]{:S(2)}, u32[]{:S(2)}) %collective-permute-start.19) | collective-permute-done | bytes 1048608 | tf_op jit(solution)/shard_map/ppermute | solution.py:43
  146.6 3.2 %collective-permute-done.17 = bf16[4,8,64,256]{3,2,1,0:T(8,128)(2,1)S(1)} collective-permute-done((bf16[4,8,64,256]{3,2,1,0:T(8,128)(2,1)S(1)}, bf16[4,8,64,256]{3,2,1,0:T(8,128)(2,1)S(1)}, u32[]{:S(2)}, u32[]{:S(2)}) %collective-permute-start.17) | collective-permute-done | bytes 1048608 | tf_op jit(solution)/shard_map/ppermute | solution.py:43
  155.1 2.7 %collective-permute-done.21 = bf16[8,64,256]{2,1,0:T(8,128)(2,1)S(1)} collective-permute-done((bf16[8,64,256]{2,1,0:T(8,128)(2,1)S(1)}, bf16[8,64,256]{2,1,0:T(8,128)(2,1)S(1)}, u32[]{:S(2)}, u32[]{:S(2)}) %collective-permute-start.21) | collective-permute-done | bytes 262176 | tf_op jit(solution)/shard_map/ppermute | solution.py:43
  161.6 4.2 %collective-permute-start.27 = (bf16[64,256]{1,0:T(8,128)(2,1)S(1)}, bf16[64,256]{1,0:T(8,128)(2,1)S(1)}, u32[]{:S(2)}, u32[]{:S(2)}) collective-permute-start(bf16[64,256]{1,0:T(8,128)(2,1)S(1)} %get-tuple-element.39), channel_id=1, source_target_pairs={{0,4},{1,5},{2,6},{3,7},{4,0},{5,1},{6,2},{7,3},{8,12},{9,13},{10,... | collective-permute-start | bytes 98312 | tf_op jit(solution)/shard_map/ppermute | solution.py:34
  170.8 2.7 %collective-permute-start.29 = (bf16[64,256]{1,0:T(8,128)(2,1)S(1)}, bf16[64,256]{1,0:T(8,128)(2,1)S(1)}, u32[]{:S(2)}, u32[]{:S(2)}) collective-permute-start(bf16[64,256]{1,0:T(8,128)(2,1)S(1)} %get-tuple-element.36), channel_id=1, source_target_pairs={{0,6},{1,7},{2,0},{3,1},{4,2},{5,3},{6,4},{7,5},{8,14},{9,15},{10,... | collective-permute-start | bytes 98312 | tf_op jit(solution)/shard_map/ppermute | solution.py:34
  173.5 3.5 %collective-permute-start.28 = (bf16[64,256]{1,0:T(8,128)(2,1)S(1)}, bf16[64,256]{1,0:T(8,128)(2,1)S(1)}, u32[]{:S(2)}, u32[]{:S(2)}) collective-permute-start(bf16[64,256]{1,0:T(8,128)(2,1)S(1)} %get-tuple-element.37), channel_id=1, source_target_pairs={{0,36},{1,37},{2,38},{3,39},{4,32},{5,33},{6,34},{7,35},{8,44},{9,... | collective-permute-start | bytes 98312 | tf_op jit(solution)/shard_map/ppermute | solution.py:34
  180.2 5.5 %collective-permute-start.31 = (bf16[64,128]{1,0:T(8,128)(2,1)S(1)}, bf16[64,128]{1,0:T(8,128)(2,1)S(1)}, u32[]{:S(2)}, u32[]{:S(2)}) collective-permute-start(bf16[64,128]{1,0:T(8,128)(2,1)S(1)} %get-tuple-element.42), channel_id=1, source_target_pairs={{0,1},{1,0},{2,3},{3,2},{4,5},{5,4},{6,7},{7,6},{8,9},{9,8},{10,11... | collective-permute-start | bytes 49160 | tf_op jit(solution)/shard_map/ppermute | solution.py:34
  (73 shorter events, 44.6 us)
Async XLA Ops:
  5.2 43.7 %collective-permute-start.14 = (bf16[16,256,256]{2,1,0:T(8,128)(2,1)S(1)}, bf16[16,256,256]{2,1,0:T(8,128)(2,1)}, u32[]{:S(2)}, u32[]{:S(2)}) collective-permute-start(bf16[16,256,256]{2,1,0:T(8,128)(2,1)S(1)} %reshape.218.refs_1_.refs_3_.wo), channel_id=1, source_target_pairs={{0,1},{1,0},{2,3},{3,2},{4,5},{5,4},{6,7},{7,6},{8,9},{9,8},{10,11... | collective-permute-start | bytes 6291464 | tf_op jit(solution)/shard_map/ppermute | solution.py:34
  5.4 27.2 %collective-permute-start.7 = (bf16[64,256]{1,0:T(8,128)(2,1)S(1)}, bf16[64,256]{1,0:T(8,128)(2,1)S(1)}, u32[]{:S(2)}, u32[]{:S(2)}) collective-permute-start(bf16[64,256]{1,0:T(8,128)(2,1)S(1)} %maximum_select_fusion.1), channel_id=1, source_target_pairs={{0,38},{1,39},{2,32},{3,33},{4,34},{5,35},{6,36},{7,37},{8,46},{9,... | collective-permute-start | bytes 98312 | tf_op jit(solution)/shard_map/ppermute | solution.py:34
  7.0 25.6 %collective-permute-start.6 = (bf16[64,256]{1,0:T(8,128)(2,1)S(1)}, bf16[64,256]{1,0:T(8,128)(2,1)S(1)}, u32[]{:S(2)}, u32[]{:S(2)}) collective-permute-start(bf16[64,256]{1,0:T(8,128)(2,1)S(1)} %maximum_select_fusion.1), channel_id=1, source_target_pairs={{0,6},{1,7},{2,0},{3,1},{4,2},{5,3},{6,4},{7,5},{8,14},{9,15},{10,... | collective-permute-start | bytes 98312 | tf_op jit(solution)/shard_map/ppermute | solution.py:34
  11.3 21.2 %collective-permute-start.5 = (bf16[64,256]{1,0:T(8,128)(2,1)S(1)}, bf16[64,256]{1,0:T(8,128)(2,1)S(1)}, u32[]{:S(2)}, u32[]{:S(2)}) collective-permute-start(bf16[64,256]{1,0:T(8,128)(2,1)S(1)} %maximum_select_fusion.1), channel_id=1, source_target_pairs={{0,36},{1,37},{2,38},{3,39},{4,32},{5,33},{6,34},{7,35},{8,44},{9,... | collective-permute-start | bytes 98312 | tf_op jit(solution)/shard_map/ppermute | solution.py:34
  25.8 6.7 %collective-permute-start.4 = (bf16[64,256]{1,0:T(8,128)(2,1)S(1)}, bf16[64,256]{1,0:T(8,128)(2,1)S(1)}, u32[]{:S(2)}, u32[]{:S(2)}) collective-permute-start(bf16[64,256]{1,0:T(8,128)(2,1)S(1)} %maximum_select_fusion.1), channel_id=1, source_target_pairs={{0,4},{1,5},{2,6},{3,7},{4,0},{5,1},{6,2},{7,3},{8,12},{9,13},{10,... | collective-permute-start | bytes 98312 | tf_op jit(solution)/shard_map/ppermute | solution.py:34
  32.6 8.7 %collective-permute-start.10 = (bf16[8,64,256]{2,1,0:T(8,128)(2,1)S(1)}, bf16[8,64,256]{2,1,0:T(8,128)(2,1)S(1)}, u32[]{:S(2)}, u32[]{:S(2)}) collective-permute-start(bf16[8,64,256]{2,1,0:T(8,128)(2,1)S(1)} %bitcast_dynamic-update-slice_fusion), channel_id=1, source_target_pairs={{0,24},{1,193},{2,26},{3,195},{4,28},{5,197},{6,30},{7,199},{8,0},... | collective-permute-start | bytes 786440 | tf_op jit(solution)/shard_map/ppermute | solution.py:43
  35.1 6.8 %collective-permute-start.9 = (bf16[8,64,256]{2,1,0:T(8,128)(2,1)S(1)}, bf16[8,64,256]{2,1,0:T(8,128)(2,1)S(1)}, u32[]{:S(2)}, u32[]{:S(2)}) collective-permute-start(bf16[8,64,256]{2,1,0:T(8,128)(2,1)S(1)} %bitcast_dynamic-update-slice_fusion), channel_id=1, source_target_pairs={{0,16},{1,129},{2,18},{3,131},{4,20},{5,133},{6,22},{7,135},{8,24}... | collective-permute-start | bytes 786440 | tf_op jit(solution)/shard_map/ppermute | solution.py:43
  35.7 9.0 %collective-permute-start.8 = (bf16[8,64,256]{2,1,0:T(8,128)(2,1)S(1)}, bf16[8,64,256]{2,1,0:T(8,128)(2,1)S(1)}, u32[]{:S(2)}, u32[]{:S(2)}) collective-permute-start(bf16[8,64,256]{2,1,0:T(8,128)(2,1)S(1)} %bitcast_dynamic-update-slice_fusion), channel_id=1, source_target_pairs={{0,8},{1,65},{2,10},{3,67},{4,12},{5,69},{6,14},{7,71},{8,16},{9,7... | collective-permute-start | bytes 786440 | tf_op jit(solution)/shard_map/ppermute | solution.py:43
  44.8 26.1 %collective-permute-start.13 = (bf16[4,8,64,256]{3,2,1,0:T(8,128)(2,1)S(1)}, bf16[4,8,64,256]{3,2,1,0:T(8,128)(2,1)}, u32[]{:S(2)}, u32[]{:S(2)}) collective-permute-start(bf16[4,8,64,256]{3,2,1,0:T(8,128)(2,1)S(1)} %pad_maximum_fusion.refs_0_.p0), channel_id=1, source_target_pairs={{0,192},{1,25},{2,194},{3,27},{4,196},{5,29},{6,198},{7,31},{8,200... | collective-permute-start | bytes 3145736 | tf_op jit(solution)/shard_map/ppermute | solution.py:43
  47.9 23.0 %collective-permute-start.12 = (bf16[4,8,64,256]{3,2,1,0:T(8,128)(2,1)S(1)}, bf16[4,8,64,256]{3,2,1,0:T(8,128)(2,1)}, u32[]{:S(2)}, u32[]{:S(2)}) collective-permute-start(bf16[4,8,64,256]{3,2,1,0:T(8,128)(2,1)S(1)} %pad_maximum_fusion.refs_0_.p0), channel_id=1, source_target_pairs={{0,128},{1,17},{2,130},{3,19},{4,132},{5,21},{6,134},{7,23},{8,136... | collective-permute-start | bytes 3145736 | tf_op jit(solution)/shard_map/ppermute | solution.py:43
  48.0 26.5 %collective-permute-start.11 = (bf16[4,8,64,256]{3,2,1,0:T(8,128)(2,1)S(1)}, bf16[4,8,64,256]{3,2,1,0:T(8,128)(2,1)}, u32[]{:S(2)}, u32[]{:S(2)}) collective-permute-start(bf16[4,8,64,256]{3,2,1,0:T(8,128)(2,1)S(1)} %pad_maximum_fusion.refs_0_.p0), channel_id=1, source_target_pairs={{0,64},{1,9},{2,66},{3,11},{4,68},{5,13},{6,70},{7,15},{8,72},{9,1... | collective-permute-start | bytes 3145736 | tf_op jit(solution)/shard_map/ppermute | solution.py:43
  79.0 22.1 %collective-permute-start.15 = (bf16[8,64,256]{2,1,0:T(8,128)(2,1)S(1)}, bf16[8,64,256]{2,1,0:T(8,128)(2,1)S(1)}, u32[]{:S(2)}, u32[]{:S(2)}) collective-permute-start(bf16[8,64,256]{2,1,0:T(8,128)(2,1)S(1)} %get-tuple-element.18), channel_id=1, source_target_pairs={{0,1},{1,0},{2,3},{3,2},{4,5},{5,4},{6,7},{7,6},{8,9},{9,8},{10,11... | collective-permute-start | bytes 786440 | tf_op jit(solution)/shard_map/ppermute | solution.py:34
  122.0 30.4 %collective-permute-start.20 = (bf16[16,256,256]{2,1,0:T(8,128)(2,1)S(1)}, bf16[16,256,256]{2,1,0:T(8,128)(2,1)S(1)}, u32[]{:S(2)}, u32[]{:S(2)}) collective-permute-start(bf16[16,256,256]{2,1,0:T(8,128)(2,1)S(1)} %get-tuple-element.27), channel_id=1, source_target_pairs={{0,1},{1,0},{2,3},{3,2},{4,5},{5,4},{6,7},{7,6},{8,9},{9,8},{10,11... | collective-permute-start | bytes 6291464 | tf_op jit(solution)/shard_map/ppermute | solution.py:34
  123.2 15.5 %collective-permute-start.18 = (bf16[4,8,64,256]{3,2,1,0:T(8,128)(2,1)S(1)}, bf16[4,8,64,256]{3,2,1,0:T(8,128)(2,1)S(1)}, u32[]{:S(2)}, u32[]{:S(2)}) collective-permute-start(bf16[4,8,64,256]{3,2,1,0:T(8,128)(2,1)S(1)} %get-tuple-element.24), channel_id=1, source_target_pairs={{0,128},{1,17},{2,130},{3,19},{4,132},{5,21},{6,134},{7,23},{8,136... | collective-permute-start | bytes 3145736 | tf_op jit(solution)/shard_map/ppermute | solution.py:43
  123.2 23.5 %collective-permute-start.19 = (bf16[4,8,64,256]{3,2,1,0:T(8,128)(2,1)S(1)}, bf16[4,8,64,256]{3,2,1,0:T(8,128)(2,1)S(1)}, u32[]{:S(2)}, u32[]{:S(2)}) collective-permute-start(bf16[4,8,64,256]{3,2,1,0:T(8,128)(2,1)S(1)} %get-tuple-element.25), channel_id=1, source_target_pairs={{0,192},{1,25},{2,194},{3,27},{4,196},{5,29},{6,198},{7,31},{8,200... | collective-permute-start | bytes 3145736 | tf_op jit(solution)/shard_map/ppermute | solution.py:43
  123.2 26.7 %collective-permute-start.17 = (bf16[4,8,64,256]{3,2,1,0:T(8,128)(2,1)S(1)}, bf16[4,8,64,256]{3,2,1,0:T(8,128)(2,1)S(1)}, u32[]{:S(2)}, u32[]{:S(2)}) collective-permute-start(bf16[4,8,64,256]{3,2,1,0:T(8,128)(2,1)S(1)} %get-tuple-element.23.refs_0_), channel_id=1, source_target_pairs={{0,64},{1,9},{2,66},{3,11},{4,68},{5,13},{6,70},{7,15},{8,72},{9,1... | collective-permute-start | bytes 3145736 | tf_op jit(solution)/shard_map/ppermute | solution.py:43
  150.6 7.2 %collective-permute-start.21 = (bf16[8,64,256]{2,1,0:T(8,128)(2,1)S(1)}, bf16[8,64,256]{2,1,0:T(8,128)(2,1)S(1)}, u32[]{:S(2)}, u32[]{:S(2)}) collective-permute-start(bf16[8,64,256]{2,1,0:T(8,128)(2,1)S(1)} %get-tuple-element.30), channel_id=1, source_target_pairs={{0,16},{1,129},{2,18},{3,131},{4,20},{5,133},{6,22},{7,135},{8,24}... | collective-permute-start | bytes 786440 | tf_op jit(solution)/shard_map/ppermute | solution.py:43
  150.9 7.7 %collective-permute-start.23 = (bf16[8,64,256]{2,1,0:T(8,128)(2,1)S(1)}, bf16[8,64,256]{2,1,0:T(8,128)(2,1)}, u32[]{:S(2)}, u32[]{:S(2)}) collective-permute-start(bf16[8,64,256]{2,1,0:T(8,128)(2,1)S(1)} %get-tuple-element.31), channel_id=1, source_target_pairs={{0,24},{1,193},{2,26},{3,195},{4,28},{5,197},{6,30},{7,199},{8,0},... | collective-permute-start | bytes 786440 | tf_op jit(solution)/shard_map/ppermute | solution.py:43
  151.8 8.8 %collective-permute-start.22 = (bf16[8,64,256]{2,1,0:T(8,128)(2,1)S(1)}, bf16[8,64,256]{2,1,0:T(8,128)(2,1)}, u32[]{:S(2)}, u32[]{:S(2)}) collective-permute-start(bf16[8,64,256]{2,1,0:T(8,128)(2,1)S(1)} %get-tuple-element.32), channel_id=1, source_target_pairs={{0,8},{1,65},{2,10},{3,67},{4,12},{5,69},{6,14},{7,71},{8,16},{9,7... | collective-permute-start | bytes 786440 | tf_op jit(solution)/shard_map/ppermute | solution.py:43
  161.5 9.3 %collective-permute-start.25 = (bf16[64,256]{1,0:T(8,128)(2,1)S(1)}, bf16[64,256]{1,0:T(8,128)(2,1)S(1)}, u32[]{:S(2)}, u32[]{:S(2)}) collective-permute-start(bf16[64,256]{1,0:T(8,128)(2,1)S(1)} %get-tuple-element.38), channel_id=1, source_target_pairs={{0,2},{1,3},{2,4},{3,5},{4,6},{5,7},{6,0},{7,1},{8,10},{9,11},{10,... | collective-permute-start | bytes 98312 | tf_op jit(solution)/shard_map/ppermute | solution.py:34
  161.6 11.9 %collective-permute-start.27 = (bf16[64,256]{1,0:T(8,128)(2,1)S(1)}, bf16[64,256]{1,0:T(8,128)(2,1)S(1)}, u32[]{:S(2)}, u32[]{:S(2)}) collective-permute-start(bf16[64,256]{1,0:T(8,128)(2,1)S(1)} %get-tuple-element.39), channel_id=1, source_target_pairs={{0,4},{1,5},{2,6},{3,7},{4,0},{5,1},{6,2},{7,3},{8,12},{9,13},{10,... | collective-permute-start | bytes 98312 | tf_op jit(solution)/shard_map/ppermute | solution.py:34
  165.8 11.2 %collective-permute-start.26 = (bf16[64,256]{1,0:T(8,128)(2,1)S(1)}, bf16[64,256]{1,0:T(8,128)(2,1)S(1)}, u32[]{:S(2)}, u32[]{:S(2)}) collective-permute-start(bf16[64,256]{1,0:T(8,128)(2,1)S(1)} %get-tuple-element.40), channel_id=1, source_target_pairs={{0,34},{1,35},{2,36},{3,37},{4,38},{5,39},{6,32},{7,33},{8,42},{9,... | collective-permute-start | bytes 98312 | tf_op jit(solution)/shard_map/ppermute | solution.py:34
  169.3 7.7 %collective-permute-start.24 = (bf16[64,256]{1,0:T(8,128)(2,1)S(1)}, bf16[64,256]{1,0:T(8,128)(2,1)S(1)}, u32[]{:S(2)}, u32[]{:S(2)}) collective-permute-start(bf16[64,256]{1,0:T(8,128)(2,1)S(1)} %get-tuple-element.34), channel_id=1, source_target_pairs={{0,32},{1,33},{2,34},{3,35},{4,36},{5,37},{6,38},{7,39},{8,40},{9,... | collective-permute-start | bytes 98312 | tf_op jit(solution)/shard_map/ppermute | solution.py:34
  169.4 7.6 %collective-permute-start.30 = (bf16[64,256]{1,0:T(8,128)(2,1)S(1)}, bf16[64,256]{1,0:T(8,128)(2,1)S(1)}, u32[]{:S(2)}, u32[]{:S(2)}) collective-permute-start(bf16[64,256]{1,0:T(8,128)(2,1)S(1)} %get-tuple-element.35), channel_id=1, source_target_pairs={{0,38},{1,39},{2,32},{3,33},{4,34},{5,35},{6,36},{7,37},{8,46},{9,... | collective-permute-start | bytes 98312 | tf_op jit(solution)/shard_map/ppermute | solution.py:34
  (11 other events, 186.2 us)

commit v2 on v1

--- a/solution.py
+++ b/solution.py
@@ -43,6 +43,14 @@
     return lax.ppermute(value, AXES, pairs)
 
 
+def rise(value, k):
+    pairs = []
+    for i in range(256):
+        x, y, z, c = coords(i)
+        pairs.append((i, index(x, y, z - k if c else z + k, c)))
+    return lax.ppermute(value, AXES, pairs)
+
+
 def nt(a, b):
     return lax.dot_general(a, b, (((1,), (1,)), ((), ())), preferred_element_type=F32)
 
@@ -51,51 +59,60 @@
     return lax.dot_general(a, b, (((1,), (0,)), ((), ())), preferred_element_type=F32)
 
 
-def project_kernel(which, last, pos, *refs):
+def slot_of(c, z, zh, zl):
+    return ((1 - 2 * c) * (z - (2 * zh + zl)) + 16) & 7
+
+
+def project_kernel(which, first, last, pos, *refs):
     n = len(which)
     x, y, z, c = pos[0], pos[1], pos[2], pos[3]
-    pieces, refs = refs[:n], refs[n:]
-    wo, wp, refs = refs[0], refs[1], refs[2:]
-    if last:
-        before, keep, send, acc = refs
-    else:
-        (acc,) = refs
-
-    def block(dys, first, height, dxs, source):
+    pieces, (wo, wp), refs = refs[: 2 * n], refs[2 * n : 2 * n + 2], refs[2 * n + 2 :]
+    if not first:
+        before, refs = refs[0], refs[1:]
+    acc = refs[-1]
+
+    def piece(outer, inner):
+        return pieces[2 * which.index(outer) + inner // 2].at[inner % 2]
+
+    def product(dys, dxs, source):
         own, par = None, None
         for dy in dys:
             yy = (y + 4 - dy) & 3
             columns = []
             for zh in range(4):
-                rows = [
-                    source(dx, dy)[(z + 8 - (2 * zh + zl)) & 7] for dx in dxs for zl in range(2)
-                ]
+                rows = [source(dx, dy)[slot_of(c, z, zh, zl)] for dx in dxs for zl in range(2)]
                 columns.append(jnp.concatenate(rows, axis=0))
             lhs = jnp.concatenate(columns, axis=1)
             own_term = nn(lhs, wo[pl.ds(yy * 4, 4)].reshape(1024, 256))
             par_term = nn(lhs, wp[pl.ds(yy * 4, 4)].reshape(1024, 256))
             own = own_term if own is None else own + own_term
             par = par_term if par is None else par + par_term
-        if last:
-            own += before[first : first + height, :256]
-            par += before[first : first + height, 256:]
-        acc[first : first + height, :256] = own
-        acc[first : first + height, 256:] = par
+        return own, par
 
     @pl.when(c == 0)
     def _():
-        first = which[0] * 128
-        if last:
-            acc[:first] = before[:first]
+        own, par = product(range(4), which, piece)
+        for dx in range(4):
+            to = slice(dx * 128, dx * 128 + 128)
+            if dx in which:
+                at = which.index(dx) * 128
+                acc[to, :256] = own[at : at + 128]
+                acc[to, 256:] = par[at : at + 128]
+            elif not first:
+                acc[to] = before[to]
+
+    @pl.when(c == 1)
+    def _():
+        own, par = product(which, range(4), lambda dx, dy: piece(dy, dx))
+        if first:
+            acc[:, :256] = own
+            acc[:, 256:] = par
         else:
-            acc[...] = jnp.zeros_like(acc)
-        block(range(4), first, n * 128, which, lambda dx, dy: pieces[which.index(dx)].at[dy])
-
-    @pl.when(c == 1)
-    def _():
-        block(which, 0, 512, range(4), lambda dx, dy: pieces[which.index(dy)].at[dx])
+            acc[:, :256] = own + before[:, :256]
+            acc[:, 256:] = par + before[:, 256:]
 
     if last:
+        keep, send = refs[0], refs[1]
         for dx in range(4):
             for zl in range(2):
                 m = ((x + 4 - dx) & 3) * 2 + zl
@@ -151,61 +168,78 @@
     outs = refs[after:]
     x, y, z, c = pos[0], pos[1], pos[2], pos[3]
 
-    def block(dys, dxs, target):
-        order = [(dx, zl, ((x + dx) & 3) * 2 + zl) for dx in dxs for zl in range(2)]
-        own = jnp.concatenate([g_own[m] for _, _, m in order], axis=0)
-        par = jnp.concatenate([g_par[m] for _, _, m in order], axis=0)
-        for dy in dys:
+    def product(dxs):
+        order = [((x + dx) & 3) * 2 + zl for dx in dxs for zl in range(2)]
+        own = jnp.concatenate([g_own[m] for m in order], axis=0)
+        par = jnp.concatenate([g_par[m] for m in order], axis=0)
+
+        def emit(dy, target):
             yy = (y + dy) & 3
             t = nt(own, wo[pl.ds(yy * 4, 4)].reshape(1024, 256))
             t = (t + nt(par, wp[pl.ds(yy * 4, 4)].reshape(1024, 256))).astype(BF)
-            for j, (dx, zl, _) in enumerate(order):
-                for zh in range(4):
-                    target(dx, dy)[(2 * zh + zl + 8 - z) & 7] = t[
-                        j * 64 : j * 64 + 64, zh * 256 : zh * 256 + 256
-                    ]
+            for i, dx in enumerate(dxs):
+                for zl in range(2):
+                    row = i * 128 + zl * 64
+                    for zh in range(4):
+                        target(dx)[slot_of(1 - c, z, zh, zl)] = t[
+                            row : row + 64, zh * 256 : zh * 256 + 256
+                        ]
+
+        return emit
 
     @pl.when(c == 0)
     def _():
-        block(range(4), which, lambda dx, dy: outs[which.index(dx)].at[dy])
+        emit = product(which)
+        for half in range(2):
+
+            def step(inner, _):
+                emit(2 * half + inner, lambda dx: outs[2 * which.index(dx) + half].at[inner])
+                return 0
+
+            lax.fori_loop(0, 2, step, 0)
 
     @pl.when(c == 1)
     def _():
-        block(which, range(4), lambda dx, dy: outs[which.index(dy)].at[dx])
-
-
-def weight_kernel(pos, p0, p1, p2, p3, g_own, g_par, _, own_ref, par_ref):
+        emit = product(range(4))
+        for i, dy in enumerate(which):
+            emit(dy, lambda dx: outs[2 * i + dx // 2].at[dx % 2])
+
+
+def weight_kernel(pos, *refs):
+    pieces, (g_own, g_par, _, own_ref, par_ref) = refs[:8], refs[8:]
     x, y, z, c = pos[0], pos[1], pos[2], pos[3]
-    pieces = [p0, p1, p2, p3]
     order = [((x + 4 - dx) & 3) * 2 + zl for dx in range(4) for zl in range(2)]
     own = jnp.concatenate([g_own[m] for m in order], axis=0)
     par = jnp.concatenate([g_par[m] for m in order], axis=0)
     grads = jnp.concatenate([own, par], axis=1).T
 
-    def product(block_of):
+    def emit(dy, zh, source):
+        rows = [source(dx)[slot_of(c, z, zh, zl)] for dx in range(4) for zl in range(2)]
+        out = nn(grads, jnp.concatenate(rows, axis=0)).astype(BF).T
+        f = ((y + 4 - dy) & 3) * 4 + zh
+        own_ref[f] = out[:, :256]
+        par_ref[f] = out[:, 256:]
+
+    @pl.when(c == 0)
+    def _():
+        for half in range(2):
+
+            def step(i, _):
+                inner = i // 4
+                emit(2 * half + inner, i & 3, lambda dx: pieces[2 * dx + half].at[inner])
+                return 0
+
+            lax.fori_loop(0, 8, step, 0)
+
+    @pl.when(c == 1)
+    def _():
         for dy in range(4):
-            yy = (y + 4 - dy) & 3
 
             def step(zh, _):
-                rows = [
-                    block_of(dx, dy)[(z + 8 - (2 * zh + zl)) & 7]
-                    for dx in range(4)
-                    for zl in range(2)
-                ]
-                out = nn(grads, jnp.concatenate(rows, axis=0)).astype(BF).T
-                own_ref[yy * 4 + zh] = out[:, :256]
-                par_ref[yy * 4 + zh] = out[:, 256:]
+                emit(dy, zh, lambda dx: pieces[2 * dy + dx // 2].at[dx % 2])
                 return 0
 
             lax.fori_loop(0, 4, step, 0)
-
-    @pl.when(c == 0)
-    def _():
-        product(lambda dx, dy: pieces[dx].at[dy])
-
-    @pl.when(c == 1)
-    def _():
-        product(lambda dx, dy: pieces[dy].at[dx])
 
 
 SMEM = pl.BlockSpec(memory_space=pltpu.SMEM)
@@ -224,12 +258,25 @@
     )
 
 
+def project(which, pos, pieces, w_own, w_par, before, last):
+    first = before is None
+    acc = ((512, 512), F32)
+    half = ((8, 64, 256), BF)
+    return whole(
+        functools.partial(project_kernel, which, first, last),
+        [VMEM] * (2 * len(which) + (2 if first else 3)),
+        [half, half] if last else [acc],
+        [VMEM] * (2 if last else 1),
+        [pltpu.VMEM((512, 512), F32)] if last else [],
+    )(pos, *pieces, w_own, w_par, *([] if first else [before]))
+
+
 def spread(which, pos, own, par, w_own, w_par, after):
     return whole(
         functools.partial(spread_kernel, which, len(after)),
         [VMEM] * 4 + [HBM] * len(after),
-        [((4, 8, 64, 256), BF)] * len(which),
-        [VMEM] * len(which),
+        [((2, 8, 64, 256), BF)] * (2 * len(which)),
+        [VMEM] * (2 * len(which)),
         [],
     )(pos, own, par, w_own, w_par, *after)
 
@@ -262,61 +309,89 @@
     pos = jnp.stack([section // 2, mp // 8, ((mp // 2) % 4) * 2 + section % 2, c]).astype(jnp.int32)
     first = c == 0
 
-    lower, upper = enc_final[0, :64], enc_final[0, 64:]
-    mine = jnp.where(first, lower, upper)
-    other = shift(jnp.where(first, upper, lower), dc=1)
-    states = jnp.where(first, jnp.concatenate([mine, other], 1), jnp.concatenate([other, mine], 1))
+    local = enc_final[0]
+    other = shift(local, dc=1)
+    states = jnp.where(
+        first, jnp.concatenate([local, other], 1), jnp.concatenate([other, local], 1)
+    ).reshape(2, 64, 256)
+
+    def halves(v, axis):
+        lower, upper = lax.index_in_dim(v, 0, axis, False), lax.index_in_dim(v, 1, axis, False)
+        return jnp.where(first, lower, upper), jnp.where(first, upper, lower)
+
+    mine, _ = halves(states, 0)
+    across = shift(mine, dz=4)
+    got = []
+    for k in (3, 2, 1):
+        got.append(rise(states, k))
+    near, passed = halves(jnp.stack(got), 1)
+    passed = shift(passed, dc=1)
+    line = jnp.concatenate([mine[None], near[::-1], across[None], passed], 0)
 
     w_own = kv_weight.reshape(16, 256, 256)
     w_par = shift(w_own, dc=1)
 
-    far = (2, 1, 3)
-    line = jnp.stack([states] + [shift(states, dz=k) for k in range(1, 8)])
-    got = {0: line}
-    for k in far:
-        got[k] = cross(line, k, 1)
-    plane = jnp.stack([got[k] for k in range(4)])
-    got = {0: plane}
-    for k in far:
-        got[k] = cross(plane, k, 0)
-    pieces = [got[k] for k in range(4)]
-
-    half = ((8, 64, 256), BF)
-    (acc,) = whole(
-        functools.partial(project_kernel, (0,), False), [VMEM] * 3, [((512, 512), F32)], [VMEM], []
-    )(pos, plane, w_own, w_par)
-    keep, send = whole(
-        functools.partial(project_kernel, (1, 2, 3), True),
-        [VMEM] * 6,
-        [half, half],
-        [VMEM] * 2,
-        [pltpu.VMEM((512, 512), F32)],
-    )(pos, *pieces[1:], w_own, w_par, acc)
+    slices = {0: line}
+    for k in (1, 3, 2):
+        slices[k] = cross(line, k, 1)
+    low = jnp.stack([slices[0], slices[1]])
+    high = jnp.stack([slices[2], slices[3]])
+    right_low = cross(low, 1, 0)
+    left_low = cross(low, 3, 0)
+    left_high = cross(high, 3, 0)
+    right_high = cross(high, 1, 0)
+    far_low = cross(right_low, 1, 0)
+    far_high = cross(left_high, 3, 0)
+    near = (right_low, right_high, left_low, left_high)
+
+    (acc,) = project((0,), pos, (low, high), w_own, w_par, None, False)
+    (acc,) = project((1, 3), pos, near, w_own, w_par, acc, False)
+    keep, send = project((2,), pos, (far_low, far_high), w_own, w_par, acc, True)
     recv = shift(send, dc=1)
     context, query_grad, grad_keep, grad_send = attend(pos, enc_len, queries, d_context, keep, recv)
     grad_recv = shift(grad_send, dc=1)
 
-    part_1, part_2, part_3 = spread((1, 2, 3), pos, grad_keep, grad_recv, w_own, w_par, ())
-    got_1 = cross(part_1, 1, 0)
-    got_2 = cross(part_2, 2, 0)
-    got_3 = cross(part_3, 3, 0)
-    (part_0,) = spread((0,), pos, grad_keep, grad_recv, w_own, w_par, (part_1,))
-    got = [part_0, got_1, got_2, got_3]
+    right_low_g, right_high_g, far_low_g, far_high_g, left_low_g, left_high_g = spread(
+        (1, 2, 3), pos, grad_keep, grad_recv, w_own, w_par, ()
+    )
+    pass_low = cross(far_low_g, 1, 0)
+    pass_high = cross(far_high_g, 3, 0)
+    from_left_high = cross(right_high_g, 1, 0)
+    from_right_low = cross(left_low_g, 3, 0)
+    own_low, own_high = spread(
+        (0,), pos, grad_keep, grad_recv, w_own, w_par, (right_low_g,)
+    )
+    from_left_low = cross(total([right_low_g, pass_low]), 1, 0)
+    from_right_high = cross(total([left_high_g, pass_high]), 3, 0)
 
     grad_own, grad_par = whole(
-        weight_kernel, [VMEM] * 6 + [HBM], [((16, 256, 256), BF)] * 2, [VMEM] * 2, []
-    )(pos, *pieces, grad_keep, grad_recv, part_0)
+        weight_kernel, [VMEM] * 10 + [HBM], [((16, 256, 256), BF)] * 2, [VMEM] * 2, []
+    )(pos, low, high, right_low, right_high, far_low, far_high, left_low, left_high, grad_keep, grad_recv, own_low)
     grad_other = shift(grad_par, dc=1)
     weight_grad = total([grad_own, grad_other]).reshape(1, 4096, 2, 128)
 
-    parts = [total([p[k] for p in got]) for k in range(4)]
-    got = [parts[0]] + [cross(parts[k], k, 1) for k in far]
+    low = [total([own_low[k], from_left_low[k], from_right_low[k]]) for k in range(2)]
+    high = [total([own_high[k], from_left_high[k], from_right_high[k]]) for k in range(2)]
+    got = [low[0]]
+    for k in (1, 3, 2):
+        got.append(cross((low + high)[k], k, 1))
     got[0], weight_grad = lax.optimization_barrier((got[0], weight_grad))
-    line = [total([p[k] for p in got]) for k in range(8)]
-    rows = total([line[0]] + [shift(line[k], dz=k) for k in range(1, 8)])
-    own = jnp.where(first, rows[:, :128], rows[:, 128:])
-    other = shift(jnp.where(first, rows[:, 128:], rows[:, :128]), dc=1)
-    enc_grad = jnp.where(first, jnp.concatenate([own, other], 0), jnp.concatenate([other, own], 0))
+    passed = [total([p[8 - k] for p in got]) for k in (3, 2, 1)]
+    passed = shift(jnp.stack(passed), dc=1)
+    across = shift(total([p[4] for p in got]), dz=4)
+    got_z = []
+    for i, k in enumerate((3, 2, 1)):
+        both = jnp.stack([total([p[k] for p in got]), passed[i]])
+        got_z.append(rise(both, k).astype(F32))
+    both = got_z[0] + got_z[1] + got_z[2]
+    mine = functools.reduce(lambda p, q: p + q, [p[0].astype(F32) for p in got])
+    both = jnp.stack([both[0] + mine + across.astype(F32), both[1]]).reshape(2, 64, 2, 128)
+    kept, passed = halves(both, 2)
+    passed = shift(passed.astype(BF), dc=1).astype(F32)
+    kept, far_half = (kept[0] + passed[1]).astype(BF), (kept[1] + passed[0]).astype(BF)
+    enc_grad = jnp.where(
+        first, jnp.concatenate([kept, far_half], 0), jnp.concatenate([far_half, kept], 0)
+    )
     return context, query_grad, weight_grad, enc_grad[None]
 
 

time: 188 us -> 139 us (0.74)
  the two profiles are of different devices: /device:TPU:33 before, /device:TPU:1 now
where the time goes in v2:
time: 139 us; the launch traced here: 138 us
  starting transfers between devices  58.8 us (42%)
  waiting for transfers between devices  41.3 us (30%)
  Pallas kernels  28 us (20%)
  local copies, waits for them, and re-layouts  5.27 us (4%)
  other arithmetic  4.12 us (3%)
    ppermute x18, waiting for transfers between devices, cross(): return lax.ppermute(value, AXES, pairs)  31.3 us
    ppermute x10, starting transfers between devices, shift(): return lax.ppermute(value, AXES, pairs)  25.8 us
    ppermute x18, starting transfers between devices, cross(): return lax.ppermute(value, AXES, pairs)  21.9 us
    ppermute x6, starting transfers between devices, rise(): return lax.ppermute(value, AXES, pairs)  11.1 us
    ppermute x10, waiting for transfers between devices, shift(): return lax.ppermute(value, AXES, pairs)  9.35 us
    pallas_call x3, Pallas kernels, project(): whole(functools.partial(project_kernel, which, first, last), [VMEM] * (2...  8.72 us
    pallas_call x1, Pallas kernels, shards(): whole(weight_kernel, [VMEM] * 10 + [HBM], [((16, 256, 256), BF)] * 2, [VM...  7.69 us
    pallas_call x1, Pallas kernels, attend(): pl.pallas_call(attend_kernel, grid_spec=pltpu.PrefetchScalarGridSpec(num_...  5.84 us
  transfers between devices with their start and end apart: 34, of which 20 were waited for; matrix products, arithmetic and copies ran while one was open for 6% of the time, Pallas kernels for 4%

profile of v2, /device:TPU:1, one launch (start us, length us, event | category | flops | bytes accessed | tf_op | source)
XLA Modules:
  0.0 138.4 jit_solution(3389092271811757975)
XLA Ops:
  0.6 3.3 %collective-permute-start = (bf16[128,128]{1,0:T(8,128)(2,1)}, bf16[128,128]{1,0:T(8,128)(2,1)S(1)}, u32[]{:S(2)}, u32[]{:S(2)}) collective-permute-start(bf16[128,128]{1,0:T(8,128)(2,1)} %bitcast.58), channel_id=1, source_target_pairs={{0,1},{1,0},{2,3},{3,2},{4,5},{5,4},{6,7},{7,6},{8,9},{9,8},{10,11... | collective-permute-start | bytes 98312 | tf_op jit(solution)/shard_map/ppermute | solution.py:34
  3.9 3.2 %reshape.125.refs_2_.refs_4_.wo = bf16[16,256,256]{2,1,0:T(8,128)(2,1)S(1)} reshape(bf16[1,4096,2,128]{3,2,1,0:T(2,128)(2,1)} %param.7) | data formatting | bytes 4194304 | tf_op jit(solution)/shard_map/reshape | solution.py:331
  7.2 4.4 %collective-permute-start.2 = (bf16[2,64,256]{2,1,0:T(8,128)(2,1)S(1)}, bf16[2,64,256]{2,1,0:T(8,128)(2,1)S(1)}, u32[]{:S(2)}, u32[]{:S(2)}) collective-permute-start(bf16[2,64,256]{2,1,0:T(8,128)(2,1)S(1)} %maximum_select_fusion.1), channel_id=1, source_target_pairs={{0,2},{1,7},{2,4},{3,1},{4,6},{5,3},{6,0},{7,5},{8,10},{9,15},{10,... | collective-permute-start | bytes 196616 | tf_op jit(solution)/shard_map/ppermute | solution.py:51
  12.9 4.5 %collective-permute-start.4 = (bf16[64,256]{1,0:T(8,128)(2,1)S(1)}, bf16[64,256]{1,0:T(8,128)(2,1)S(1)}, u32[]{:S(2)}, u32[]{:S(2)}) collective-permute-start(bf16[64,256]{1,0:T(8,128)(2,1)S(1)} %slice_select_fusion.1), channel_id=1, source_target_pairs={{0,4},{1,5},{2,6},{3,7},{4,0},{5,1},{6,2},{7,3},{8,12},{9,13},{10,... | collective-permute-start | bytes 98312 | tf_op jit(solution)/shard_map/ppermute | solution.py:34
  21.5 2.8 %collective-permute-start.9 = (bf16[8,64,256]{2,1,0:T(8,128)(2,1)S(1)}, bf16[8,64,256]{2,1,0:T(8,128)(2,1)S(1)}, u32[]{:S(2)}, u32[]{:S(2)}) collective-permute-start(bf16[8,64,256]{2,1,0:T(8,128)(2,1)S(1)} %get-tuple-element.52), channel_id=1, source_target_pairs={{0,16},{1,129},{2,18},{3,131},{4,20},{5,133},{6,22},{7,135},{8,24}... | collective-permute-start | bytes 786440 | tf_op jit(solution)/shard_map/ppermute | solution.py:43
  25.7 2.9 %collective-permute-done.9 = bf16[8,64,256]{2,1,0:T(8,128)(2,1)S(1)} collective-permute-done((bf16[8,64,256]{2,1,0:T(8,128)(2,1)S(1)}, bf16[8,64,256]{2,1,0:T(8,128)(2,1)S(1)}, u32[]{:S(2)}, u32[]{:S(2)}) %collective-permute-start.9) | collective-permute-done | bytes 262176 | tf_op jit(solution)/shard_map/ppermute | solution.py:43
  28.6 2.9 %collective-permute-done.10 = bf16[8,64,256]{2,1,0:T(8,128)(2,1)S(1)} collective-permute-done((bf16[8,64,256]{2,1,0:T(8,128)(2,1)S(1)}, bf16[8,64,256]{2,1,0:T(8,128)(2,1)S(1)}, u32[]{:S(2)}, u32[]{:S(2)}) %collective-permute-start.10) | collective-permute-done | bytes 262176 | tf_op jit(solution)/shard_map/ppermute | solution.py:43
  31.5 2.8 %collective-permute-start.11 = (bf16[2,8,64,256]{3,2,1,0:T(8,128)(2,1)S(1)}, bf16[2,8,64,256]{3,2,1,0:T(8,128)(2,1)}, u32[]{:S(2)}, u32[]{:S(2)}) collective-permute-start(bf16[2,8,64,256]{3,2,1,0:T(8,128)(2,1)S(1)} %pad_maximum_fusion.1.refs_1_), channel_id=1, source_target_pairs={{0,192},{1,25},{2,194},{3,27},{4,196},{5,29},{6,198},{7,31},{8,200... | collective-permute-start | bytes 1572872 | tf_op jit(solution)/shard_map/ppermute | solution.py:43
  37.3 3.2 %collective-permute-done.11.refs_3_.refs_7_ = bf16[2,8,64,256]{3,2,1,0:T(8,128)(2,1)} collective-permute-done((bf16[2,8,64,256]{3,2,1,0:T(8,128)(2,1)S(1)}, bf16[2,8,64,256]{3,2,1,0:T(8,128)(2,1)}, u32[]{:S(2)}, u32[]{:S(2)}) %collective-permute-start.11) | collective-permute-done | bytes 524320 | tf_op jit(solution)/shard_map/ppermute | solution.py:43
  40.5 3.2 %collective-permute-start.12 = (bf16[2,8,64,256]{3,2,1,0:T(8,128)(2,1)}, bf16[2,8,64,256]{3,2,1,0:T(8,128)(2,1)}, u32[]{:S(2)}, u32[]{:S(2)}) collective-permute-start(bf16[2,8,64,256]{3,2,1,0:T(8,128)(2,1)} %collective-permute-done.11.refs_3_.refs_7_), channel_id=1, source_target_pairs={{0,192},{1,25},{2,194},{3,27},{4,196},{5,29},{6,198},{7,31},{8,200... | collective-permute-start | bytes 1572872 | tf_op jit(solution)/shard_map/ppermute | solution.py:43
  46.7 3.0 %collective-permute-done.14.refs_1_.refs_3_ = bf16[2,8,64,256]{3,2,1,0:T(8,128)(2,1)} collective-permute-done((bf16[2,8,64,256]{3,2,1,0:T(8,128)(2,1)S(1)}, bf16[2,8,64,256]{3,2,1,0:T(8,128)(2,1)}, u32[]{:S(2)}, u32[]{:S(2)}) %collective-permute-start.14) | collective-permute-done | bytes 524320 | tf_op jit(solution)/shard_map/ppermute | solution.py:43
  49.7 3.5 %shard_map.85.refs_4_ = f32[512,512]{1,0:T(8,128)S(1)} custom-call(s32[4]{0:T(128)S(1)} %pad_add_fusion.pos, bf16[2,8,64,256]{3,2,1,0:T(8,128)(2,1)} %collective-permute-done.7.refs_0_.refs_2_, bf16[2,8,64,256]{3,2,1,0:T(8,128)(2,1)} %collective-permute-done.14.refs_1_.refs_3_, bf16[2,8,64,256]{3,2,1,0:T(8,128)(2,1)} %collective-permute-done.15.refs_2_.refs_6_, ...), custom_call_target="tpu_custom_call" | custom-call | tf_op jit(solution)/shard_map/pallas_call | solution.py:265
  55.4 2.7 %shard_map.86 = (bf16[8,64,256]{2,1,0:T(8,128)(2,1)S(1)}, bf16[8,64,256]{2,1,0:T(8,128)(2,1)S(1)}) custom-call(s32[4]{0:T(128)S(1)} %pad_add_fusion.pos, bf16[2,8,64,256]{3,2,1,0:T(8,128)(2,1)} %collective-permute-done.8.refs_0_.refs_4_, bf16[2,8,64,256]{3,2,1,0:T(8,128)(2,1)} %collective-permute-done.12.refs_1_.refs_5_, ...), custom_call_target="tpu_custom_call" | custom-call | tf_op jit(solution)/shard_map/pallas_call | solution.py:265
  58.1 4.1 %collective-permute-start.16 = (bf16[8,64,256]{2,1,0:T(8,128)(2,1)S(1)}, bf16[8,64,256]{2,1,0:T(8,128)(2,1)S(1)}, u32[]{:S(2)}, u32[]{:S(2)}) collective-permute-start(bf16[8,64,256]{2,1,0:T(8,128)(2,1)S(1)} %get-tuple-element.23), channel_id=1, source_target_pairs={{0,1},{1,0},{2,3},{3,2},{4,5},{5,4},{6,7},{7,6},{8,9},{9,8},{10,11... | collective-permute-start | bytes 786440 | tf_op jit(solution)/shard_map/ppermute | solution.py:34
  63.4 5.8 %attend.1 = (bf16[1,8,512,128]{3,2,1,0:T(8,128)(2,1)}, bf16[1,8,512,128]{3,2,1,0:T(8,128)(2,1)}, bf16[8,64,256]{2,1,0:T(8,128)(2,1)S(1)}, bf16[8,64,256]{2,1,0:T(8,128)(2,1)S(1)}) custom-call(s32[4]{0:T(128)S(1)} %pad_add_fusion.pos, s32[8]{0:T(128)S(1)} %copy-done.2, bf16[1,8,512,128]{3,2,1,0:T(8,128)(2,1)S(1)} %copy-done, ...), custom_call_target="tpu_custom_call" | custom-call | tf_op jit(solution)/shard_map/attend/pallas_call | solution.py:287
  70.7 3.4 %shard_map.87 = (bf16[2,8,64,256]{3,2,1,0:T(8,128)(2,1)S(1)}, bf16[2,8,64,256]{3,2,1,0:T(8,128)(2,1)S(1)}, bf16[2,8,64,256]{3,2,1,0:T(8,128)(2,1)S(1)}, bf16[2,8...) custom-call(s32[4]{0:T(128)S(1)} %pad_add_fusion.pos, ...), custom_call_target="tpu_custom_call" | custom-call | tf_op jit(solution)/shard_map/pallas_call | solution.py:275
  76.5 7.7 %shard_map.89 = (bf16[16,256,256]{2,1,0:T(8,128)(2,1)S(1)}, bf16[16,256,256]{2,1,0:T(8,128)(2,1)S(1)}) custom-call(s32[4]{0:T(128)S(1)} %pad_add_fusion.pos, bf16[2,8,64,256]{3,2,1,0:T(8,128)(2,1)S(1)} %pad_maximum_fusion.refs_0_, bf16[2,8,64,256]{3,2,1,0:T(8,128)(2,1)S(1)} %pad_maximum_fusion.1.refs_1_, ...), custom_call_target="tpu_custom_call" | custom-call | tf_op jit(solution)/shard_map/pallas_call | solution.py:367
  91.5 3.4 %collective-permute-done.24 = bf16[2,8,64,256]{3,2,1,0:T(8,128)(2,1)S(1)} collective-permute-done((bf16[2,8,64,256]{3,2,1,0:T(8,128)(2,1)S(1)}, bf16[2,8,64,256]{3,2,1,0:T(8,128)(2,1)S(1)}, u32[]{:S(2)}, u32[]{:S(2)}) %collective-permute-start.24) | collective-permute-done | bytes 524320 | tf_op jit(solution)/shard_map/ppermute | solution.py:43
  95.1 3.5 %collective-permute-start.25 = (bf16[2,8,64,256]{3,2,1,0:T(8,128)(2,1)S(1)}, bf16[2,8,64,256]{3,2,1,0:T(8,128)(2,1)S(1)}, u32[]{:S(2)}, u32[]{:S(2)}) collective-permute-start(bf16[2,8,64,256]{3,2,1,0:T(8,128)(2,1)S(1)} %add_convert_fusion.1), channel_id=1, source_target_pairs={{0,192},{1,25},{2,194},{3,27},{4,196},{5,29},{6,198},{7,31},{8,200... | collective-permute-start | bytes 1572872 | tf_op jit(solution)/shard_map/ppermute | solution.py:43
  98.8 5.1 %collective-permute-done.23 = bf16[2,8,64,256]{3,2,1,0:T(8,128)(2,1)S(1)} collective-permute-done((bf16[2,8,64,256]{3,2,1,0:T(8,128)(2,1)S(1)}, bf16[2,8,64,256]{3,2,1,0:T(8,128)(2,1)S(1)}, u32[]{:S(2)}, u32[]{:S(2)}) %collective-permute-start.23) | collective-permute-done | bytes 524320 | tf_op jit(solution)/shard_map/ppermute | solution.py:43
  113.9 3.3 %collective-permute-done.22 = bf16[8,64,256]{2,1,0:T(8,128)(2,1)S(1)} collective-permute-done((bf16[8,64,256]{2,1,0:T(8,128)(2,1)}, bf16[8,64,256]{2,1,0:T(8,128)(2,1)S(1)}, u32[]{:S(2)}, u32[]{:S(2)}) %collective-permute-start.22) | collective-permute-done | bytes 262176 | tf_op jit(solution)/shard_map/ppermute | solution.py:43
  117.3 4.4 %collective-permute-start.28 = (bf16[3,64,256]{2,1,0:T(8,128)(2,1)S(1)}, bf16[3,64,256]{2,1,0:T(8,128)(2,1)S(1)}, u32[]{:S(2)}, u32[]{:S(2)}) collective-permute-start(bf16[3,64,256]{2,1,0:T(8,128)(2,1)S(1)} %pad_maximum_fusion.4), channel_id=1, source_target_pairs={{0,1},{1,0},{2,3},{3,2},{4,5},{5,4},{6,7},{7,6},{8,9},{9,8},{10,11... | collective-permute-start | bytes 294920 | tf_op jit(solution)/shard_map/ppermute | solution.py:34
  128.1 2.8 %collective-permute-start.32 = (bf16[64,256]{1,0:T(8,128)(2,1)S(1)}, bf16[64,256]{1,0:T(8,128)(2,1)S(1)}, u32[]{:S(2)}, u32[]{:S(2)}) collective-permute-start(bf16[64,256]{1,0:T(8,128)(2,1)S(1)} %get-tuple-element.44), channel_id=1, source_target_pairs={{0,4},{1,5},{2,6},{3,7},{4,0},{5,1},{6,2},{7,3},{8,12},{9,13},{10,... | collective-permute-start | bytes 98312 | tf_op jit(solution)/shard_map/ppermute | solution.py:34
  131.5 3.3 %collective-permute-done.32 = bf16[64,256]{1,0:T(8,128)(2,1)S(1)} collective-permute-done((bf16[64,256]{1,0:T(8,128)(2,1)S(1)}, bf16[64,256]{1,0:T(8,128)(2,1)S(1)}, u32[]{:S(2)}, u32[]{:S(2)}) %collective-permute-start.32) | collective-permute-done | bytes 32800 | tf_op jit(solution)/shard_map/ppermute | solution.py:34
  (94 shorter events, 48.2 us)
Async XLA Ops:
  7.1 37.1 %collective-permute-start.13 = (bf16[16,256,256]{2,1,0:T(8,128)(2,1)S(1)}, bf16[16,256,256]{2,1,0:T(8,128)(2,1)}, u32[]{:S(2)}, u32[]{:S(2)}) collective-permute-start(bf16[16,256,256]{2,1,0:T(8,128)(2,1)S(1)} %reshape.125.refs_2_.refs_4_.wo), channel_id=1, source_target_pairs={{0,1},{1,0},{2,3},{3,2},{4,5},{5,4},{6,7},{7,6},{8,9},{9,8},{10,11... | collective-permute-start | bytes 6291464 | tf_op jit(solution)/shard_map/ppermute | solution.py:34
  7.2 10.2 %collective-permute-start.2 = (bf16[2,64,256]{2,1,0:T(8,128)(2,1)S(1)}, bf16[2,64,256]{2,1,0:T(8,128)(2,1)S(1)}, u32[]{:S(2)}, u32[]{:S(2)}) collective-permute-start(bf16[2,64,256]{2,1,0:T(8,128)(2,1)S(1)} %maximum_select_fusion.1), channel_id=1, source_target_pairs={{0,2},{1,7},{2,4},{3,1},{4,6},{5,3},{6,0},{7,5},{8,10},{9,15},{10,... | collective-permute-start | bytes 196616 | tf_op jit(solution)/shard_map/ppermute | solution.py:51
  12.9 8.5 %collective-permute-start.4 = (bf16[64,256]{1,0:T(8,128)(2,1)S(1)}, bf16[64,256]{1,0:T(8,128)(2,1)S(1)}, u32[]{:S(2)}, u32[]{:S(2)}) collective-permute-start(bf16[64,256]{1,0:T(8,128)(2,1)S(1)} %slice_select_fusion.1), channel_id=1, source_target_pairs={{0,4},{1,5},{2,6},{3,7},{4,0},{5,1},{6,2},{7,3},{8,12},{9,13},{10,... | collective-permute-start | bytes 98312 | tf_op jit(solution)/shard_map/ppermute | solution.py:34
  21.5 7.1 %collective-permute-start.9 = (bf16[8,64,256]{2,1,0:T(8,128)(2,1)S(1)}, bf16[8,64,256]{2,1,0:T(8,128)(2,1)S(1)}, u32[]{:S(2)}, u32[]{:S(2)}) collective-permute-start(bf16[8,64,256]{2,1,0:T(8,128)(2,1)S(1)} %get-tuple-element.52), channel_id=1, source_target_pairs={{0,16},{1,129},{2,18},{3,131},{4,20},{5,133},{6,22},{7,135},{8,24}... | collective-permute-start | bytes 786440 | tf_op jit(solution)/shard_map/ppermute | solution.py:43
  24.3 7.2 %collective-permute-start.10 = (bf16[8,64,256]{2,1,0:T(8,128)(2,1)S(1)}, bf16[8,64,256]{2,1,0:T(8,128)(2,1)S(1)}, u32[]{:S(2)}, u32[]{:S(2)}) collective-permute-start(bf16[8,64,256]{2,1,0:T(8,128)(2,1)S(1)} %get-tuple-element.52), channel_id=1, source_target_pairs={{0,24},{1,193},{2,26},{3,195},{4,28},{5,197},{6,30},{7,199},{8,0},... | collective-permute-start | bytes 786440 | tf_op jit(solution)/shard_map/ppermute | solution.py:43
  25.1 9.2 %collective-permute-start.6 = (bf16[8,64,256]{2,1,0:T(8,128)(2,1)S(1)}, bf16[8,64,256]{2,1,0:T(8,128)(2,1)S(1)}, u32[]{:S(2)}, u32[]{:S(2)}) collective-permute-start(bf16[8,64,256]{2,1,0:T(8,128)(2,1)S(1)} %get-tuple-element.52), channel_id=1, source_target_pairs={{0,8},{1,65},{2,10},{3,67},{4,12},{5,69},{6,14},{7,71},{8,16},{9,7... | collective-permute-start | bytes 786440 | tf_op jit(solution)/shard_map/ppermute | solution.py:43
  31.5 8.9 %collective-permute-start.11 = (bf16[2,8,64,256]{3,2,1,0:T(8,128)(2,1)S(1)}, bf16[2,8,64,256]{3,2,1,0:T(8,128)(2,1)}, u32[]{:S(2)}, u32[]{:S(2)}) collective-permute-start(bf16[2,8,64,256]{3,2,1,0:T(8,128)(2,1)S(1)} %pad_maximum_fusion.1.refs_1_), channel_id=1, source_target_pairs={{0,192},{1,25},{2,194},{3,27},{4,196},{5,29},{6,198},{7,31},{8,200... | collective-permute-start | bytes 1572872 | tf_op jit(solution)/shard_map/ppermute | solution.py:43
  34.4 9.7 %collective-permute-start.7 = (bf16[2,8,64,256]{3,2,1,0:T(8,128)(2,1)S(1)}, bf16[2,8,64,256]{3,2,1,0:T(8,128)(2,1)}, u32[]{:S(2)}, u32[]{:S(2)}) collective-permute-start(bf16[2,8,64,256]{3,2,1,0:T(8,128)(2,1)S(1)} %pad_maximum_fusion.refs_0_), channel_id=1, source_target_pairs={{0,64},{1,9},{2,66},{3,11},{4,68},{5,13},{6,70},{7,15},{8,72},{9,1... | collective-permute-start | bytes 1572872 | tf_op jit(solution)/shard_map/ppermute | solution.py:43
  34.5 15.2 %collective-permute-start.14 = (bf16[2,8,64,256]{3,2,1,0:T(8,128)(2,1)S(1)}, bf16[2,8,64,256]{3,2,1,0:T(8,128)(2,1)}, u32[]{:S(2)}, u32[]{:S(2)}) collective-permute-start(bf16[2,8,64,256]{3,2,1,0:T(8,128)(2,1)S(1)} %pad_maximum_fusion.1.refs_1_), channel_id=1, source_target_pairs={{0,64},{1,9},{2,66},{3,11},{4,68},{5,13},{6,70},{7,15},{8,72},{9,1... | collective-permute-start | bytes 1572872 | tf_op jit(solution)/shard_map/ppermute | solution.py:43
  34.6 15.2 %collective-permute-start.15 = (bf16[2,8,64,256]{3,2,1,0:T(8,128)(2,1)S(1)}, bf16[2,8,64,256]{3,2,1,0:T(8,128)(2,1)}, u32[]{:S(2)}, u32[]{:S(2)}) collective-permute-start(bf16[2,8,64,256]{3,2,1,0:T(8,128)(2,1)S(1)} %pad_maximum_fusion.refs_0_), channel_id=1, source_target_pairs={{0,192},{1,25},{2,194},{3,27},{4,196},{5,29},{6,198},{7,31},{8,200... | collective-permute-start | bytes 1572872 | tf_op jit(solution)/shard_map/ppermute | solution.py:43
  40.5 12.8 %collective-permute-start.12 = (bf16[2,8,64,256]{3,2,1,0:T(8,128)(2,1)}, bf16[2,8,64,256]{3,2,1,0:T(8,128)(2,1)}, u32[]{:S(2)}, u32[]{:S(2)}) collective-permute-start(bf16[2,8,64,256]{3,2,1,0:T(8,128)(2,1)} %collective-permute-done.11.refs_3_.refs_7_), channel_id=1, source_target_pairs={{0,192},{1,25},{2,194},{3,27},{4,196},{5,29},{6,198},{7,31},{8,200... | collective-permute-start | bytes 1572872 | tf_op jit(solution)/shard_map/ppermute | solution.py:43
  44.1 11.2 %collective-permute-start.8 = (bf16[2,8,64,256]{3,2,1,0:T(8,128)(2,1)}, bf16[2,8,64,256]{3,2,1,0:T(8,128)(2,1)}, u32[]{:S(2)}, u32[]{:S(2)}) collective-permute-start(bf16[2,8,64,256]{3,2,1,0:T(8,128)(2,1)} %collective-permute-done.7.refs_0_.refs_2_), channel_id=1, source_target_pairs={{0,64},{1,9},{2,66},{3,11},{4,68},{5,13},{6,70},{7,15},{8,72},{9,1... | collective-permute-start | bytes 1572872 | tf_op jit(solution)/shard_map/ppermute | solution.py:43
  84.2 26.0 %collective-permute-start.21 = (bf16[16,256,256]{2,1,0:T(8,128)(2,1)S(1)}, bf16[16,256,256]{2,1,0:T(8,128)(2,1)S(1)}, u32[]{:S(2)}, u32[]{:S(2)}) collective-permute-start(bf16[16,256,256]{2,1,0:T(8,128)(2,1)S(1)} %get-tuple-element.33), channel_id=1, source_target_pairs={{0,1},{1,0},{2,3},{3,2},{4,5},{5,4},{6,7},{7,6},{8,9},{9,8},{10,11... | collective-permute-start | bytes 6291464 | tf_op jit(solution)/shard_map/ppermute | solution.py:34
  86.6 8.3 %collective-permute-start.24 = (bf16[2,8,64,256]{3,2,1,0:T(8,128)(2,1)S(1)}, bf16[2,8,64,256]{3,2,1,0:T(8,128)(2,1)S(1)}, u32[]{:S(2)}, u32[]{:S(2)}) collective-permute-start(bf16[2,8,64,256]{3,2,1,0:T(8,128)(2,1)S(1)} %get-tuple-element.39), channel_id=1, source_target_pairs={{0,192},{1,25},{2,194},{3,27},{4,196},{5,29},{6,198},{7,31},{8,200... | collective-permute-start | bytes 1572872 | tf_op jit(solution)/shard_map/ppermute | solution.py:43
  88.8 9.8 %collective-permute-start.18 = (bf16[2,8,64,256]{3,2,1,0:T(8,128)(2,1)S(1)}, bf16[2,8,64,256]{3,2,1,0:T(8,128)(2,1)S(1)}, u32[]{:S(2)}, u32[]{:S(2)}) collective-permute-start(bf16[2,8,64,256]{3,2,1,0:T(8,128)(2,1)S(1)} %get-tuple-element.30), channel_id=1, source_target_pairs={{0,64},{1,9},{2,66},{3,11},{4,68},{5,13},{6,70},{7,15},{8,72},{9,1... | collective-permute-start | bytes 1572872 | tf_op jit(solution)/shard_map/ppermute | solution.py:43
  88.8 15.2 %collective-permute-start.23 = (bf16[2,8,64,256]{3,2,1,0:T(8,128)(2,1)S(1)}, bf16[2,8,64,256]{3,2,1,0:T(8,128)(2,1)S(1)}, u32[]{:S(2)}, u32[]{:S(2)}) collective-permute-start(bf16[2,8,64,256]{3,2,1,0:T(8,128)(2,1)S(1)} %get-tuple-element.37), channel_id=1, source_target_pairs={{0,64},{1,9},{2,66},{3,11},{4,68},{5,13},{6,70},{7,15},{8,72},{9,1... | collective-permute-start | bytes 1572872 | tf_op jit(solution)/shard_map/ppermute | solution.py:43
  88.8 18.6 %collective-permute-start.20 = (bf16[2,8,64,256]{3,2,1,0:T(8,128)(2,1)S(1)}, bf16[2,8,64,256]{3,2,1,0:T(8,128)(2,1)S(1)}, u32[]{:S(2)}, u32[]{:S(2)}) collective-permute-start(bf16[2,8,64,256]{3,2,1,0:T(8,128)(2,1)S(1)} %get-tuple-element.31), channel_id=1, source_target_pairs={{0,192},{1,25},{2,194},{3,27},{4,196},{5,29},{6,198},{7,31},{8,200... | collective-permute-start | bytes 1572872 | tf_op jit(solution)/shard_map/ppermute | solution.py:43
  95.1 11.1 %collective-permute-start.25 = (bf16[2,8,64,256]{3,2,1,0:T(8,128)(2,1)S(1)}, bf16[2,8,64,256]{3,2,1,0:T(8,128)(2,1)S(1)}, u32[]{:S(2)}, u32[]{:S(2)}) collective-permute-start(bf16[2,8,64,256]{3,2,1,0:T(8,128)(2,1)S(1)} %add_convert_fusion.1), channel_id=1, source_target_pairs={{0,192},{1,25},{2,194},{3,27},{4,196},{5,29},{6,198},{7,31},{8,200... | collective-permute-start | bytes 1572872 | tf_op jit(solution)/shard_map/ppermute | solution.py:43
  98.8 10.5 %collective-permute-start.19 = (bf16[2,8,64,256]{3,2,1,0:T(8,128)(2,1)S(1)}, bf16[2,8,64,256]{3,2,1,0:T(8,128)(2,1)S(1)}, u32[]{:S(2)}, u32[]{:S(2)}) collective-permute-start(bf16[2,8,64,256]{3,2,1,0:T(8,128)(2,1)S(1)} %add_convert_fusion.2), channel_id=1, source_target_pairs={{0,64},{1,9},{2,66},{3,11},{4,68},{5,13},{6,70},{7,15},{8,72},{9,1... | collective-permute-start | bytes 1572872 | tf_op jit(solution)/shard_map/ppermute | solution.py:43
  107.1 6.7 %collective-permute-start.27 = (bf16[8,64,256]{2,1,0:T(8,128)(2,1)S(1)}, bf16[8,64,256]{2,1,0:T(8,128)(2,1)S(1)}, u32[]{:S(2)}, u32[]{:S(2)}) collective-permute-start(bf16[8,64,256]{2,1,0:T(8,128)(2,1)S(1)} %get-tuple-element.43), channel_id=1, source_target_pairs={{0,16},{1,129},{2,18},{3,131},{4,20},{5,133},{6,22},{7,135},{8,24}... | collective-permute-start | bytes 786440 | tf_op jit(solution)/shard_map/ppermute | solution.py:43
  110.2 6.9 %collective-permute-start.22 = (bf16[8,64,256]{2,1,0:T(8,128)(2,1)}, bf16[8,64,256]{2,1,0:T(8,128)(2,1)S(1)}, u32[]{:S(2)}, u32[]{:S(2)}) collective-permute-start(bf16[8,64,256]{2,1,0:T(8,128)(2,1)} %get-tuple-element.40), channel_id=1, source_target_pairs={{0,8},{1,65},{2,10},{3,67},{4,12},{5,69},{6,14},{7,71},{8,16},{9,7... | collective-permute-start | bytes 786440 | tf_op jit(solution)/shard_map/ppermute | solution.py:43
  122.6 8.3 %collective-permute-start.29 = (bf16[2,64,256]{2,1,0:T(8,128)(2,1)S(1)}, bf16[2,64,256]{2,1,0:T(8,128)(2,1)S(1)}, u32[]{:S(2)}, u32[]{:S(2)}) collective-permute-start(bf16[2,64,256]{2,1,0:T(8,128)(2,1)S(1)} %pad_maximum_fusion.5), channel_id=1, source_target_pairs={{0,34},{1,37},{2,36},{3,39},{4,38},{5,33},{6,32},{7,35},{8,42},{9,... | collective-permute-start | bytes 196616 | tf_op jit(solution)/shard_map/ppermute | solution.py:51
  123.4 7.5 %collective-permute-start.30 = (bf16[2,64,256]{2,1,0:T(8,128)(2,1)S(1)}, bf16[2,64,256]{2,1,0:T(8,128)(2,1)S(1)}, u32[]{:S(2)}, u32[]{:S(2)}) collective-permute-start(bf16[2,64,256]{2,1,0:T(8,128)(2,1)S(1)} %pad_maximum_fusion.6), channel_id=1, source_target_pairs={{0,2},{1,7},{2,4},{3,1},{4,6},{5,3},{6,0},{7,5},{8,10},{9,15},{10,... | collective-permute-start | bytes 196616 | tf_op jit(solution)/shard_map/ppermute | solution.py:51
  128.1 6.7 %collective-permute-start.32 = (bf16[64,256]{1,0:T(8,128)(2,1)S(1)}, bf16[64,256]{1,0:T(8,128)(2,1)S(1)}, u32[]{:S(2)}, u32[]{:S(2)}) collective-permute-start(bf16[64,256]{1,0:T(8,128)(2,1)S(1)} %get-tuple-element.44), channel_id=1, source_target_pairs={{0,4},{1,5},{2,6},{3,7},{4,0},{5,1},{6,2},{7,3},{8,12},{9,13},{10,... | collective-permute-start | bytes 98312 | tf_op jit(solution)/shard_map/ppermute | solution.py:34
  (14 other events, 85.0 us)

commit v3 on v2

--- a/solution.py
+++ b/solution.py
@@ -67,43 +67,54 @@
     n = len(which)
     x, y, z, c = pos[0], pos[1], pos[2], pos[3]
     pieces, (wo, wp), refs = refs[: 2 * n], refs[2 * n : 2 * n + 2], refs[2 * n + 2 :]
-    if not first:
+    if first:
+        refs[0][...] = wp[...]
+    else:
         before, refs = refs[0], refs[1:]
     acc = refs[-1]
 
-    def piece(outer, inner):
-        return pieces[2 * which.index(outer) + inner // 2].at[inner % 2]
-
-    def product(dys, dxs, source):
+    def product(dy, dxs, source):
+        f = ((y + 4 - dy) & 3) * 4
+        columns = []
+        for zh in range(4):
+            rows = [source(dx)[slot_of(c, z, zh, zl)] for dx in dxs for zl in range(2)]
+            columns.append(jnp.concatenate(rows, axis=0))
+        lhs = jnp.concatenate(columns, axis=1)
+        own = nn(lhs, wo[pl.ds(f, 4)].reshape(1024, 256))
+        return own, nn(lhs, wp[pl.ds(f, 4)].reshape(1024, 256))
+
+    @pl.when(c == 0)
+    def _():
+        for dx in range(4):
+            to = slice(dx * 128, dx * 128 + 128)
+            if dx in which or first:
+                acc[to] = jnp.zeros((128, 512), F32)
+            else:
+                acc[to] = before[to]
+        for half in range(2):
+
+            def step(inner, _):
+                own, par = product(
+                    2 * half + inner,
+                    which,
+                    lambda dx: pieces[2 * which.index(dx) + half].at[inner],
+                )
+                for i, dx in enumerate(which):
+                    acc[dx * 128 : dx * 128 + 128, :256] += own[i * 128 : i * 128 + 128]
+                    acc[dx * 128 : dx * 128 + 128, 256:] += par[i * 128 : i * 128 + 128]
+                return 0
+
+            lax.fori_loop(0, 2, step, 0)
+
+    @pl.when(c == 1)
+    def _():
         own, par = None, None
-        for dy in dys:
-            yy = (y + 4 - dy) & 3
-            columns = []
-            for zh in range(4):
-                rows = [source(dx, dy)[slot_of(c, z, zh, zl)] for dx in dxs for zl in range(2)]
-                columns.append(jnp.concatenate(rows, axis=0))
-            lhs = jnp.concatenate(columns, axis=1)
-            own_term = nn(lhs, wo[pl.ds(yy * 4, 4)].reshape(1024, 256))
-            par_term = nn(lhs, wp[pl.ds(yy * 4, 4)].reshape(1024, 256))
+        for i, dy in enumerate(which):
+            own_term, par_term = product(
+                dy, range(4), lambda dx: pieces[2 * i + dx // 2].at[dx % 2]
+            )
             own = own_term if own is None else own + own_term
             par = par_term if par is None else par + par_term
-        return own, par
-
-    @pl.when(c == 0)
-    def _():
-        own, par = product(range(4), which, piece)
-        for dx in range(4):
-            to = slice(dx * 128, dx * 128 + 128)
-            if dx in which:
-                at = which.index(dx) * 128
-                acc[to, :256] = own[at : at + 128]
-                acc[to, 256:] = par[at : at + 128]
-            elif not first:
-                acc[to] = before[to]
-
-    @pl.when(c == 1)
-    def _():
-        own, par = product(which, range(4), lambda dx, dy: piece(dy, dx))
         if first:
             acc[:, :256] = own
             acc[:, 256:] = par
@@ -262,11 +273,14 @@
     first = before is None
     acc = ((512, 512), F32)
     half = ((8, 64, 256), BF)
+    outs = [half, half] if last else [acc]
+    if first:
+        outs = [((16, 256, 256), BF), acc]
     return whole(
         functools.partial(project_kernel, which, first, last),
         [VMEM] * (2 * len(which) + (2 if first else 3)),
-        [half, half] if last else [acc],
-        [VMEM] * (2 if last else 1),
+        outs,
+        [VMEM] * len(outs),
         [pltpu.VMEM((512, 512), F32)] if last else [],
     )(pos, *pieces, w_own, w_par, *([] if first else [before]))
 
@@ -344,18 +358,19 @@
     far_high = cross(left_high, 3, 0)
     near = (right_low, right_high, left_low, left_high)
 
-    (acc,) = project((0,), pos, (low, high), w_own, w_par, None, False)
+    w_par, acc = project((0,), pos, (low, high), w_own, w_par, None, False)
     (acc,) = project((1, 3), pos, near, w_own, w_par, acc, False)
     keep, send = project((2,), pos, (far_low, far_high), w_own, w_par, acc, True)
     recv = shift(send, dc=1)
     context, query_grad, grad_keep, grad_send = attend(pos, enc_len, queries, d_context, keep, recv)
     grad_recv = shift(grad_send, dc=1)
 
-    right_low_g, right_high_g, far_low_g, far_high_g, left_low_g, left_high_g = spread(
-        (1, 2, 3), pos, grad_keep, grad_recv, w_own, w_par, ()
-    )
+    far_low_g, far_high_g = spread((2,), pos, grad_keep, grad_recv, w_own, w_par, ())
     pass_low = cross(far_low_g, 1, 0)
     pass_high = cross(far_high_g, 3, 0)
+    right_low_g, right_high_g, left_low_g, left_high_g = spread(
+        (1, 3), pos, grad_keep, grad_recv, w_own, w_par, (far_low_g,)
+    )
     from_left_high = cross(right_high_g, 1, 0)
     from_right_low = cross(left_low_g, 3, 0)
     own_low, own_high = spread(

time: 139 us -> 138 us (level)
  Pallas kernels: 28 us -> 25.4 us
  starting transfers between devices: 58.8 us -> 60.4 us
    ppermute x10, starting transfers between devices: 25.8 us -> 27.4 us  [shift(): return lax.ppermute(value, AXES, pairs)]
    pallas_call x2 -> x3, Pallas kernels: 5.8 us -> 4.43 us  [spread(): whole(functools.partial(spread_kernel, which, len(after)), [VMEM] * 4 + [...]
where the time goes in v3:
time: 138 us
  starting transfers between devices  60.4 us (44%)
  waiting for transfers between devices  41.9 us (30%)
  Pallas kernels  25.4 us (18%)
  local copies, waits for them, and re-layouts  5.27 us (4%)
  other arithmetic  4.11 us (3%)
    ppermute x18, waiting for transfers between devices, cross(): return lax.ppermute(value, AXES, pairs)  31.9 us
    ppermute x10, starting transfers between devices, shift(): return lax.ppermute(value, AXES, pairs)  27.4 us
    ppermute x18, starting transfers between devices, cross(): return lax.ppermute(value, AXES, pairs)  21.9 us
    ppermute x6, starting transfers between devices, rise(): return lax.ppermute(value, AXES, pairs)  11.1 us
    ppermute x10, waiting for transfers between devices, shift(): return lax.ppermute(value, AXES, pairs)  9.35 us
    pallas_call x1, Pallas kernels, shards(): whole(weight_kernel, [VMEM] * 10 + [HBM], [((16, 256, 256), BF)] * 2, [VM...  7.69 us
    pallas_call x3, Pallas kernels, project(): whole(functools.partial(project_kernel, which, first, last), [VMEM] * (2...  7.4 us
    pallas_call x1, Pallas kernels, attend(): pl.pallas_call(attend_kernel, grid_spec=pltpu.PrefetchScalarGridSpec(num_...  5.84 us
  transfers between devices with their start and end apart: 34, of which 20 were waited for; matrix products, arithmetic and copies ran while one was open for 6% of the time, Pallas kernels for 4%

profile of v3, /device:TPU:1, one launch (start us, length us, event | category | flops | bytes accessed | tf_op | source)
XLA Modules:
  0.0 137.9 jit_solution(1588403708093589579)
XLA Ops:
  0.6 3.3 %collective-permute-start = (bf16[128,128]{1,0:T(8,128)(2,1)}, bf16[128,128]{1,0:T(8,128)(2,1)S(1)}, u32[]{:S(2)}, u32[]{:S(2)}) collective-permute-start(bf16[128,128]{1,0:T(8,128)(2,1)} %bitcast.58), channel_id=1, source_target_pairs={{0,1},{1,0},{2,3},{3,2},{4,5},{5,4},{6,7},{7,6},{8,9},{9,8},{10,11... | collective-permute-start | bytes 98312 | tf_op jit(solution)/shard_map/ppermute | solution.py:34
  3.9 3.2 %reshape.125.refs_2_.refs_4_.wo = bf16[16,256,256]{2,1,0:T(8,128)(2,1)S(1)} reshape(bf16[1,4096,2,128]{3,2,1,0:T(2,128)(2,1)} %param.7) | data formatting | bytes 4194304 | tf_op jit(solution)/shard_map/reshape | solution.py:345
  7.2 4.4 %collective-permute-start.2 = (bf16[2,64,256]{2,1,0:T(8,128)(2,1)S(1)}, bf16[2,64,256]{2,1,0:T(8,128)(2,1)S(1)}, u32[]{:S(2)}, u32[]{:S(2)}) collective-permute-start(bf16[2,64,256]{2,1,0:T(8,128)(2,1)S(1)} %maximum_select_fusion.1), channel_id=1, source_target_pairs={{0,2},{1,7},{2,4},{3,1},{4,6},{5,3},{6,0},{7,5},{8,10},{9,15},{10,... | collective-permute-start | bytes 196616 | tf_op jit(solution)/shard_map/ppermute | solution.py:51
  12.9 4.5 %collective-permute-start.4 = (bf16[64,256]{1,0:T(8,128)(2,1)S(1)}, bf16[64,256]{1,0:T(8,128)(2,1)S(1)}, u32[]{:S(2)}, u32[]{:S(2)}) collective-permute-start(bf16[64,256]{1,0:T(8,128)(2,1)S(1)} %slice_select_fusion.1), channel_id=1, source_target_pairs={{0,4},{1,5},{2,6},{3,7},{4,0},{5,1},{6,2},{7,3},{8,12},{9,13},{10,... | collective-permute-start | bytes 98312 | tf_op jit(solution)/shard_map/ppermute | solution.py:34
  21.5 2.8 %collective-permute-start.9 = (bf16[8,64,256]{2,1,0:T(8,128)(2,1)S(1)}, bf16[8,64,256]{2,1,0:T(8,128)(2,1)S(1)}, u32[]{:S(2)}, u32[]{:S(2)}) collective-permute-start(bf16[8,64,256]{2,1,0:T(8,128)(2,1)S(1)} %get-tuple-element.56), channel_id=1, source_target_pairs={{0,16},{1,129},{2,18},{3,131},{4,20},{5,133},{6,22},{7,135},{8,24}... | collective-permute-start | bytes 786440 | tf_op jit(solution)/shard_map/ppermute | solution.py:43
  25.7 2.9 %collective-permute-done.9 = bf16[8,64,256]{2,1,0:T(8,128)(2,1)S(1)} collective-permute-done((bf16[8,64,256]{2,1,0:T(8,128)(2,1)S(1)}, bf16[8,64,256]{2,1,0:T(8,128)(2,1)S(1)}, u32[]{:S(2)}, u32[]{:S(2)}) %collective-permute-start.9) | collective-permute-done | bytes 262176 | tf_op jit(solution)/shard_map/ppermute | solution.py:43
  28.6 2.9 %collective-permute-done.10 = bf16[8,64,256]{2,1,0:T(8,128)(2,1)S(1)} collective-permute-done((bf16[8,64,256]{2,1,0:T(8,128)(2,1)S(1)}, bf16[8,64,256]{2,1,0:T(8,128)(2,1)S(1)}, u32[]{:S(2)}, u32[]{:S(2)}) %collective-permute-start.10) | collective-permute-done | bytes 262176 | tf_op jit(solution)/shard_map/ppermute | solution.py:43
  31.5 2.8 %collective-permute-start.11 = (bf16[2,8,64,256]{3,2,1,0:T(8,128)(2,1)S(1)}, bf16[2,8,64,256]{3,2,1,0:T(8,128)(2,1)}, u32[]{:S(2)}, u32[]{:S(2)}) collective-permute-start(bf16[2,8,64,256]{3,2,1,0:T(8,128)(2,1)S(1)} %pad_maximum_fusion.1.refs_1_), channel_id=1, source_target_pairs={{0,192},{1,25},{2,194},{3,27},{4,196},{5,29},{6,198},{7,31},{8,200... | collective-permute-start | bytes 1572872 | tf_op jit(solution)/shard_map/ppermute | solution.py:43
  37.3 3.2 %collective-permute-done.11.refs_3_.refs_7_ = bf16[2,8,64,256]{3,2,1,0:T(8,128)(2,1)} collective-permute-done((bf16[2,8,64,256]{3,2,1,0:T(8,128)(2,1)S(1)}, bf16[2,8,64,256]{3,2,1,0:T(8,128)(2,1)}, u32[]{:S(2)}, u32[]{:S(2)}) %collective-permute-start.11) | collective-permute-done | bytes 524320 | tf_op jit(solution)/shard_map/ppermute | solution.py:43
  40.5 3.2 %collective-permute-start.12 = (bf16[2,8,64,256]{3,2,1,0:T(8,128)(2,1)}, bf16[2,8,64,256]{3,2,1,0:T(8,128)(2,1)}, u32[]{:S(2)}, u32[]{:S(2)}) collective-permute-start(bf16[2,8,64,256]{3,2,1,0:T(8,128)(2,1)} %collective-permute-done.11.refs_3_.refs_7_), channel_id=1, source_target_pairs={{0,192},{1,25},{2,194},{3,27},{4,196},{5,29},{6,198},{7,31},{8,200... | collective-permute-start | bytes 1572872 | tf_op jit(solution)/shard_map/ppermute | solution.py:43
  46.8 2.9 %collective-permute-done.14.refs_1_.refs_3_ = bf16[2,8,64,256]{3,2,1,0:T(8,128)(2,1)} collective-permute-done((bf16[2,8,64,256]{3,2,1,0:T(8,128)(2,1)S(1)}, bf16[2,8,64,256]{3,2,1,0:T(8,128)(2,1)}, u32[]{:S(2)}, u32[]{:S(2)}) %collective-permute-start.14) | collective-permute-done | bytes 524320 | tf_op jit(solution)/shard_map/ppermute | solution.py:43
  49.7 2.8 %shard_map.85.refs_4_ = f32[512,512]{1,0:T(8,128)S(1)} custom-call(s32[4]{0:T(128)S(1)} %pad_add_fusion.pos, bf16[2,8,64,256]{3,2,1,0:T(8,128)(2,1)} %collective-permute-done.7.refs_0_.refs_2_, bf16[2,8,64,256]{3,2,1,0:T(8,128)(2,1)} %collective-permute-done.14.refs_1_.refs_3_, bf16[2,8,64,256]{3,2,1,0:T(8,128)(2,1)} %collective-permute-done.15.refs_2_.refs_6_, ...), custom_call_target="tpu_custom_call" | custom-call | tf_op jit(solution)/shard_map/pallas_call | solution.py:279
  52.6 2.8 %collective-permute-done.8.refs_0_.refs_4_ = bf16[2,8,64,256]{3,2,1,0:T(8,128)(2,1)} collective-permute-done((bf16[2,8,64,256]{3,2,1,0:T(8,128)(2,1)}, bf16[2,8,64,256]{3,2,1,0:T(8,128)(2,1)}, u32[]{:S(2)}, u32[]{:S(2)}) %collective-permute-start.8) | collective-permute-done | bytes 524320 | tf_op jit(solution)/shard_map/ppermute | solution.py:43
  57.4 4.7 %collective-permute-start.16 = (bf16[8,64,256]{2,1,0:T(8,128)(2,1)S(1)}, bf16[8,64,256]{2,1,0:T(8,128)(2,1)S(1)}, u32[]{:S(2)}, u32[]{:S(2)}) collective-permute-start(bf16[8,64,256]{2,1,0:T(8,128)(2,1)S(1)} %get-tuple-element.27), channel_id=1, source_target_pairs={{0,1},{1,0},{2,3},{3,2},{4,5},{5,4},{6,7},{7,6},{8,9},{9,8},{10,11... | collective-permute-start | bytes 786440 | tf_op jit(solution)/shard_map/ppermute | solution.py:34
  63.3 5.8 %attend.1 = (bf16[1,8,512,128]{3,2,1,0:T(8,128)(2,1)}, bf16[1,8,512,128]{3,2,1,0:T(8,128)(2,1)}, bf16[8,64,256]{2,1,0:T(8,128)(2,1)S(1)}, bf16[8,64,256]{2,1,0:T(8,128)(2,1)S(1)}) custom-call(s32[4]{0:T(128)S(1)} %pad_add_fusion.pos, s32[8]{0:T(128)S(1)} %copy-done.2, bf16[1,8,512,128]{3,2,1,0:T(8,128)(2,1)S(1)} %copy-done, ...), custom_call_target="tpu_custom_call" | custom-call | tf_op jit(solution)/shard_map/attend/pallas_call | solution.py:301
  75.1 7.7 %shard_map.90 = (bf16[16,256,256]{2,1,0:T(8,128)(2,1)S(1)}, bf16[16,256,256]{2,1,0:T(8,128)(2,1)S(1)}) custom-call(s32[4]{0:T(128)S(1)} %pad_add_fusion.pos, bf16[2,8,64,256]{3,2,1,0:T(8,128)(2,1)S(1)} %pad_maximum_fusion.refs_0_, bf16[2,8,64,256]{3,2,1,0:T(8,128)(2,1)S(1)} %pad_maximum_fusion.1.refs_1_, ...), custom_call_target="tpu_custom_call" | custom-call | tf_op jit(solution)/shard_map/pallas_call | solution.py:382
  82.8 3.6 %collective-permute-start.21 = (bf16[16,256,256]{2,1,0:T(8,128)(2,1)S(1)}, bf16[16,256,256]{2,1,0:T(8,128)(2,1)S(1)}, u32[]{:S(2)}, u32[]{:S(2)}) collective-permute-start(bf16[16,256,256]{2,1,0:T(8,128)(2,1)S(1)} %get-tuple-element.37), channel_id=1, source_target_pairs={{0,1},{1,0},{2,3},{3,2},{4,5},{5,4},{6,7},{7,6},{8,9},{9,8},{10,11... | collective-permute-start | bytes 6291464 | tf_op jit(solution)/shard_map/ppermute | solution.py:34
  91.2 3.4 %collective-permute-done.24 = bf16[2,8,64,256]{3,2,1,0:T(8,128)(2,1)S(1)} collective-permute-done((bf16[2,8,64,256]{3,2,1,0:T(8,128)(2,1)S(1)}, bf16[2,8,64,256]{3,2,1,0:T(8,128)(2,1)S(1)}, u32[]{:S(2)}, u32[]{:S(2)}) %collective-permute-start.24) | collective-permute-done | bytes 524320 | tf_op jit(solution)/shard_map/ppermute | solution.py:43
  94.9 3.5 %collective-permute-start.25 = (bf16[2,8,64,256]{3,2,1,0:T(8,128)(2,1)S(1)}, bf16[2,8,64,256]{3,2,1,0:T(8,128)(2,1)S(1)}, u32[]{:S(2)}, u32[]{:S(2)}) collective-permute-start(bf16[2,8,64,256]{3,2,1,0:T(8,128)(2,1)S(1)} %add_convert_fusion.1), channel_id=1, source_target_pairs={{0,192},{1,25},{2,194},{3,27},{4,196},{5,29},{6,198},{7,31},{8,200... | collective-permute-start | bytes 1572872 | tf_op jit(solution)/shard_map/ppermute | solution.py:43
  98.6 5.1 %collective-permute-done.23 = bf16[2,8,64,256]{3,2,1,0:T(8,128)(2,1)S(1)} collective-permute-done((bf16[2,8,64,256]{3,2,1,0:T(8,128)(2,1)S(1)}, bf16[2,8,64,256]{3,2,1,0:T(8,128)(2,1)S(1)}, u32[]{:S(2)}, u32[]{:S(2)}) %collective-permute-start.23) | collective-permute-done | bytes 524320 | tf_op jit(solution)/shard_map/ppermute | solution.py:43
  113.6 3.3 %collective-permute-done.22 = bf16[8,64,256]{2,1,0:T(8,128)(2,1)S(1)} collective-permute-done((bf16[8,64,256]{2,1,0:T(8,128)(2,1)}, bf16[8,64,256]{2,1,0:T(8,128)(2,1)S(1)}, u32[]{:S(2)}, u32[]{:S(2)}) %collective-permute-start.22) | collective-permute-done | bytes 262176 | tf_op jit(solution)/shard_map/ppermute | solution.py:43
  117.1 4.2 %collective-permute-start.28 = (bf16[3,64,256]{2,1,0:T(8,128)(2,1)S(1)}, bf16[3,64,256]{2,1,0:T(8,128)(2,1)S(1)}, u32[]{:S(2)}, u32[]{:S(2)}) collective-permute-start(bf16[3,64,256]{2,1,0:T(8,128)(2,1)S(1)} %pad_maximum_fusion.4), channel_id=1, source_target_pairs={{0,1},{1,0},{2,3},{3,2},{4,5},{5,4},{6,7},{7,6},{8,9},{9,8},{10,11... | collective-permute-start | bytes 294920 | tf_op jit(solution)/shard_map/ppermute | solution.py:34
  127.7 2.8 %collective-permute-start.32 = (bf16[64,256]{1,0:T(8,128)(2,1)S(1)}, bf16[64,256]{1,0:T(8,128)(2,1)S(1)}, u32[]{:S(2)}, u32[]{:S(2)}) collective-permute-start(bf16[64,256]{1,0:T(8,128)(2,1)S(1)} %get-tuple-element.48), channel_id=1, source_target_pairs={{0,4},{1,5},{2,6},{3,7},{4,0},{5,1},{6,2},{7,3},{8,12},{9,13},{10,... | collective-permute-start | bytes 98312 | tf_op jit(solution)/shard_map/ppermute | solution.py:34
  131.0 3.3 %collective-permute-done.32 = bf16[64,256]{1,0:T(8,128)(2,1)S(1)} collective-permute-done((bf16[64,256]{1,0:T(8,128)(2,1)S(1)}, bf16[64,256]{1,0:T(8,128)(2,1)S(1)}, u32[]{:S(2)}, u32[]{:S(2)}) %collective-permute-start.32) | collective-permute-done | bytes 32800 | tf_op jit(solution)/shard_map/ppermute | solution.py:34
  (95 shorter events, 48.0 us)
Async XLA Ops:
  7.1 37.1 %collective-permute-start.13 = (bf16[16,256,256]{2,1,0:T(8,128)(2,1)S(1)}, bf16[16,256,256]{2,1,0:T(8,128)(2,1)}, u32[]{:S(2)}, u32[]{:S(2)}) collective-permute-start(bf16[16,256,256]{2,1,0:T(8,128)(2,1)S(1)} %reshape.125.refs_2_.refs_4_.wo), channel_id=1, source_target_pairs={{0,1},{1,0},{2,3},{3,2},{4,5},{5,4},{6,7},{7,6},{8,9},{9,8},{10,11... | collective-permute-start | bytes 6291464 | tf_op jit(solution)/shard_map/ppermute | solution.py:34
  7.2 10.2 %collective-permute-start.2 = (bf16[2,64,256]{2,1,0:T(8,128)(2,1)S(1)}, bf16[2,64,256]{2,1,0:T(8,128)(2,1)S(1)}, u32[]{:S(2)}, u32[]{:S(2)}) collective-permute-start(bf16[2,64,256]{2,1,0:T(8,128)(2,1)S(1)} %maximum_select_fusion.1), channel_id=1, source_target_pairs={{0,2},{1,7},{2,4},{3,1},{4,6},{5,3},{6,0},{7,5},{8,10},{9,15},{10,... | collective-permute-start | bytes 196616 | tf_op jit(solution)/shard_map/ppermute | solution.py:51
  12.9 8.5 %collective-permute-start.4 = (bf16[64,256]{1,0:T(8,128)(2,1)S(1)}, bf16[64,256]{1,0:T(8,128)(2,1)S(1)}, u32[]{:S(2)}, u32[]{:S(2)}) collective-permute-start(bf16[64,256]{1,0:T(8,128)(2,1)S(1)} %slice_select_fusion.1), channel_id=1, source_target_pairs={{0,4},{1,5},{2,6},{3,7},{4,0},{5,1},{6,2},{7,3},{8,12},{9,13},{10,... | collective-permute-start | bytes 98312 | tf_op jit(solution)/shard_map/ppermute | solution.py:34
  21.5 7.1 %collective-permute-start.9 = (bf16[8,64,256]{2,1,0:T(8,128)(2,1)S(1)}, bf16[8,64,256]{2,1,0:T(8,128)(2,1)S(1)}, u32[]{:S(2)}, u32[]{:S(2)}) collective-permute-start(bf16[8,64,256]{2,1,0:T(8,128)(2,1)S(1)} %get-tuple-element.56), channel_id=1, source_target_pairs={{0,16},{1,129},{2,18},{3,131},{4,20},{5,133},{6,22},{7,135},{8,24}... | collective-permute-start | bytes 786440 | tf_op jit(solution)/shard_map/ppermute | solution.py:43
  24.3 7.2 %collective-permute-start.10 = (bf16[8,64,256]{2,1,0:T(8,128)(2,1)S(1)}, bf16[8,64,256]{2,1,0:T(8,128)(2,1)S(1)}, u32[]{:S(2)}, u32[]{:S(2)}) collective-permute-start(bf16[8,64,256]{2,1,0:T(8,128)(2,1)S(1)} %get-tuple-element.56), channel_id=1, source_target_pairs={{0,24},{1,193},{2,26},{3,195},{4,28},{5,197},{6,30},{7,199},{8,0},... | collective-permute-start | bytes 786440 | tf_op jit(solution)/shard_map/ppermute | solution.py:43
  25.1 9.2 %collective-permute-start.6 = (bf16[8,64,256]{2,1,0:T(8,128)(2,1)S(1)}, bf16[8,64,256]{2,1,0:T(8,128)(2,1)S(1)}, u32[]{:S(2)}, u32[]{:S(2)}) collective-permute-start(bf16[8,64,256]{2,1,0:T(8,128)(2,1)S(1)} %get-tuple-element.56), channel_id=1, source_target_pairs={{0,8},{1,65},{2,10},{3,67},{4,12},{5,69},{6,14},{7,71},{8,16},{9,7... | collective-permute-start | bytes 786440 | tf_op jit(solution)/shard_map/ppermute | solution.py:43
  31.5 8.9 %collective-permute-start.11 = (bf16[2,8,64,256]{3,2,1,0:T(8,128)(2,1)S(1)}, bf16[2,8,64,256]{3,2,1,0:T(8,128)(2,1)}, u32[]{:S(2)}, u32[]{:S(2)}) collective-permute-start(bf16[2,8,64,256]{3,2,1,0:T(8,128)(2,1)S(1)} %pad_maximum_fusion.1.refs_1_), channel_id=1, source_target_pairs={{0,192},{1,25},{2,194},{3,27},{4,196},{5,29},{6,198},{7,31},{8,200... | collective-permute-start | bytes 1572872 | tf_op jit(solution)/shard_map/ppermute | solution.py:43
  34.4 9.7 %collective-permute-start.7 = (bf16[2,8,64,256]{3,2,1,0:T(8,128)(2,1)S(1)}, bf16[2,8,64,256]{3,2,1,0:T(8,128)(2,1)}, u32[]{:S(2)}, u32[]{:S(2)}) collective-permute-start(bf16[2,8,64,256]{3,2,1,0:T(8,128)(2,1)S(1)} %pad_maximum_fusion.refs_0_), channel_id=1, source_target_pairs={{0,64},{1,9},{2,66},{3,11},{4,68},{5,13},{6,70},{7,15},{8,72},{9,1... | collective-permute-start | bytes 1572872 | tf_op jit(solution)/shard_map/ppermute | solution.py:43
  34.5 15.2 %collective-permute-start.14 = (bf16[2,8,64,256]{3,2,1,0:T(8,128)(2,1)S(1)}, bf16[2,8,64,256]{3,2,1,0:T(8,128)(2,1)}, u32[]{:S(2)}, u32[]{:S(2)}) collective-permute-start(bf16[2,8,64,256]{3,2,1,0:T(8,128)(2,1)S(1)} %pad_maximum_fusion.1.refs_1_), channel_id=1, source_target_pairs={{0,64},{1,9},{2,66},{3,11},{4,68},{5,13},{6,70},{7,15},{8,72},{9,1... | collective-permute-start | bytes 1572872 | tf_op jit(solution)/shard_map/ppermute | solution.py:43
  34.6 15.2 %collective-permute-start.15 = (bf16[2,8,64,256]{3,2,1,0:T(8,128)(2,1)S(1)}, bf16[2,8,64,256]{3,2,1,0:T(8,128)(2,1)}, u32[]{:S(2)}, u32[]{:S(2)}) collective-permute-start(bf16[2,8,64,256]{3,2,1,0:T(8,128)(2,1)S(1)} %pad_maximum_fusion.refs_0_), channel_id=1, source_target_pairs={{0,192},{1,25},{2,194},{3,27},{4,196},{5,29},{6,198},{7,31},{8,200... | collective-permute-start | bytes 1572872 | tf_op jit(solution)/shard_map/ppermute | solution.py:43
  40.5 12.1 %collective-permute-start.12 = (bf16[2,8,64,256]{3,2,1,0:T(8,128)(2,1)}, bf16[2,8,64,256]{3,2,1,0:T(8,128)(2,1)}, u32[]{:S(2)}, u32[]{:S(2)}) collective-permute-start(bf16[2,8,64,256]{3,2,1,0:T(8,128)(2,1)} %collective-permute-done.11.refs_3_.refs_7_), channel_id=1, source_target_pairs={{0,192},{1,25},{2,194},{3,27},{4,196},{5,29},{6,198},{7,31},{8,200... | collective-permute-start | bytes 1572872 | tf_op jit(solution)/shard_map/ppermute | solution.py:43
  44.1 11.2 %collective-permute-start.8 = (bf16[2,8,64,256]{3,2,1,0:T(8,128)(2,1)}, bf16[2,8,64,256]{3,2,1,0:T(8,128)(2,1)}, u32[]{:S(2)}, u32[]{:S(2)}) collective-permute-start(bf16[2,8,64,256]{3,2,1,0:T(8,128)(2,1)} %collective-permute-done.7.refs_0_.refs_2_), channel_id=1, source_target_pairs={{0,64},{1,9},{2,66},{3,11},{4,68},{5,13},{6,70},{7,15},{8,72},{9,1... | collective-permute-start | bytes 1572872 | tf_op jit(solution)/shard_map/ppermute | solution.py:43
  82.8 27.2 %collective-permute-start.21 = (bf16[16,256,256]{2,1,0:T(8,128)(2,1)S(1)}, bf16[16,256,256]{2,1,0:T(8,128)(2,1)S(1)}, u32[]{:S(2)}, u32[]{:S(2)}) collective-permute-start(bf16[16,256,256]{2,1,0:T(8,128)(2,1)S(1)} %get-tuple-element.37), channel_id=1, source_target_pairs={{0,1},{1,0},{2,3},{3,2},{4,5},{5,4},{6,7},{7,6},{8,9},{9,8},{10,11... | collective-permute-start | bytes 6291464 | tf_op jit(solution)/shard_map/ppermute | solution.py:34
  86.4 8.3 %collective-permute-start.24 = (bf16[2,8,64,256]{3,2,1,0:T(8,128)(2,1)S(1)}, bf16[2,8,64,256]{3,2,1,0:T(8,128)(2,1)S(1)}, u32[]{:S(2)}, u32[]{:S(2)}) collective-permute-start(bf16[2,8,64,256]{3,2,1,0:T(8,128)(2,1)S(1)} %get-tuple-element.43), channel_id=1, source_target_pairs={{0,192},{1,25},{2,194},{3,27},{4,196},{5,29},{6,198},{7,31},{8,200... | collective-permute-start | bytes 1572872 | tf_op jit(solution)/shard_map/ppermute | solution.py:43
  88.5 9.8 %collective-permute-start.18 = (bf16[2,8,64,256]{3,2,1,0:T(8,128)(2,1)S(1)}, bf16[2,8,64,256]{3,2,1,0:T(8,128)(2,1)S(1)}, u32[]{:S(2)}, u32[]{:S(2)}) collective-permute-start(bf16[2,8,64,256]{3,2,1,0:T(8,128)(2,1)S(1)} %get-tuple-element.32.refs_0_), channel_id=1, source_target_pairs={{0,64},{1,9},{2,66},{3,11},{4,68},{5,13},{6,70},{7,15},{8,72},{9,1... | collective-permute-start | bytes 1572872 | tf_op jit(solution)/shard_map/ppermute | solution.py:43
  88.6 15.2 %collective-permute-start.23 = (bf16[2,8,64,256]{3,2,1,0:T(8,128)(2,1)S(1)}, bf16[2,8,64,256]{3,2,1,0:T(8,128)(2,1)S(1)}, u32[]{:S(2)}, u32[]{:S(2)}) collective-permute-start(bf16[2,8,64,256]{3,2,1,0:T(8,128)(2,1)S(1)} %get-tuple-element.41), channel_id=1, source_target_pairs={{0,64},{1,9},{2,66},{3,11},{4,68},{5,13},{6,70},{7,15},{8,72},{9,1... | collective-permute-start | bytes 1572872 | tf_op jit(solution)/shard_map/ppermute | solution.py:43
  88.6 18.6 %collective-permute-start.20 = (bf16[2,8,64,256]{3,2,1,0:T(8,128)(2,1)S(1)}, bf16[2,8,64,256]{3,2,1,0:T(8,128)(2,1)S(1)}, u32[]{:S(2)}, u32[]{:S(2)}) collective-permute-start(bf16[2,8,64,256]{3,2,1,0:T(8,128)(2,1)S(1)} %get-tuple-element.35), channel_id=1, source_target_pairs={{0,192},{1,25},{2,194},{3,27},{4,196},{5,29},{6,198},{7,31},{8,200... | collective-permute-start | bytes 1572872 | tf_op jit(solution)/shard_map/ppermute | solution.py:43
  94.9 11.1 %collective-permute-start.25 = (bf16[2,8,64,256]{3,2,1,0:T(8,128)(2,1)S(1)}, bf16[2,8,64,256]{3,2,1,0:T(8,128)(2,1)S(1)}, u32[]{:S(2)}, u32[]{:S(2)}) collective-permute-start(bf16[2,8,64,256]{3,2,1,0:T(8,128)(2,1)S(1)} %add_convert_fusion.1), channel_id=1, source_target_pairs={{0,192},{1,25},{2,194},{3,27},{4,196},{5,29},{6,198},{7,31},{8,200... | collective-permute-start | bytes 1572872 | tf_op jit(solution)/shard_map/ppermute | solution.py:43
  98.5 10.5 %collective-permute-start.19 = (bf16[2,8,64,256]{3,2,1,0:T(8,128)(2,1)S(1)}, bf16[2,8,64,256]{3,2,1,0:T(8,128)(2,1)S(1)}, u32[]{:S(2)}, u32[]{:S(2)}) collective-permute-start(bf16[2,8,64,256]{3,2,1,0:T(8,128)(2,1)S(1)} %add_convert_fusion.2), channel_id=1, source_target_pairs={{0,64},{1,9},{2,66},{3,11},{4,68},{5,13},{6,70},{7,15},{8,72},{9,1... | collective-permute-start | bytes 1572872 | tf_op jit(solution)/shard_map/ppermute | solution.py:43
  106.9 6.7 %collective-permute-start.27 = (bf16[8,64,256]{2,1,0:T(8,128)(2,1)S(1)}, bf16[8,64,256]{2,1,0:T(8,128)(2,1)S(1)}, u32[]{:S(2)}, u32[]{:S(2)}) collective-permute-start(bf16[8,64,256]{2,1,0:T(8,128)(2,1)S(1)} %get-tuple-element.47), channel_id=1, source_target_pairs={{0,16},{1,129},{2,18},{3,131},{4,20},{5,133},{6,22},{7,135},{8,24}... | collective-permute-start | bytes 786440 | tf_op jit(solution)/shard_map/ppermute | solution.py:43
  110.0 6.9 %collective-permute-start.22 = (bf16[8,64,256]{2,1,0:T(8,128)(2,1)}, bf16[8,64,256]{2,1,0:T(8,128)(2,1)S(1)}, u32[]{:S(2)}, u32[]{:S(2)}) collective-permute-start(bf16[8,64,256]{2,1,0:T(8,128)(2,1)} %get-tuple-element.44), channel_id=1, source_target_pairs={{0,8},{1,65},{2,10},{3,67},{4,12},{5,69},{6,14},{7,71},{8,16},{9,7... | collective-permute-start | bytes 786440 | tf_op jit(solution)/shard_map/ppermute | solution.py:43
  122.2 8.3 %collective-permute-start.29 = (bf16[2,64,256]{2,1,0:T(8,128)(2,1)S(1)}, bf16[2,64,256]{2,1,0:T(8,128)(2,1)S(1)}, u32[]{:S(2)}, u32[]{:S(2)}) collective-permute-start(bf16[2,64,256]{2,1,0:T(8,128)(2,1)S(1)} %pad_maximum_fusion.5), channel_id=1, source_target_pairs={{0,34},{1,37},{2,36},{3,39},{4,38},{5,33},{6,32},{7,35},{8,42},{9,... | collective-permute-start | bytes 196616 | tf_op jit(solution)/shard_map/ppermute | solution.py:51
  123.0 7.5 %collective-permute-start.30 = (bf16[2,64,256]{2,1,0:T(8,128)(2,1)S(1)}, bf16[2,64,256]{2,1,0:T(8,128)(2,1)S(1)}, u32[]{:S(2)}, u32[]{:S(2)}) collective-permute-start(bf16[2,64,256]{2,1,0:T(8,128)(2,1)S(1)} %pad_maximum_fusion.6), channel_id=1, source_target_pairs={{0,2},{1,7},{2,4},{3,1},{4,6},{5,3},{6,0},{7,5},{8,10},{9,15},{10,... | collective-permute-start | bytes 196616 | tf_op jit(solution)/shard_map/ppermute | solution.py:51
  127.7 6.7 %collective-permute-start.32 = (bf16[64,256]{1,0:T(8,128)(2,1)S(1)}, bf16[64,256]{1,0:T(8,128)(2,1)S(1)}, u32[]{:S(2)}, u32[]{:S(2)}) collective-permute-start(bf16[64,256]{1,0:T(8,128)(2,1)S(1)} %get-tuple-element.48), channel_id=1, source_target_pairs={{0,4},{1,5},{2,6},{3,7},{4,0},{5,1},{6,2},{7,3},{8,12},{9,13},{10,... | collective-permute-start | bytes 98312 | tf_op jit(solution)/shard_map/ppermute | solution.py:34
  (14 other events, 87.3 us)

commit v4 on v3

--- a/solution.py
+++ b/solution.py
@@ -216,8 +216,9 @@
             emit(dy, lambda dx: outs[2 * i + dx // 2].at[dx % 2])
 
 
-def weight_kernel(pos, *refs):
-    pieces, (g_own, g_par, _, own_ref, par_ref) = refs[:8], refs[8:]
+def weight_kernel(half, pos, *refs):
+    pieces, (g_own, g_par) = refs[:8], refs[8:10]
+    own_ref, par_ref = refs[-2:]
     x, y, z, c = pos[0], pos[1], pos[2], pos[3]
     order = [((x + 4 - dx) & 3) * 2 + zl for dx in range(4) for zl in range(2)]
     own = jnp.concatenate([g_own[m] for m in order], axis=0)
@@ -233,18 +234,16 @@
 
     @pl.when(c == 0)
     def _():
-        for half in range(2):
-
-            def step(i, _):
-                inner = i // 4
-                emit(2 * half + inner, i & 3, lambda dx: pieces[2 * dx + half].at[inner])
-                return 0
-
-            lax.fori_loop(0, 8, step, 0)
+        def step(i, _):
+            inner = i // 4
+            emit(2 * half + inner, i & 3, lambda dx: pieces[2 * dx + half].at[inner])
+            return 0
+
+        lax.fori_loop(0, 8, step, 0)
 
     @pl.when(c == 1)
     def _():
-        for dy in range(4):
+        for dy in (2 * half, 2 * half + 1):
 
             def step(zh, _):
                 emit(dy, zh, lambda dx: pieces[2 * dy + dx // 2].at[dx % 2])
@@ -258,13 +257,14 @@
 HBM = pl.BlockSpec(memory_space=pl.ANY)
 
 
-def whole(kernel, ins, outs, out_specs, scratch):
+def whole(kernel, ins, outs, out_specs, scratch, aliases=None):
     return pl.pallas_call(
         kernel,
         in_specs=[SMEM] + ins,
         out_specs=out_specs,
         out_shape=[jax.ShapeDtypeStruct(s, d) for s, d in outs],
         scratch_shapes=scratch,
+        input_output_aliases=aliases or {},
         compiler_params=pltpu.CompilerParams(vmem_limit_bytes=20 * 2**20),
     )
 
@@ -379,9 +379,20 @@
     from_left_low = cross(total([right_low_g, pass_low]), 1, 0)
     from_right_high = cross(total([left_high_g, pass_high]), 3, 0)
 
-    grad_own, grad_par = whole(
-        weight_kernel, [VMEM] * 10 + [HBM], [((16, 256, 256), BF)] * 2, [VMEM] * 2, []
-    )(pos, low, high, right_low, right_high, far_low, far_high, left_low, left_high, grad_keep, grad_recv, own_low)
+    states_in = (low, high, right_low, right_high, far_low, far_high, left_low, left_high)
+
+    def weight(half, done):
+        return whole(
+            functools.partial(weight_kernel, half),
+            [VMEM] * (10 + len(done)),
+            [((16, 256, 256), BF)] * 2,
+            [VMEM] * 2,
+            [],
+            {11: 0, 12: 1} if done else None,
+        )(pos, *states_in, grad_keep, grad_recv, *done)
+
+    grad_parts = weight(0, ())
+    grad_own, grad_par = weight(1, grad_parts)
     grad_other = shift(grad_par, dc=1)
     weight_grad = total([grad_own, grad_other]).reshape(1, 4096, 2, 128)
 
@@ -390,7 +401,6 @@
     got = [low[0]]
     for k in (1, 3, 2):
         got.append(cross((low + high)[k], k, 1))
-    got[0], weight_grad = lax.optimization_barrier((got[0], weight_grad))
     passed = [total([p[8 - k] for p in got]) for k in (3, 2, 1)]
     passed = shift(jnp.stack(passed), dc=1)
     across = shift(total([p[4] for p in got]), dz=4)
@@ -398,6 +408,7 @@
     for i, k in enumerate((3, 2, 1)):
         both = jnp.stack([total([p[k] for p in got]), passed[i]])
         got_z.append(rise(both, k).astype(F32))
+    got_z[0], weight_grad = lax.optimization_barrier((got_z[0], weight_grad))
     both = got_z[0] + got_z[1] + got_z[2]
     mine = functools.reduce(lambda p, q: p + q, [p[0].astype(F32) for p in got])
     both = jnp.stack([both[0] + mine + across.astype(F32), both[1]]).reshape(2, 64, 2, 128)

time: 138 us -> 132 us (0.957)
  the two profiles are of different devices: /device:TPU:1 before, /device:TPU:8 now
where the time goes in v4:
time: 132 us; the launch traced here: 130 us
  starting transfers between devices  47.9 us (36%)
  waiting for transfers between devices  39.3 us (30%)
  Pallas kernels  32.3 us (24%)
  local copies, waits for them, and re-layouts  5.27 us (4%)
  other arithmetic  3.98 us (3%)
    ppermute x18, starting transfers between devices, cross(): return lax.ppermute(value, AXES, pairs)  27.9 us
    ppermute x18, waiting for transfers between devices, cross(): return lax.ppermute(value, AXES, pairs)  24 us
    ppermute x6, starting transfers between devices, rise(): return lax.ppermute(value, AXES, pairs)  15.7 us
    pallas_call x2, Pallas kernels, weight(): whole(functools.partial(weight_kernel, half), [VMEM] * (10 + len(done)),...  9.84 us
    pallas_call x3, Pallas kernels, project(): whole(functools.partial(project_kernel, which, first, last), [VMEM] * (2...  9.18 us
    ppermute x10, waiting for transfers between devices, shift(): return lax.ppermute(value, AXES, pairs)  7.79 us
    ppermute x6, waiting for transfers between devices, rise(): return lax.ppermute(value, AXES, pairs)  7.55 us
    pallas_call x3, Pallas kernels, spread(): whole(functools.partial(spread_kernel, which, len(after)), [VMEM] * 4 + [...  7.42 us
  transfers between devices with their start and end apart: 34, of which 16 were waited for; matrix products, arithmetic and copies ran while one was open for 6% of the time, Pallas kernels for 16%

profile of v4, /device:TPU:8, one launch (start us, length us, event | category | flops | bytes accessed | tf_op | source)
XLA Modules:
  0.0 129.8 jit_solution(16159849928618912043)
XLA Ops:
  0.7 3.2 %reshape.133.refs_2_.refs_4_.wo = bf16[16,256,256]{2,1,0:T(8,128)(2,1)S(1)} reshape(bf16[1,4096,2,128]{3,2,1,0:T(2,128)(2,1)} %param.7) | data formatting | bytes 4194304 | tf_op jit(solution)/shard_map/reshape | solution.py:345
  4.5 3.3 %collective-permute-start.2 = (bf16[2,64,256]{2,1,0:T(8,128)(2,1)S(1)}, bf16[2,64,256]{2,1,0:T(8,128)(2,1)S(1)}, u32[]{:S(2)}, u32[]{:S(2)}) collective-permute-start(bf16[2,64,256]{2,1,0:T(8,128)(2,1)S(1)} %maximum_select_fusion.1), channel_id=1, source_target_pairs={{0,2},{1,7},{2,4},{3,1},{4,6},{5,3},{6,0},{7,5},{8,10},{9,15},{10,... | collective-permute-start | bytes 196616 | tf_op jit(solution)/shard_map/ppermute | solution.py:51
  9.8 4.0 %collective-permute-start.1 = (bf16[2,64,256]{2,1,0:T(8,128)(2,1)S(1)}, bf16[2,64,256]{2,1,0:T(8,128)(2,1)S(1)}, u32[]{:S(2)}, u32[]{:S(2)}) collective-permute-start(bf16[2,64,256]{2,1,0:T(8,128)(2,1)S(1)} %maximum_select_fusion.1), channel_id=1, source_target_pairs={{0,34},{1,37},{2,36},{3,39},{4,38},{5,33},{6,32},{7,35},{8,42},{9,... | collective-permute-start | bytes 196616 | tf_op jit(solution)/shard_map/ppermute | solution.py:51
  14.5 3.4 %collective-permute-done.1 = bf16[2,64,256]{2,1,0:T(8,128)(2,1)S(1)} collective-permute-done((bf16[2,64,256]{2,1,0:T(8,128)(2,1)S(1)}, bf16[2,64,256]{2,1,0:T(8,128)(2,1)S(1)}, u32[]{:S(2)}, u32[]{:S(2)}) %collective-permute-start.1) | collective-permute-done | bytes 65568 | tf_op jit(solution)/shard_map/ppermute | solution.py:51
  18.1 3.7 %collective-permute-done.4 = bf16[64,256]{1,0:T(8,128)(2,1)S(1)} collective-permute-done((bf16[64,256]{1,0:T(8,128)(2,1)S(1)}, bf16[64,256]{1,0:T(8,128)(2,1)S(1)}, u32[]{:S(2)}, u32[]{:S(2)}) %collective-permute-start.4) | collective-permute-done | bytes 32800 | tf_op jit(solution)/shard_map/ppermute | solution.py:34
  26.2 3.7 %collective-permute-done.9 = bf16[8,64,256]{2,1,0:T(8,128)(2,1)S(1)} collective-permute-done((bf16[8,64,256]{2,1,0:T(8,128)(2,1)S(1)}, bf16[8,64,256]{2,1,0:T(8,128)(2,1)S(1)}, u32[]{:S(2)}, u32[]{:S(2)}) %collective-permute-start.9) | collective-permute-done | bytes 262176 | tf_op jit(solution)/shard_map/ppermute | solution.py:43
  29.9 2.7 %collective-permute-done.10 = bf16[8,64,256]{2,1,0:T(8,128)(2,1)S(1)} collective-permute-done((bf16[8,64,256]{2,1,0:T(8,128)(2,1)S(1)}, bf16[8,64,256]{2,1,0:T(8,128)(2,1)S(1)}, u32[]{:S(2)}, u32[]{:S(2)}) %collective-permute-start.10) | collective-permute-done | bytes 262176 | tf_op jit(solution)/shard_map/ppermute | solution.py:43
  32.6 2.8 %collective-permute-start.11 = (bf16[2,8,64,256]{3,2,1,0:T(8,128)(2,1)S(1)}, bf16[2,8,64,256]{3,2,1,0:T(8,128)(2,1)}, u32[]{:S(2)}, u32[]{:S(2)}) collective-permute-start(bf16[2,8,64,256]{3,2,1,0:T(8,128)(2,1)S(1)} %pad_maximum_fusion.1.refs_1_), channel_id=1, source_target_pairs={{0,192},{1,25},{2,194},{3,27},{4,196},{5,29},{6,198},{7,31},{8,200... | collective-permute-start | bytes 1572872 | tf_op jit(solution)/shard_map/ppermute | solution.py:43
  36.4 2.6 %collective-permute-start.15 = (bf16[2,8,64,256]{3,2,1,0:T(8,128)(2,1)S(1)}, bf16[2,8,64,256]{3,2,1,0:T(8,128)(2,1)}, u32[]{:S(2)}, u32[]{:S(2)}) collective-permute-start(bf16[2,8,64,256]{3,2,1,0:T(8,128)(2,1)S(1)} %pad_maximum_fusion.refs_0_), channel_id=1, source_target_pairs={{0,192},{1,25},{2,194},{3,27},{4,196},{5,29},{6,198},{7,31},{8,200... | collective-permute-start | bytes 1572872 | tf_op jit(solution)/shard_map/ppermute | solution.py:43
  38.9 3.2 %collective-permute-done.11.refs_3_.refs_7_ = bf16[2,8,64,256]{3,2,1,0:T(8,128)(2,1)} collective-permute-done((bf16[2,8,64,256]{3,2,1,0:T(8,128)(2,1)S(1)}, bf16[2,8,64,256]{3,2,1,0:T(8,128)(2,1)}, u32[]{:S(2)}, u32[]{:S(2)}) %collective-permute-start.11) | collective-permute-done | bytes 524320 | tf_op jit(solution)/shard_map/ppermute | solution.py:43
  42.2 3.8 %collective-permute-start.12 = (bf16[2,8,64,256]{3,2,1,0:T(8,128)(2,1)}, bf16[2,8,64,256]{3,2,1,0:T(8,128)(2,1)}, u32[]{:S(2)}, u32[]{:S(2)}) collective-permute-start(bf16[2,8,64,256]{3,2,1,0:T(8,128)(2,1)} %collective-permute-done.11.refs_3_.refs_7_), channel_id=1, source_target_pairs={{0,192},{1,25},{2,194},{3,27},{4,196},{5,29},{6,198},{7,31},{8,200... | collective-permute-start | bytes 1572872 | tf_op jit(solution)/shard_map/ppermute | solution.py:43
  46.2 3.2 %shard_map.84 = (bf16[16,256,256]{2,1,0:T(8,128)(2,1)S(1)}, f32[512,512]{1,0:T(8,128)S(1)}) custom-call(s32[4]{0:T(128)S(1)} %pad_add_fusion.pos, bf16[2,8,64,256]{3,2,1,0:T(8,128)(2,1)S(1)} %pad_maximum_fusion.refs_0_, bf16[2,8,64,256]{3,2,1,0:T(8,128)(2,1)S(1)} %pad_maximum_fusion.1.refs_1_, bf16[16,256,256]{2,1,0:T(8,128)(2,1)S(1)} %reshape.133.refs_2_.refs_4_.wo, ...), custom_call_target="tpu_custom_call" | custom-call | tf_op jit(solution)/shard_map/pallas_call | solution.py:279
  51.7 3.4 %shard_map.85.refs_4_ = f32[512,512]{1,0:T(8,128)S(1)} custom-call(s32[4]{0:T(128)S(1)} %pad_add_fusion.pos, bf16[2,8,64,256]{3,2,1,0:T(8,128)(2,1)} %collective-permute-done.7.refs_0_.refs_2_, bf16[2,8,64,256]{3,2,1,0:T(8,128)(2,1)} %collective-permute-done.14.refs_1_.refs_3_, bf16[2,8,64,256]{3,2,1,0:T(8,128)(2,1)} %collective-permute-done.15.refs_2_.refs_6_, ...), custom_call_target="tpu_custom_call" | custom-call | tf_op jit(solution)/shard_map/pallas_call | solution.py:279
  57.3 2.6 %shard_map.86 = (bf16[8,64,256]{2,1,0:T(8,128)(2,1)S(1)}, bf16[8,64,256]{2,1,0:T(8,128)(2,1)S(1)}) custom-call(s32[4]{0:T(128)S(1)} %pad_add_fusion.pos, bf16[2,8,64,256]{3,2,1,0:T(8,128)(2,1)} %collective-permute-done.8.refs_0_.refs_4_, bf16[2,8,64,256]{3,2,1,0:T(8,128)(2,1)} %collective-permute-done.12.refs_1_.refs_5_, ...), custom_call_target="tpu_custom_call" | custom-call | tf_op jit(solution)/shard_map/pallas_call | solution.py:279
  61.6 5.9 %attend.1 = (bf16[1,8,512,128]{3,2,1,0:T(8,128)(2,1)}, bf16[1,8,512,128]{3,2,1,0:T(8,128)(2,1)}, bf16[8,64,256]{2,1,0:T(8,128)(2,1)S(1)}, bf16[8,64,256]{2,1,0:T(8,128)(2,1)S(1)}) custom-call(s32[4]{0:T(128)S(1)} %pad_add_fusion.pos, s32[8]{0:T(128)S(1)} %copy-done.2, bf16[1,8,512,128]{3,2,1,0:T(8,128)(2,1)S(1)} %copy-done, ...), custom_call_target="tpu_custom_call" | custom-call | tf_op jit(solution)/shard_map/attend/pallas_call | solution.py:301
  71.5 3.2 %collective-permute-start.23 = (bf16[2,8,64,256]{3,2,1,0:T(8,128)(2,1)S(1)}, bf16[2,8,64,256]{3,2,1,0:T(8,128)(2,1)S(1)}, u32[]{:S(2)}, u32[]{:S(2)}) collective-permute-start(bf16[2,8,64,256]{3,2,1,0:T(8,128)(2,1)S(1)} %get-tuple-element.41), channel_id=1, source_target_pairs={{0,192},{1,25},{2,194},{3,27},{4,196},{5,29},{6,198},{7,31},{8,200... | collective-permute-start | bytes 1572872 | tf_op jit(solution)/shard_map/ppermute | solution.py:43
  74.8 2.5 %shard_map.88 = (bf16[2,8,64,256]{3,2,1,0:T(8,128)(2,1)S(1)}, bf16[2,8,64,256]{3,2,1,0:T(8,128)(2,1)S(1)}, bf16[2,8,64,256]{3,2,1,0:T(8,128)(2,1)S(1)}, bf16[2,8,64,256]{3,2,1,0:T(8,128)(2,1)S(1)}) custom-call(s32[4]{0:T(128)S(1)} %pad_add_fusion.pos, bf16[8,64,256]{2,1,0:T(8,128)(2,1)S(1)} %get-tuple-element.32.g_own.refs_8_, ...), custom_call_target="tpu_custom_call" | custom-call | tf_op jit(solution)/shard_map/pallas_call | solution.py:289
  79.3 2.6 %collective-permute-done.18 = bf16[2,8,64,256]{3,2,1,0:T(8,128)(2,1)S(1)} collective-permute-done((bf16[2,8,64,256]{3,2,1,0:T(8,128)(2,1)S(1)}, bf16[2,8,64,256]{3,2,1,0:T(8,128)(2,1)S(1)}, u32[]{:S(2)}, u32[]{:S(2)}) %collective-permute-start.18) | collective-permute-done | bytes 524320 | tf_op jit(solution)/shard_map/ppermute | solution.py:43
  82.5 3.3 %collective-permute-start.24 = (bf16[2,8,64,256]{3,2,1,0:T(8,128)(2,1)S(1)}, bf16[2,8,64,256]{3,2,1,0:T(8,128)(2,1)S(1)}, u32[]{:S(2)}, u32[]{:S(2)}) collective-permute-start(bf16[2,8,64,256]{3,2,1,0:T(8,128)(2,1)S(1)} %add_convert_fusion.1), channel_id=1, source_target_pairs={{0,192},{1,25},{2,194},{3,27},{4,196},{5,29},{6,198},{7,31},{8,200... | collective-permute-start | bytes 1572872 | tf_op jit(solution)/shard_map/ppermute | solution.py:43
  85.8 4.9 %shard_map.90 = (bf16[16,256,256]{2,1,0:T(8,128)(2,1)S(1)}, bf16[16,256,256]{2,1,0:T(8,128)(2,1)S(1)}) custom-call(s32[4]{0:T(128)S(1)} %pad_add_fusion.pos, bf16[2,8,64,256]{3,2,1,0:T(8,128)(2,1)S(1)} %pad_maximum_fusion.refs_0_, bf16[2,8,64,256]{3,2,1,0:T(8,128)(2,1)S(1)} %pad_maximum_fusion.1.refs_1_, ...), custom_call_target="tpu_custom_call" | custom-call | tf_op jit(solution)/shard_map/pallas_call | solution.py:385
  90.8 4.9 %shard_map.91 = (bf16[16,256,256]{2,1,0:T(8,128)(2,1)S(1)}, bf16[16,256,256]{2,1,0:T(8,128)(2,1)S(1)}) custom-call(s32[4]{0:T(128)S(1)} %pad_add_fusion.pos, bf16[2,8,64,256]{3,2,1,0:T(8,128)(2,1)S(1)} %pad_maximum_fusion.refs_0_, bf16[2,8,64,256]{3,2,1,0:T(8,128)(2,1)S(1)} %pad_maximum_fusion.1.refs_1_, ...), custom_call_target="tpu_custom_call", output_to_operand_aliasing={{0}: (11, {}), {1}: (12, {})} | custom-call | tf_op jit(solution)/shard_map/pallas_call | solution.py:385
  106.2 4.3 %collective-permute-done.26 = bf16[8,64,256]{2,1,0:T(8,128)(2,1)S(1)} collective-permute-done((bf16[8,64,256]{2,1,0:T(8,128)(2,1)S(1)}, bf16[8,64,256]{2,1,0:T(8,128)(2,1)S(1)}, u32[]{:S(2)}, u32[]{:S(2)}) %collective-permute-start.26) | collective-permute-done | bytes 262176 | tf_op jit(solution)/shard_map/ppermute | solution.py:43
  113.7 2.9 %collective-permute-start.30 = (bf16[2,64,256]{2,1,0:T(8,128)(2,1)S(1)}, bf16[2,64,256]{2,1,0:T(8,128)(2,1)S(1)}, u32[]{:S(2)}, u32[]{:S(2)}) collective-permute-start(bf16[2,64,256]{2,1,0:T(8,128)(2,1)S(1)} %pad_maximum_fusion.6), channel_id=1, source_target_pairs={{0,2},{1,7},{2,4},{3,1},{4,6},{5,3},{6,0},{7,5},{8,10},{9,15},{10,... | collective-permute-start | bytes 196616 | tf_op jit(solution)/shard_map/ppermute | solution.py:51
  120.1 4.1 %collective-permute-done.28 = bf16[2,64,256]{2,1,0:T(8,128)(2,1)S(1)} collective-permute-done((bf16[2,64,256]{2,1,0:T(8,128)(2,1)S(1)}, bf16[2,64,256]{2,1,0:T(8,128)(2,1)S(1)}, u32[]{:S(2)}, u32[]{:S(2)}) %collective-permute-start.28) | collective-permute-done | bytes 65568 | tf_op jit(solution)/shard_map/ppermute | solution.py:51
  (97 shorter events, 44.6 us)
Async XLA Ops:
  3.9 42.3 %collective-permute-start.13 = (bf16[16,256,256]{2,1,0:T(8,128)(2,1)S(1)}, bf16[16,256,256]{2,1,0:T(8,128)(2,1)}, u32[]{:S(2)}, u32[]{:S(2)}) collective-permute-start(bf16[16,256,256]{2,1,0:T(8,128)(2,1)S(1)} %reshape.133.refs_2_.refs_4_.wo), channel_id=1, source_target_pairs={{0,1},{1,0},{2,3},{3,2},{4,5},{5,4},{6,7},{7,6},{8,9},{9,8},{10,11... | collective-permute-start | bytes 6291464 | tf_op jit(solution)/shard_map/ppermute | solution.py:34
  4.5 10.0 %collective-permute-start.2 = (bf16[2,64,256]{2,1,0:T(8,128)(2,1)S(1)}, bf16[2,64,256]{2,1,0:T(8,128)(2,1)S(1)}, u32[]{:S(2)}, u32[]{:S(2)}) collective-permute-start(bf16[2,64,256]{2,1,0:T(8,128)(2,1)S(1)} %maximum_select_fusion.1), channel_id=1, source_target_pairs={{0,2},{1,7},{2,4},{3,1},{4,6},{5,3},{6,0},{7,5},{8,10},{9,15},{10,... | collective-permute-start | bytes 196616 | tf_op jit(solution)/shard_map/ppermute | solution.py:51
  9.8 8.1 %collective-permute-start.1 = (bf16[2,64,256]{2,1,0:T(8,128)(2,1)S(1)}, bf16[2,64,256]{2,1,0:T(8,128)(2,1)S(1)}, u32[]{:S(2)}, u32[]{:S(2)}) collective-permute-start(bf16[2,64,256]{2,1,0:T(8,128)(2,1)S(1)} %maximum_select_fusion.1), channel_id=1, source_target_pairs={{0,34},{1,37},{2,36},{3,39},{4,38},{5,33},{6,32},{7,35},{8,42},{9,... | collective-permute-start | bytes 196616 | tf_op jit(solution)/shard_map/ppermute | solution.py:51
  13.8 7.9 %collective-permute-start.4 = (bf16[64,256]{1,0:T(8,128)(2,1)S(1)}, bf16[64,256]{1,0:T(8,128)(2,1)S(1)}, u32[]{:S(2)}, u32[]{:S(2)}) collective-permute-start(bf16[64,256]{1,0:T(8,128)(2,1)S(1)} %slice_select_fusion.1), channel_id=1, source_target_pairs={{0,4},{1,5},{2,6},{3,7},{4,0},{5,1},{6,2},{7,3},{8,12},{9,13},{10,... | collective-permute-start | bytes 98312 | tf_op jit(solution)/shard_map/ppermute | solution.py:34
  21.8 8.1 %collective-permute-start.9 = (bf16[8,64,256]{2,1,0:T(8,128)(2,1)S(1)}, bf16[8,64,256]{2,1,0:T(8,128)(2,1)S(1)}, u32[]{:S(2)}, u32[]{:S(2)}) collective-permute-start(bf16[8,64,256]{2,1,0:T(8,128)(2,1)S(1)} %get-tuple-element.60), channel_id=1, source_target_pairs={{0,16},{1,129},{2,18},{3,131},{4,20},{5,133},{6,22},{7,135},{8,24}... | collective-permute-start | bytes 786440 | tf_op jit(solution)/shard_map/ppermute | solution.py:43
  24.2 8.4 %collective-permute-start.10 = (bf16[8,64,256]{2,1,0:T(8,128)(2,1)S(1)}, bf16[8,64,256]{2,1,0:T(8,128)(2,1)S(1)}, u32[]{:S(2)}, u32[]{:S(2)}) collective-permute-start(bf16[8,64,256]{2,1,0:T(8,128)(2,1)S(1)} %get-tuple-element.60), channel_id=1, source_target_pairs={{0,24},{1,193},{2,26},{3,195},{4,28},{5,197},{6,30},{7,199},{8,0},... | collective-permute-start | bytes 786440 | tf_op jit(solution)/shard_map/ppermute | solution.py:43
  25.5 9.9 %collective-permute-start.6 = (bf16[8,64,256]{2,1,0:T(8,128)(2,1)S(1)}, bf16[8,64,256]{2,1,0:T(8,128)(2,1)S(1)}, u32[]{:S(2)}, u32[]{:S(2)}) collective-permute-start(bf16[8,64,256]{2,1,0:T(8,128)(2,1)S(1)} %get-tuple-element.60), channel_id=1, source_target_pairs={{0,8},{1,65},{2,10},{3,67},{4,12},{5,69},{6,14},{7,71},{8,16},{9,7... | collective-permute-start | bytes 786440 | tf_op jit(solution)/shard_map/ppermute | solution.py:43
  32.6 9.5 %collective-permute-start.11 = (bf16[2,8,64,256]{3,2,1,0:T(8,128)(2,1)S(1)}, bf16[2,8,64,256]{3,2,1,0:T(8,128)(2,1)}, u32[]{:S(2)}, u32[]{:S(2)}) collective-permute-start(bf16[2,8,64,256]{3,2,1,0:T(8,128)(2,1)S(1)} %pad_maximum_fusion.1.refs_1_), channel_id=1, source_target_pairs={{0,192},{1,25},{2,194},{3,27},{4,196},{5,29},{6,198},{7,31},{8,200... | collective-permute-start | bytes 1572872 | tf_op jit(solution)/shard_map/ppermute | solution.py:43
  35.5 10.6 %collective-permute-start.7 = (bf16[2,8,64,256]{3,2,1,0:T(8,128)(2,1)S(1)}, bf16[2,8,64,256]{3,2,1,0:T(8,128)(2,1)}, u32[]{:S(2)}, u32[]{:S(2)}) collective-permute-start(bf16[2,8,64,256]{3,2,1,0:T(8,128)(2,1)S(1)} %pad_maximum_fusion.refs_0_), channel_id=1, source_target_pairs={{0,64},{1,9},{2,66},{3,11},{4,68},{5,13},{6,70},{7,15},{8,72},{9,1... | collective-permute-start | bytes 1572872 | tf_op jit(solution)/shard_map/ppermute | solution.py:43
  35.6 16.1 %collective-permute-start.14 = (bf16[2,8,64,256]{3,2,1,0:T(8,128)(2,1)S(1)}, bf16[2,8,64,256]{3,2,1,0:T(8,128)(2,1)}, u32[]{:S(2)}, u32[]{:S(2)}) collective-permute-start(bf16[2,8,64,256]{3,2,1,0:T(8,128)(2,1)S(1)} %pad_maximum_fusion.1.refs_1_), channel_id=1, source_target_pairs={{0,64},{1,9},{2,66},{3,11},{4,68},{5,13},{6,70},{7,15},{8,72},{9,1... | collective-permute-start | bytes 1572872 | tf_op jit(solution)/shard_map/ppermute | solution.py:43
  36.4 15.4 %collective-permute-start.15 = (bf16[2,8,64,256]{3,2,1,0:T(8,128)(2,1)S(1)}, bf16[2,8,64,256]{3,2,1,0:T(8,128)(2,1)}, u32[]{:S(2)}, u32[]{:S(2)}) collective-permute-start(bf16[2,8,64,256]{3,2,1,0:T(8,128)(2,1)S(1)} %pad_maximum_fusion.refs_0_), channel_id=1, source_target_pairs={{0,192},{1,25},{2,194},{3,27},{4,196},{5,29},{6,198},{7,31},{8,200... | collective-permute-start | bytes 1572872 | tf_op jit(solution)/shard_map/ppermute | solution.py:43
  42.2 13.0 %collective-permute-start.12 = (bf16[2,8,64,256]{3,2,1,0:T(8,128)(2,1)}, bf16[2,8,64,256]{3,2,1,0:T(8,128)(2,1)}, u32[]{:S(2)}, u32[]{:S(2)}) collective-permute-start(bf16[2,8,64,256]{3,2,1,0:T(8,128)(2,1)} %collective-permute-done.11.refs_3_.refs_7_), channel_id=1, source_target_pairs={{0,192},{1,25},{2,194},{3,27},{4,196},{5,29},{6,198},{7,31},{8,200... | collective-permute-start | bytes 1572872 | tf_op jit(solution)/shard_map/ppermute | solution.py:43
  46.1 11.2 %collective-permute-start.8 = (bf16[2,8,64,256]{3,2,1,0:T(8,128)(2,1)}, bf16[2,8,64,256]{3,2,1,0:T(8,128)(2,1)}, u32[]{:S(2)}, u32[]{:S(2)}) collective-permute-start(bf16[2,8,64,256]{3,2,1,0:T(8,128)(2,1)} %collective-permute-done.7.refs_0_.refs_2_), channel_id=1, source_target_pairs={{0,64},{1,9},{2,66},{3,11},{4,68},{5,13},{6,70},{7,15},{8,72},{9,1... | collective-permute-start | bytes 1572872 | tf_op jit(solution)/shard_map/ppermute | solution.py:43
  71.4 10.5 %collective-permute-start.18 = (bf16[2,8,64,256]{3,2,1,0:T(8,128)(2,1)S(1)}, bf16[2,8,64,256]{3,2,1,0:T(8,128)(2,1)S(1)}, u32[]{:S(2)}, u32[]{:S(2)}) collective-permute-start(bf16[2,8,64,256]{3,2,1,0:T(8,128)(2,1)S(1)} %get-tuple-element.34.refs_0_), channel_id=1, source_target_pairs={{0,64},{1,9},{2,66},{3,11},{4,68},{5,13},{6,70},{7,15},{8,72},{9,1... | collective-permute-start | bytes 1572872 | tf_op jit(solution)/shard_map/ppermute | solution.py:43
  71.5 10.8 %collective-permute-start.23 = (bf16[2,8,64,256]{3,2,1,0:T(8,128)(2,1)S(1)}, bf16[2,8,64,256]{3,2,1,0:T(8,128)(2,1)S(1)}, u32[]{:S(2)}, u32[]{:S(2)}) collective-permute-start(bf16[2,8,64,256]{3,2,1,0:T(8,128)(2,1)S(1)} %get-tuple-element.41), channel_id=1, source_target_pairs={{0,192},{1,25},{2,194},{3,27},{4,196},{5,29},{6,198},{7,31},{8,200... | collective-permute-start | bytes 1572872 | tf_op jit(solution)/shard_map/ppermute | solution.py:43
  77.2 21.0 %collective-permute-start.20 = (bf16[2,8,64,256]{3,2,1,0:T(8,128)(2,1)S(1)}, bf16[2,8,64,256]{3,2,1,0:T(8,128)(2,1)S(1)}, u32[]{:S(2)}, u32[]{:S(2)}) collective-permute-start(bf16[2,8,64,256]{3,2,1,0:T(8,128)(2,1)S(1)} %get-tuple-element.37), channel_id=1, source_target_pairs={{0,192},{1,25},{2,194},{3,27},{4,196},{5,29},{6,198},{7,31},{8,200... | collective-permute-start | bytes 1572872 | tf_op jit(solution)/shard_map/ppermute | solution.py:43
  77.3 21.9 %collective-permute-start.22 = (bf16[2,8,64,256]{3,2,1,0:T(8,128)(2,1)S(1)}, bf16[2,8,64,256]{3,2,1,0:T(8,128)(2,1)S(1)}, u32[]{:S(2)}, u32[]{:S(2)}) collective-permute-start(bf16[2,8,64,256]{3,2,1,0:T(8,128)(2,1)S(1)} %get-tuple-element.39), channel_id=1, source_target_pairs={{0,64},{1,9},{2,66},{3,11},{4,68},{5,13},{6,70},{7,15},{8,72},{9,1... | collective-permute-start | bytes 1572872 | tf_op jit(solution)/shard_map/ppermute | solution.py:43
  82.1 16.2 %collective-permute-start.19 = (bf16[2,8,64,256]{3,2,1,0:T(8,128)(2,1)S(1)}, bf16[2,8,64,256]{3,2,1,0:T(8,128)(2,1)S(1)}, u32[]{:S(2)}, u32[]{:S(2)}) collective-permute-start(bf16[2,8,64,256]{3,2,1,0:T(8,128)(2,1)S(1)} %add_convert_fusion.2), channel_id=1, source_target_pairs={{0,64},{1,9},{2,66},{3,11},{4,68},{5,13},{6,70},{7,15},{8,72},{9,1... | collective-permute-start | bytes 1572872 | tf_op jit(solution)/shard_map/ppermute | solution.py:43
  82.5 16.7 %collective-permute-start.24 = (bf16[2,8,64,256]{3,2,1,0:T(8,128)(2,1)S(1)}, bf16[2,8,64,256]{3,2,1,0:T(8,128)(2,1)S(1)}, u32[]{:S(2)}, u32[]{:S(2)}) collective-permute-start(bf16[2,8,64,256]{3,2,1,0:T(8,128)(2,1)S(1)} %add_convert_fusion.1), channel_id=1, source_target_pairs={{0,192},{1,25},{2,194},{3,27},{4,196},{5,29},{6,198},{7,31},{8,200... | collective-permute-start | bytes 1572872 | tf_op jit(solution)/shard_map/ppermute | solution.py:43
  95.7 28.5 %collective-permute-start.29 = (bf16[16,256,256]{2,1,0:T(8,128)(2,1)S(1)}, bf16[16,256,256]{2,1,0:T(8,128)(2,1)S(1)}, u32[]{:S(2)}, u32[]{:S(2)}) collective-permute-start(bf16[16,256,256]{2,1,0:T(8,128)(2,1)S(1)} %get-tuple-element.45), channel_id=1, source_target_pairs={{0,1},{1,0},{2,3},{3,2},{4,5},{5,4},{6,7},{7,6},{8,9},{9,8},{10,11... | collective-permute-start | bytes 6291464 | tf_op jit(solution)/shard_map/ppermute | solution.py:34
  101.0 9.5 %collective-permute-start.26 = (bf16[8,64,256]{2,1,0:T(8,128)(2,1)S(1)}, bf16[8,64,256]{2,1,0:T(8,128)(2,1)S(1)}, u32[]{:S(2)}, u32[]{:S(2)}) collective-permute-start(bf16[8,64,256]{2,1,0:T(8,128)(2,1)S(1)} %get-tuple-element.51), channel_id=1, source_target_pairs={{0,16},{1,129},{2,18},{3,131},{4,20},{5,133},{6,22},{7,135},{8,24}... | collective-permute-start | bytes 786440 | tf_op jit(solution)/shard_map/ppermute | solution.py:43
  111.3 15.7 %collective-permute-start.32 = (bf16[64,256]{1,0:T(8,128)(2,1)}, bf16[64,256]{1,0:T(8,128)(2,1)}, u32[]{:S(2)}, u32[]{:S(2)}) collective-permute-start(bf16[64,256]{1,0:T(8,128)(2,1)} %get-tuple-element.52), channel_id=1, source_target_pairs={{0,4},{1,5},{2,6},{3,7},{4,0},{5,1},{6,2},{7,3},{8,12},{9,13},{10,... | collective-permute-start | bytes 98312 | tf_op jit(solution)/shard_map/ppermute | solution.py:34
  113.7 13.2 %collective-permute-start.30 = (bf16[2,64,256]{2,1,0:T(8,128)(2,1)S(1)}, bf16[2,64,256]{2,1,0:T(8,128)(2,1)S(1)}, u32[]{:S(2)}, u32[]{:S(2)}) collective-permute-start(bf16[2,64,256]{2,1,0:T(8,128)(2,1)S(1)} %pad_maximum_fusion.6), channel_id=1, source_target_pairs={{0,2},{1,7},{2,4},{3,1},{4,6},{5,3},{6,0},{7,5},{8,10},{9,15},{10,... | collective-permute-start | bytes 196616 | tf_op jit(solution)/shard_map/ppermute | solution.py:51
  118.5 8.4 %collective-permute-start.31 = (bf16[2,64,256]{2,1,0:T(8,128)(2,1)S(1)}, bf16[2,64,256]{2,1,0:T(8,128)(2,1)S(1)}, u32[]{:S(2)}, u32[]{:S(2)}) collective-permute-start(bf16[2,64,256]{2,1,0:T(8,128)(2,1)S(1)} %pad_maximum_fusion.7), channel_id=1, source_target_pairs={{0,32},{1,39},{2,34},{3,33},{4,36},{5,35},{6,38},{7,37},{8,40},{9,... | collective-permute-start | bytes 196616 | tf_op jit(solution)/shard_map/ppermute | solution.py:51
  (14 other events, 65.2 us)

commit v5 on v3

--- a/solution.py
+++ b/solution.py
@@ -217,7 +217,7 @@
 
 
 def weight_kernel(pos, *refs):
-    pieces, (g_own, g_par, _, own_ref, par_ref) = refs[:8], refs[8:]
+    pieces, (g_own, g_par, own_ref, par_ref) = refs[:8], refs[8:]
     x, y, z, c = pos[0], pos[1], pos[2], pos[3]
     order = [((x + 4 - dx) & 3) * 2 + zl for dx in range(4) for zl in range(2)]
     own = jnp.concatenate([g_own[m] for m in order], axis=0)
@@ -265,7 +265,7 @@
         out_specs=out_specs,
         out_shape=[jax.ShapeDtypeStruct(s, d) for s, d in outs],
         scratch_shapes=scratch,
-        compiler_params=pltpu.CompilerParams(vmem_limit_bytes=20 * 2**20),
+        compiler_params=pltpu.CompilerParams(vmem_limit_bytes=12 * 2**20),
     )
 
 
@@ -308,7 +308,7 @@
         ),
         out_shape=[jax.ShapeDtypeStruct((1, 8, 512, 128), BF)] * 2
         + [jax.ShapeDtypeStruct((8, 64, 256), BF)] * 2,
-        compiler_params=pltpu.CompilerParams(vmem_limit_bytes=24 * 2**20),
+        compiler_params=pltpu.CompilerParams(vmem_limit_bytes=12 * 2**20),
         name="attend",
     )(pos, lens, queries, d_context, keep, recv)
 
@@ -379,9 +379,11 @@
     from_left_low = cross(total([right_low_g, pass_low]), 1, 0)
     from_right_high = cross(total([left_high_g, pass_high]), 3, 0)
 
+    states_in = (low, high, right_low, right_high, far_low, far_high, left_low, left_high)
+
     grad_own, grad_par = whole(
-        weight_kernel, [VMEM] * 10 + [HBM], [((16, 256, 256), BF)] * 2, [VMEM] * 2, []
-    )(pos, low, high, right_low, right_high, far_low, far_high, left_low, left_high, grad_keep, grad_recv, own_low)
+        weight_kernel, [VMEM] * 10, [((16, 256, 256), BF)] * 2, [VMEM] * 2, []
+    )(pos, *states_in, grad_keep, grad_recv)
     grad_other = shift(grad_par, dc=1)
     weight_grad = total([grad_own, grad_other]).reshape(1, 4096, 2, 128)
 
@@ -390,7 +392,6 @@
     got = [low[0]]
     for k in (1, 3, 2):
         got.append(cross((low + high)[k], k, 1))
-    got[0], weight_grad = lax.optimization_barrier((got[0], weight_grad))
     passed = [total([p[8 - k] for p in got]) for k in (3, 2, 1)]
     passed = shift(jnp.stack(passed), dc=1)
     across = shift(total([p[4] for p in got]), dz=4)
@@ -398,6 +399,7 @@
     for i, k in enumerate((3, 2, 1)):
         both = jnp.stack([total([p[k] for p in got]), passed[i]])
         got_z.append(rise(both, k).astype(F32))
+    got_z[0], weight_grad = lax.optimization_barrier((got_z[0], weight_grad))
     both = got_z[0] + got_z[1] + got_z[2]
     mine = functools.reduce(lambda p, q: p + q, [p[0].astype(F32) for p in got])
     both = jnp.stack([both[0] + mine + across.astype(F32), both[1]]).reshape(2, 64, 2, 128)

time: 138 us -> 126 us (0.913)
  waiting for transfers between devices: 41.9 us -> 25.3 us
  starting transfers between devices: 60.4 us -> 64.9 us
    ppermute x18, waiting for transfers between devices: 31.9 us -> 19.7 us  [cross(): return lax.ppermute(value, AXES, pairs)]
    ppermute x10, waiting for transfers between devices: 9.35 us -> 4.86 us  [shift(): return lax.ppermute(value, AXES, pairs)]
    ppermute x6, starting transfers between devices: 11.1 us -> 13.5 us  [rise(): return lax.ppermute(value, AXES, pairs)]
    ppermute x18, starting transfers between devices: 21.9 us -> 24.2 us  [cross(): return lax.ppermute(value, AXES, pairs)]
    convert_element_type x6, other arithmetic: 2.98 us -> 1.5 us  [total(): functools.reduce(lambda p, q: p + q, [p.astype(F32) for p in parts])]
  transfers between devices with their start and end apart: 34 -> 34, of which waited for: 20 -> 16; matrix products, arithmetic and copies ran while one was open for 6% -> 6% of each run, Pallas kernels for 4% -> 13%
where the time goes in v5:
time: 126 us
  starting transfers between devices  64.9 us (52%)
  waiting for transfers between devices  25.3 us (20%)
  Pallas kernels  25.3 us (20%)
  local copies, waits for them, and re-layouts  5.26 us (4%)
  other arithmetic  4.02 us (3%)
    ppermute x10, starting transfers between devices, shift(): return lax.ppermute(value, AXES, pairs)  27.3 us
    ppermute x18, starting transfers between devices, cross(): return lax.ppermute(value, AXES, pairs)  24.2 us
    ppermute x18, waiting for transfers between devices, cross(): return lax.ppermute(value, AXES, pairs)  19.7 us
    ppermute x6, starting transfers between devices, rise(): return lax.ppermute(value, AXES, pairs)  13.5 us
    pallas_call x1, Pallas kernels, shards(): whole(weight_kernel, [VMEM] * 10, [((16, 256, 256), BF)] * 2, [VMEM] * 2,...  7.69 us
    pallas_call x3, Pallas kernels, project(): whole(functools.partial(project_kernel, which, first, last), [VMEM] * (2...  7.4 us
    pallas_call x1, Pallas kernels, attend(): pl.pallas_call(attend_kernel, grid_spec=pltpu.PrefetchScalarGridSpec(num_...  5.77 us
    ppermute x10, waiting for transfers between devices, shift(): return lax.ppermute(value, AXES, pairs)  4.86 us
  transfers between devices with their start and end apart: 34, of which 16 were waited for; matrix products, arithmetic and copies ran while one was open for 6% of the time, Pallas kernels for 13%

profile of v5, /device:TPU:1, one launch (start us, length us, event | category | flops | bytes accessed | tf_op | source)
XLA Modules:
  0.0 125.8 jit_solution(5448462572632369532)
XLA Ops:
  0.6 3.3 %collective-permute-start = (bf16[128,128]{1,0:T(8,128)(2,1)}, bf16[128,128]{1,0:T(8,128)(2,1)S(1)}, u32[]{:S(2)}, u32[]{:S(2)}) collective-permute-start(bf16[128,128]{1,0:T(8,128)(2,1)} %bitcast.96), channel_id=1, source_target_pairs={{0,1},{1,0},{2,3},{3,2},{4,5},{5,4},{6,7},{7,6},{8,9},{9,8},{10,11... | collective-permute-start | bytes 98312 | tf_op jit(solution)/shard_map/ppermute | solution.py:34
  3.9 3.2 %reshape.133.refs_2_.refs_4_.wo = bf16[16,256,256]{2,1,0:T(8,128)(2,1)S(1)} reshape(bf16[1,4096,2,128]{3,2,1,0:T(2,128)(2,1)} %param.7) | data formatting | bytes 4194304 | tf_op jit(solution)/shard_map/reshape | solution.py:345
  7.2 3.9 %collective-permute-start.3 = (bf16[2,64,256]{2,1,0:T(8,128)(2,1)S(1)}, bf16[2,64,256]{2,1,0:T(8,128)(2,1)S(1)}, u32[]{:S(2)}, u32[]{:S(2)}) collective-permute-start(bf16[2,64,256]{2,1,0:T(8,128)(2,1)S(1)} %maximum_select_fusion.1), channel_id=1, source_target_pairs={{0,32},{1,39},{2,34},{3,33},{4,36},{5,35},{6,38},{7,37},{8,40},{9,... | collective-permute-start | bytes 196616 | tf_op jit(solution)/shard_map/ppermute | solution.py:51
  12.9 4.6 %collective-permute-start.4 = (bf16[64,256]{1,0:T(8,128)(2,1)S(1)}, bf16[64,256]{1,0:T(8,128)(2,1)S(1)}, u32[]{:S(2)}, u32[]{:S(2)}) collective-permute-start(bf16[64,256]{1,0:T(8,128)(2,1)S(1)} %slice_select_fusion.1), channel_id=1, source_target_pairs={{0,4},{1,5},{2,6},{3,7},{4,0},{5,1},{6,2},{7,3},{8,12},{9,13},{10,... | collective-permute-start | bytes 98312 | tf_op jit(solution)/shard_map/ppermute | solution.py:34
  25.6 2.5 %collective-permute-done.6 = bf16[8,64,256]{2,1,0:T(8,128)(2,1)S(1)} collective-permute-done((bf16[8,64,256]{2,1,0:T(8,128)(2,1)S(1)}, bf16[8,64,256]{2,1,0:T(8,128)(2,1)S(1)}, u32[]{:S(2)}, u32[]{:S(2)}) %collective-permute-start.6) | collective-permute-done | bytes 262176 | tf_op jit(solution)/shard_map/ppermute | solution.py:43
  29.3 2.7 %collective-permute-done.9 = bf16[8,64,256]{2,1,0:T(8,128)(2,1)S(1)} collective-permute-done((bf16[8,64,256]{2,1,0:T(8,128)(2,1)S(1)}, bf16[8,64,256]{2,1,0:T(8,128)(2,1)S(1)}, u32[]{:S(2)}, u32[]{:S(2)}) %collective-permute-start.9) | collective-permute-done | bytes 262176 | tf_op jit(solution)/shard_map/ppermute | solution.py:43
  32.0 2.8 %collective-permute-start.11 = (bf16[2,8,64,256]{3,2,1,0:T(8,128)(2,1)S(1)}, bf16[2,8,64,256]{3,2,1,0:T(8,128)(2,1)}, u32[]{:S(2)}, u32[]{:S(2)}) collective-permute-start(bf16[2,8,64,256]{3,2,1,0:T(8,128)(2,1)S(1)} %pad_maximum_fusion.1.refs_1_), channel_id=1, source_target_pairs={{0,192},{1,25},{2,194},{3,27},{4,196},{5,29},{6,198},{7,31},{8,200... | collective-permute-start | bytes 1572872 | tf_op jit(solution)/shard_map/ppermute | solution.py:43
  34.8 2.7 %collective-permute-start.15 = (bf16[2,8,64,256]{3,2,1,0:T(8,128)(2,1)S(1)}, bf16[2,8,64,256]{3,2,1,0:T(8,128)(2,1)}, u32[]{:S(2)}, u32[]{:S(2)}) collective-permute-start(bf16[2,8,64,256]{3,2,1,0:T(8,128)(2,1)S(1)} %pad_maximum_fusion.refs_0_), channel_id=1, source_target_pairs={{0,192},{1,25},{2,194},{3,27},{4,196},{5,29},{6,198},{7,31},{8,200... | collective-permute-start | bytes 1572872 | tf_op jit(solution)/shard_map/ppermute | solution.py:43
  37.5 2.9 %collective-permute-done.7.refs_0_.refs_2_ = bf16[2,8,64,256]{3,2,1,0:T(8,128)(2,1)} collective-permute-done((bf16[2,8,64,256]{3,2,1,0:T(8,128)(2,1)S(1)}, bf16[2,8,64,256]{3,2,1,0:T(8,128)(2,1)}, u32[]{:S(2)}, u32[]{:S(2)}) %collective-permute-start.7) | collective-permute-done | bytes 524320 | tf_op jit(solution)/shard_map/ppermute | solution.py:43
  40.9 3.5 %collective-permute-start.12 = (bf16[2,8,64,256]{3,2,1,0:T(8,128)(2,1)}, bf16[2,8,64,256]{3,2,1,0:T(8,128)(2,1)}, u32[]{:S(2)}, u32[]{:S(2)}) collective-permute-start(bf16[2,8,64,256]{3,2,1,0:T(8,128)(2,1)} %collective-permute-done.11.refs_3_.refs_7_), channel_id=1, source_target_pairs={{0,192},{1,25},{2,194},{3,27},{4,196},{5,29},{6,198},{7,31},{8,200... | collective-permute-start | bytes 1572872 | tf_op jit(solution)/shard_map/ppermute | solution.py:43
  44.5 2.6 %shard_map.84 = (bf16[16,256,256]{2,1,0:T(8,128)(2,1)S(1)}, f32[512,512]{1,0:T(8,128)S(1)}) custom-call(s32[4]{0:T(128)S(1)} %pad_add_fusion.pos, bf16[2,8,64,256]{3,2,1,0:T(8,128)(2,1)S(1)} %pad_maximum_fusion.refs_0_, bf16[2,8,64,256]{3,2,1,0:T(8,128)(2,1)S(1)} %pad_maximum_fusion.1.refs_1_, bf16[16,256,256]{2,1,0:T(8,128)(2,1)S(1)} %reshape.133.refs_2_.refs_4_.wo, ...), custom_call_target="tpu_custom_call" | custom-call | tf_op jit(solution)/shard_map/pallas_call | solution.py:279
  47.2 2.8 %shard_map.85.refs_4_ = f32[512,512]{1,0:T(8,128)S(1)} custom-call(s32[4]{0:T(128)S(1)} %pad_add_fusion.pos, bf16[2,8,64,256]{3,2,1,0:T(8,128)(2,1)} %collective-permute-done.7.refs_0_.refs_2_, bf16[2,8,64,256]{3,2,1,0:T(8,128)(2,1)} %collective-permute-done.14.refs_1_.refs_3_, bf16[2,8,64,256]{3,2,1,0:T(8,128)(2,1)} %collective-permute-done.15.refs_2_.refs_6_, ...), custom_call_target="tpu_custom_call" | custom-call | tf_op jit(solution)/shard_map/pallas_call | solution.py:279
  52.3 2.0 %shard_map.86 = (bf16[8,64,256]{2,1,0:T(8,128)(2,1)S(1)}, bf16[8,64,256]{2,1,0:T(8,128)(2,1)S(1)}) custom-call(s32[4]{0:T(128)S(1)} %pad_add_fusion.pos, bf16[2,8,64,256]{3,2,1,0:T(8,128)(2,1)} %collective-permute-done.8.refs_0_.refs_4_, bf16[2,8,64,256]{3,2,1,0:T(8,128)(2,1)} %collective-permute-done.12.refs_1_.refs_5_, ...), custom_call_target="tpu_custom_call" | custom-call | tf_op jit(solution)/shard_map/pallas_call | solution.py:279
  54.2 6.8 %collective-permute-start.16 = (bf16[8,64,256]{2,1,0:T(8,128)(2,1)S(1)}, bf16[8,64,256]{2,1,0:T(8,128)(2,1)S(1)}, u32[]{:S(2)}, u32[]{:S(2)}) collective-permute-start(bf16[8,64,256]{2,1,0:T(8,128)(2,1)S(1)} %get-tuple-element.27), channel_id=1, source_target_pairs={{0,1},{1,0},{2,3},{3,2},{4,5},{5,4},{6,7},{7,6},{8,9},{9,8},{10,11... | collective-permute-start | bytes 786440 | tf_op jit(solution)/shard_map/ppermute | solution.py:34
  62.2 5.8 %attend.1 = (bf16[1,8,512,128]{3,2,1,0:T(8,128)(2,1)}, bf16[1,8,512,128]{3,2,1,0:T(8,128)(2,1)}, bf16[8,64,256]{2,1,0:T(8,128)(2,1)S(1)}, bf16[8,64,256]{2,1,0:T(8,128)(2,1)S(1)}) custom-call(s32[4]{0:T(128)S(1)} %pad_add_fusion.pos, s32[8]{0:T(128)S(1)} %copy-done.2, bf16[1,8,512,128]{3,2,1,0:T(8,128)(2,1)S(1)} %copy-done, ...), custom_call_target="tpu_custom_call" | custom-call | tf_op jit(solution)/shard_map/attend/pallas_call | solution.py:301
  74.3 2.7 %collective-permute-start.20 = (bf16[2,8,64,256]{3,2,1,0:T(8,128)(2,1)S(1)}, bf16[2,8,64,256]{3,2,1,0:T(8,128)(2,1)S(1)}, u32[]{:S(2)}, u32[]{:S(2)}) collective-permute-start(bf16[2,8,64,256]{3,2,1,0:T(8,128)(2,1)S(1)} %get-tuple-element.35), channel_id=1, source_target_pairs={{0,192},{1,25},{2,194},{3,27},{4,196},{5,29},{6,198},{7,31},{8,200... | collective-permute-start | bytes 1572872 | tf_op jit(solution)/shard_map/ppermute | solution.py:43
  77.0 2.3 %collective-permute-done.23 = bf16[2,8,64,256]{3,2,1,0:T(8,128)(2,1)S(1)} collective-permute-done((bf16[2,8,64,256]{3,2,1,0:T(8,128)(2,1)S(1)}, bf16[2,8,64,256]{3,2,1,0:T(8,128)(2,1)S(1)}, u32[]{:S(2)}, u32[]{:S(2)}) %collective-permute-start.23) | collective-permute-done | bytes 524320 | tf_op jit(solution)/shard_map/ppermute | solution.py:43
  81.4 7.7 %shard_map.90 = (bf16[16,256,256]{2,1,0:T(8,128)(2,1)S(1)}, bf16[16,256,256]{2,1,0:T(8,128)(2,1)S(1)}) custom-call(s32[4]{0:T(128)S(1)} %pad_add_fusion.pos, bf16[2,8,64,256]{3,2,1,0:T(8,128)(2,1)S(1)} %pad_maximum_fusion.refs_0_, bf16[2,8,64,256]{3,2,1,0:T(8,128)(2,1)S(1)} %pad_maximum_fusion.1.refs_1_, ...), custom_call_target="tpu_custom_call" | custom-call | tf_op jit(solution)/shard_map/pallas_call | solution.py:384
  89.1 6.0 %collective-permute-start.29 = (bf16[16,256,256]{2,1,0:T(8,128)(2,1)S(1)}, bf16[16,256,256]{2,1,0:T(8,128)(2,1)S(1)}, u32[]{:S(2)}, u32[]{:S(2)}) collective-permute-start(bf16[16,256,256]{2,1,0:T(8,128)(2,1)S(1)} %get-tuple-element.41), channel_id=1, source_target_pairs={{0,1},{1,0},{2,3},{3,2},{4,5},{5,4},{6,7},{7,6},{8,9},{9,8},{10,11... | collective-permute-start | bytes 6291464 | tf_op jit(solution)/shard_map/ppermute | solution.py:34
  100.7 3.2 %collective-permute-done.26 = bf16[8,64,256]{2,1,0:T(8,128)(2,1)S(1)} collective-permute-done((bf16[8,64,256]{2,1,0:T(8,128)(2,1)S(1)}, bf16[8,64,256]{2,1,0:T(8,128)(2,1)S(1)}, u32[]{:S(2)}, u32[]{:S(2)}) %collective-permute-start.26) | collective-permute-done | bytes 262176 | tf_op jit(solution)/shard_map/ppermute | solution.py:43
  103.9 3.4 %collective-permute-done.25 = bf16[8,64,256]{2,1,0:T(8,128)(2,1)S(1)} collective-permute-done((bf16[8,64,256]{2,1,0:T(8,128)(2,1)S(1)}, bf16[8,64,256]{2,1,0:T(8,128)(2,1)S(1)}, u32[]{:S(2)}, u32[]{:S(2)}) %collective-permute-start.25) | collective-permute-done | bytes 262176 | tf_op jit(solution)/shard_map/ppermute | solution.py:43
  110.6 3.2 %collective-permute-start.28 = (bf16[2,64,256]{2,1,0:T(8,128)(2,1)S(1)}, bf16[2,64,256]{2,1,0:T(8,128)(2,1)S(1)}, u32[]{:S(2)}, u32[]{:S(2)}) collective-permute-start(bf16[2,64,256]{2,1,0:T(8,128)(2,1)S(1)} %pad_maximum_fusion.5), channel_id=1, source_target_pairs={{0,34},{1,37},{2,36},{3,39},{4,38},{5,33},{6,32},{7,35},{8,42},{9,... | collective-permute-start | bytes 196616 | tf_op jit(solution)/shard_map/ppermute | solution.py:51
  115.4 3.1 %collective-permute-start.30 = (bf16[2,64,256]{2,1,0:T(8,128)(2,1)S(1)}, bf16[2,64,256]{2,1,0:T(8,128)(2,1)S(1)}, u32[]{:S(2)}, u32[]{:S(2)}) collective-permute-start(bf16[2,64,256]{2,1,0:T(8,128)(2,1)S(1)} %pad_maximum_fusion.6), channel_id=1, source_target_pairs={{0,2},{1,7},{2,4},{3,1},{4,6},{5,3},{6,0},{7,5},{8,10},{9,15},{10,... | collective-permute-start | bytes 196616 | tf_op jit(solution)/shard_map/ppermute | solution.py:51
  119.6 2.0 %reshape.134 = bf16[1,4096,2,128]{3,2,1,0:T(2,128)(2,1)} reshape(bf16[16,256,256]{2,1,0:T(8,128)(2,1)S(1)} %add_convert_fusion) | data formatting | bytes 4194304 | tf_op jit(solution)/shard_map/reshape | solution.py:388
  (96 shorter events, 39.3 us)
Async XLA Ops:
  7.1 37.4 %collective-permute-start.13 = (bf16[16,256,256]{2,1,0:T(8,128)(2,1)S(1)}, bf16[16,256,256]{2,1,0:T(8,128)(2,1)}, u32[]{:S(2)}, u32[]{:S(2)}) collective-permute-start(bf16[16,256,256]{2,1,0:T(8,128)(2,1)S(1)} %reshape.133.refs_2_.refs_4_.wo), channel_id=1, source_target_pairs={{0,1},{1,0},{2,3},{3,2},{4,5},{5,4},{6,7},{7,6},{8,9},{9,8},{10,11... | collective-permute-start | bytes 6291464 | tf_op jit(solution)/shard_map/ppermute | solution.py:34
  7.2 10.2 %collective-permute-start.3 = (bf16[2,64,256]{2,1,0:T(8,128)(2,1)S(1)}, bf16[2,64,256]{2,1,0:T(8,128)(2,1)S(1)}, u32[]{:S(2)}, u32[]{:S(2)}) collective-permute-start(bf16[2,64,256]{2,1,0:T(8,128)(2,1)S(1)} %maximum_select_fusion.1), channel_id=1, source_target_pairs={{0,32},{1,39},{2,34},{3,33},{4,36},{5,35},{6,38},{7,37},{8,40},{9,... | collective-permute-start | bytes 196616 | tf_op jit(solution)/shard_map/ppermute | solution.py:51
  12.9 8.4 %collective-permute-start.4 = (bf16[64,256]{1,0:T(8,128)(2,1)S(1)}, bf16[64,256]{1,0:T(8,128)(2,1)S(1)}, u32[]{:S(2)}, u32[]{:S(2)}) collective-permute-start(bf16[64,256]{1,0:T(8,128)(2,1)S(1)} %slice_select_fusion.1), channel_id=1, source_target_pairs={{0,4},{1,5},{2,6},{3,7},{4,0},{5,1},{6,2},{7,3},{8,12},{9,13},{10,... | collective-permute-start | bytes 98312 | tf_op jit(solution)/shard_map/ppermute | solution.py:34
  24.1 7.8 %collective-permute-start.9 = (bf16[8,64,256]{2,1,0:T(8,128)(2,1)S(1)}, bf16[8,64,256]{2,1,0:T(8,128)(2,1)S(1)}, u32[]{:S(2)}, u32[]{:S(2)}) collective-permute-start(bf16[8,64,256]{2,1,0:T(8,128)(2,1)S(1)} %get-tuple-element.56), channel_id=1, source_target_pairs={{0,16},{1,129},{2,18},{3,131},{4,20},{5,133},{6,22},{7,135},{8,24}... | collective-permute-start | bytes 786440 | tf_op jit(solution)/shard_map/ppermute | solution.py:43
  28.2 12.2 %collective-permute-start.7 = (bf16[2,8,64,256]{3,2,1,0:T(8,128)(2,1)S(1)}, bf16[2,8,64,256]{3,2,1,0:T(8,128)(2,1)}, u32[]{:S(2)}, u32[]{:S(2)}) collective-permute-start(bf16[2,8,64,256]{3,2,1,0:T(8,128)(2,1)S(1)} %pad_maximum_fusion.refs_0_), channel_id=1, source_target_pairs={{0,64},{1,9},{2,66},{3,11},{4,68},{5,13},{6,70},{7,15},{8,72},{9,1... | collective-permute-start | bytes 1572872 | tf_op jit(solution)/shard_map/ppermute | solution.py:43
  32.0 8.9 %collective-permute-start.11 = (bf16[2,8,64,256]{3,2,1,0:T(8,128)(2,1)S(1)}, bf16[2,8,64,256]{3,2,1,0:T(8,128)(2,1)}, u32[]{:S(2)}, u32[]{:S(2)}) collective-permute-start(bf16[2,8,64,256]{3,2,1,0:T(8,128)(2,1)S(1)} %pad_maximum_fusion.1.refs_1_), channel_id=1, source_target_pairs={{0,192},{1,25},{2,194},{3,27},{4,196},{5,29},{6,198},{7,31},{8,200... | collective-permute-start | bytes 1572872 | tf_op jit(solution)/shard_map/ppermute | solution.py:43
  34.8 12.4 %collective-permute-start.14 = (bf16[2,8,64,256]{3,2,1,0:T(8,128)(2,1)S(1)}, bf16[2,8,64,256]{3,2,1,0:T(8,128)(2,1)}, u32[]{:S(2)}, u32[]{:S(2)}) collective-permute-start(bf16[2,8,64,256]{3,2,1,0:T(8,128)(2,1)S(1)} %pad_maximum_fusion.1.refs_1_), channel_id=1, source_target_pairs={{0,64},{1,9},{2,66},{3,11},{4,68},{5,13},{6,70},{7,15},{8,72},{9,1... | collective-permute-start | bytes 1572872 | tf_op jit(solution)/shard_map/ppermute | solution.py:43
  34.8 12.4 %collective-permute-start.15 = (bf16[2,8,64,256]{3,2,1,0:T(8,128)(2,1)S(1)}, bf16[2,8,64,256]{3,2,1,0:T(8,128)(2,1)}, u32[]{:S(2)}, u32[]{:S(2)}) collective-permute-start(bf16[2,8,64,256]{3,2,1,0:T(8,128)(2,1)S(1)} %pad_maximum_fusion.refs_0_), channel_id=1, source_target_pairs={{0,192},{1,25},{2,194},{3,27},{4,196},{5,29},{6,198},{7,31},{8,200... | collective-permute-start | bytes 1572872 | tf_op jit(solution)/shard_map/ppermute | solution.py:43
  40.3 11.2 %collective-permute-start.8 = (bf16[2,8,64,256]{3,2,1,0:T(8,128)(2,1)}, bf16[2,8,64,256]{3,2,1,0:T(8,128)(2,1)}, u32[]{:S(2)}, u32[]{:S(2)}) collective-permute-start(bf16[2,8,64,256]{3,2,1,0:T(8,128)(2,1)} %collective-permute-done.7.refs_0_.refs_2_), channel_id=1, source_target_pairs={{0,64},{1,9},{2,66},{3,11},{4,68},{5,13},{6,70},{7,15},{8,72},{9,1... | collective-permute-start | bytes 1572872 | tf_op jit(solution)/shard_map/ppermute | solution.py:43
  40.9 11.3 %collective-permute-start.12 = (bf16[2,8,64,256]{3,2,1,0:T(8,128)(2,1)}, bf16[2,8,64,256]{3,2,1,0:T(8,128)(2,1)}, u32[]{:S(2)}, u32[]{:S(2)}) collective-permute-start(bf16[2,8,64,256]{3,2,1,0:T(8,128)(2,1)} %collective-permute-done.11.refs_3_.refs_7_), channel_id=1, source_target_pairs={{0,192},{1,25},{2,194},{3,27},{4,196},{5,29},{6,198},{7,31},{8,200... | collective-permute-start | bytes 1572872 | tf_op jit(solution)/shard_map/ppermute | solution.py:43
  54.2 8.0 %collective-permute-start.16 = (bf16[8,64,256]{2,1,0:T(8,128)(2,1)S(1)}, bf16[8,64,256]{2,1,0:T(8,128)(2,1)S(1)}, u32[]{:S(2)}, u32[]{:S(2)}) collective-permute-start(bf16[8,64,256]{2,1,0:T(8,128)(2,1)S(1)} %get-tuple-element.27), channel_id=1, source_target_pairs={{0,1},{1,0},{2,3},{3,2},{4,5},{5,4},{6,7},{7,6},{8,9},{9,8},{10,11... | collective-permute-start | bytes 786440 | tf_op jit(solution)/shard_map/ppermute | solution.py:34
  70.8 8.4 %collective-permute-start.23 = (bf16[2,8,64,256]{3,2,1,0:T(8,128)(2,1)S(1)}, bf16[2,8,64,256]{3,2,1,0:T(8,128)(2,1)S(1)}, u32[]{:S(2)}, u32[]{:S(2)}) collective-permute-start(bf16[2,8,64,256]{3,2,1,0:T(8,128)(2,1)S(1)} %get-tuple-element.39), channel_id=1, source_target_pairs={{0,192},{1,25},{2,194},{3,27},{4,196},{5,29},{6,198},{7,31},{8,200... | collective-permute-start | bytes 1572872 | tf_op jit(solution)/shard_map/ppermute | solution.py:43
  70.9 10.0 %collective-permute-start.18 = (bf16[2,8,64,256]{3,2,1,0:T(8,128)(2,1)S(1)}, bf16[2,8,64,256]{3,2,1,0:T(8,128)(2,1)S(1)}, u32[]{:S(2)}, u32[]{:S(2)}) collective-permute-start(bf16[2,8,64,256]{3,2,1,0:T(8,128)(2,1)S(1)} %get-tuple-element.32.refs_0_), channel_id=1, source_target_pairs={{0,64},{1,9},{2,66},{3,11},{4,68},{5,13},{6,70},{7,15},{8,72},{9,1... | collective-permute-start | bytes 1572872 | tf_op jit(solution)/shard_map/ppermute | solution.py:43
  74.2 22.2 %collective-permute-start.22 = (bf16[2,8,64,256]{3,2,1,0:T(8,128)(2,1)S(1)}, bf16[2,8,64,256]{3,2,1,0:T(8,128)(2,1)S(1)}, u32[]{:S(2)}, u32[]{:S(2)}) collective-permute-start(bf16[2,8,64,256]{3,2,1,0:T(8,128)(2,1)S(1)} %get-tuple-element.37), channel_id=1, source_target_pairs={{0,64},{1,9},{2,66},{3,11},{4,68},{5,13},{6,70},{7,15},{8,72},{9,1... | collective-permute-start | bytes 1572872 | tf_op jit(solution)/shard_map/ppermute | solution.py:43
  74.3 25.5 %collective-permute-start.20 = (bf16[2,8,64,256]{3,2,1,0:T(8,128)(2,1)S(1)}, bf16[2,8,64,256]{3,2,1,0:T(8,128)(2,1)S(1)}, u32[]{:S(2)}, u32[]{:S(2)}) collective-permute-start(bf16[2,8,64,256]{3,2,1,0:T(8,128)(2,1)S(1)} %get-tuple-element.35), channel_id=1, source_target_pairs={{0,192},{1,25},{2,194},{3,27},{4,196},{5,29},{6,198},{7,31},{8,200... | collective-permute-start | bytes 1572872 | tf_op jit(solution)/shard_map/ppermute | solution.py:43
  79.4 17.1 %collective-permute-start.24 = (bf16[2,8,64,256]{3,2,1,0:T(8,128)(2,1)S(1)}, bf16[2,8,64,256]{3,2,1,0:T(8,128)(2,1)S(1)}, u32[]{:S(2)}, u32[]{:S(2)}) collective-permute-start(bf16[2,8,64,256]{3,2,1,0:T(8,128)(2,1)S(1)} %add_convert_fusion.1), channel_id=1, source_target_pairs={{0,192},{1,25},{2,194},{3,27},{4,196},{5,29},{6,198},{7,31},{8,200... | collective-permute-start | bytes 1572872 | tf_op jit(solution)/shard_map/ppermute | solution.py:43
  81.1 18.8 %collective-permute-start.19 = (bf16[2,8,64,256]{3,2,1,0:T(8,128)(2,1)S(1)}, bf16[2,8,64,256]{3,2,1,0:T(8,128)(2,1)S(1)}, u32[]{:S(2)}, u32[]{:S(2)}) collective-permute-start(bf16[2,8,64,256]{3,2,1,0:T(8,128)(2,1)S(1)} %add_convert_fusion.2), channel_id=1, source_target_pairs={{0,64},{1,9},{2,66},{3,11},{4,68},{5,13},{6,70},{7,15},{8,72},{9,1... | collective-permute-start | bytes 1572872 | tf_op jit(solution)/shard_map/ppermute | solution.py:43
  89.1 29.8 %collective-permute-start.29 = (bf16[16,256,256]{2,1,0:T(8,128)(2,1)S(1)}, bf16[16,256,256]{2,1,0:T(8,128)(2,1)S(1)}, u32[]{:S(2)}, u32[]{:S(2)}) collective-permute-start(bf16[16,256,256]{2,1,0:T(8,128)(2,1)S(1)} %get-tuple-element.41), channel_id=1, source_target_pairs={{0,1},{1,0},{2,3},{3,2},{4,5},{5,4},{6,7},{7,6},{8,9},{9,8},{10,11... | collective-permute-start | bytes 6291464 | tf_op jit(solution)/shard_map/ppermute | solution.py:34
  96.7 7.1 %collective-permute-start.26 = (bf16[8,64,256]{2,1,0:T(8,128)(2,1)S(1)}, bf16[8,64,256]{2,1,0:T(8,128)(2,1)S(1)}, u32[]{:S(2)}, u32[]{:S(2)}) collective-permute-start(bf16[8,64,256]{2,1,0:T(8,128)(2,1)S(1)} %get-tuple-element.47), channel_id=1, source_target_pairs={{0,16},{1,129},{2,18},{3,131},{4,20},{5,133},{6,22},{7,135},{8,24}... | collective-permute-start | bytes 786440 | tf_op jit(solution)/shard_map/ppermute | solution.py:43
  98.0 9.2 %collective-permute-start.25 = (bf16[8,64,256]{2,1,0:T(8,128)(2,1)S(1)}, bf16[8,64,256]{2,1,0:T(8,128)(2,1)S(1)}, u32[]{:S(2)}, u32[]{:S(2)}) collective-permute-start(bf16[8,64,256]{2,1,0:T(8,128)(2,1)S(1)} %get-tuple-element.46), channel_id=1, source_target_pairs={{0,24},{1,193},{2,26},{3,195},{4,28},{5,197},{6,30},{7,199},{8,0},... | collective-permute-start | bytes 786440 | tf_op jit(solution)/shard_map/ppermute | solution.py:43
  100.1 7.1 %collective-permute-start.21 = (bf16[8,64,256]{2,1,0:T(8,128)(2,1)S(1)}, bf16[8,64,256]{2,1,0:T(8,128)(2,1)S(1)}, u32[]{:S(2)}, u32[]{:S(2)}) collective-permute-start(bf16[8,64,256]{2,1,0:T(8,128)(2,1)S(1)} %get-tuple-element.45), channel_id=1, source_target_pairs={{0,8},{1,65},{2,10},{3,67},{4,12},{5,69},{6,14},{7,71},{8,16},{9,7... | collective-permute-start | bytes 786440 | tf_op jit(solution)/shard_map/ppermute | solution.py:43
  109.6 12.2 %collective-permute-start.32 = (bf16[64,256]{1,0:T(8,128)(2,1)}, bf16[64,256]{1,0:T(8,128)(2,1)}, u32[]{:S(2)}, u32[]{:S(2)}) collective-permute-start(bf16[64,256]{1,0:T(8,128)(2,1)} %get-tuple-element.48), channel_id=1, source_target_pairs={{0,4},{1,5},{2,6},{3,7},{4,0},{5,1},{6,2},{7,3},{8,12},{9,13},{10,... | collective-permute-start | bytes 98312 | tf_op jit(solution)/shard_map/ppermute | solution.py:34
  110.6 8.3 %collective-permute-start.28 = (bf16[2,64,256]{2,1,0:T(8,128)(2,1)S(1)}, bf16[2,64,256]{2,1,0:T(8,128)(2,1)S(1)}, u32[]{:S(2)}, u32[]{:S(2)}) collective-permute-start(bf16[2,64,256]{2,1,0:T(8,128)(2,1)S(1)} %pad_maximum_fusion.5), channel_id=1, source_target_pairs={{0,34},{1,37},{2,36},{3,39},{4,38},{5,33},{6,32},{7,35},{8,42},{9,... | collective-permute-start | bytes 196616 | tf_op jit(solution)/shard_map/ppermute | solution.py:51
  113.8 7.8 %collective-permute-start.31 = (bf16[2,64,256]{2,1,0:T(8,128)(2,1)S(1)}, bf16[2,64,256]{2,1,0:T(8,128)(2,1)S(1)}, u32[]{:S(2)}, u32[]{:S(2)}) collective-permute-start(bf16[2,64,256]{2,1,0:T(8,128)(2,1)S(1)} %pad_maximum_fusion.7), channel_id=1, source_target_pairs={{0,32},{1,39},{2,34},{3,33},{4,36},{5,35},{6,38},{7,37},{8,40},{9,... | collective-permute-start | bytes 196616 | tf_op jit(solution)/shard_map/ppermute | solution.py:51
  (14 other events, 91.4 us)

commit v6 on v3

--- a/solution.py
+++ b/solution.py
@@ -57,6 +57,45 @@
 
 def nn(a, b):
     return lax.dot_general(a, b, (((1,), (0,)), ((), ())), preferred_element_type=F32)
+
+
+def states_kernel(pos, local, other, states, mine):
+    for core in range(2):
+
+        @pl.when(pos[3] == core)
+        def _():
+            own, par = slice(core * 128, core * 128 + 128), slice(128 - core * 128, 256 - core * 128)
+            for half in range(2):
+                states[half, :, own] = local[half * 64 : half * 64 + 64]
+                states[half, :, par] = other[half * 64 : half * 64 + 64]
+            mine[:, own] = local[core * 64 : core * 64 + 64]
+            mine[:, par] = other[core * 64 : core * 64 + 64]
+
+
+def ends_kernel(pos, r3, r2, r1, p0, p1, p2, p3, across, kept, passed):
+    both = r3[...].astype(F32) + r2[...].astype(F32) + r1[...].astype(F32)
+    mine = across[...].astype(F32)
+    for p in (p0, p1, p2, p3):
+        mine += p[0].astype(F32)
+    sums = (both[0] + mine, both[1])
+    for core in range(2):
+
+        @pl.when(pos[3] == core)
+        def _():
+            for half in range(2):
+                kept[half] = sums[half][:, core * 128 : core * 128 + 128]
+                passed[half] = sums[half][:, 128 - core * 128 : 256 - core * 128].astype(BF)
+
+
+def result_kernel(pos, kept, passed, out):
+    for half in range(2):
+        total_half = (kept[half] + passed[1 - half].astype(F32)).astype(BF)
+        for core in range(2):
+            at = 64 * (half if core == 0 else 1 - half)
+
+            @pl.when(pos[3] == core)
+            def _():
+                out[0, at : at + 64] = total_half
 
 
 def slot_of(c, z, zh, zl):
@@ -265,7 +304,7 @@
         out_specs=out_specs,
         out_shape=[jax.ShapeDtypeStruct(s, d) for s, d in outs],
         scratch_shapes=scratch,
-        compiler_params=pltpu.CompilerParams(vmem_limit_bytes=20 * 2**20),
+        compiler_params=pltpu.CompilerParams(vmem_limit_bytes=12 * 2**20),
     )
 
 
@@ -308,7 +347,7 @@
         ),
         out_shape=[jax.ShapeDtypeStruct((1, 8, 512, 128), BF)] * 2
         + [jax.ShapeDtypeStruct((8, 64, 256), BF)] * 2,
-        compiler_params=pltpu.CompilerParams(vmem_limit_bytes=24 * 2**20),
+        compiler_params=pltpu.CompilerParams(vmem_limit_bytes=12 * 2**20),
         name="attend",
     )(pos, lens, queries, d_context, keep, recv)
 
@@ -325,15 +364,14 @@
 
     local = enc_final[0]
     other = shift(local, dc=1)
-    states = jnp.where(
-        first, jnp.concatenate([local, other], 1), jnp.concatenate([other, local], 1)
-    ).reshape(2, 64, 256)
+    states, mine = whole(
+        states_kernel, [VMEM] * 2, [((2, 64, 256), BF), ((64, 256), BF)], [VMEM] * 2, []
+    )(pos, local, other)
 
     def halves(v, axis):
         lower, upper = lax.index_in_dim(v, 0, axis, False), lax.index_in_dim(v, 1, axis, False)
         return jnp.where(first, lower, upper), jnp.where(first, upper, lower)
 
-    mine, _ = halves(states, 0)
     across = shift(mine, dz=4)
     got = []
     for k in (3, 2, 1):
@@ -390,24 +428,22 @@
     got = [low[0]]
     for k in (1, 3, 2):
         got.append(cross((low + high)[k], k, 1))
-    got[0], weight_grad = lax.optimization_barrier((got[0], weight_grad))
     passed = [total([p[8 - k] for p in got]) for k in (3, 2, 1)]
     passed = shift(jnp.stack(passed), dc=1)
     across = shift(total([p[4] for p in got]), dz=4)
     got_z = []
     for i, k in enumerate((3, 2, 1)):
         both = jnp.stack([total([p[k] for p in got]), passed[i]])
-        got_z.append(rise(both, k).astype(F32))
-    both = got_z[0] + got_z[1] + got_z[2]
-    mine = functools.reduce(lambda p, q: p + q, [p[0].astype(F32) for p in got])
-    both = jnp.stack([both[0] + mine + across.astype(F32), both[1]]).reshape(2, 64, 2, 128)
-    kept, passed = halves(both, 2)
-    passed = shift(passed.astype(BF), dc=1).astype(F32)
-    kept, far_half = (kept[0] + passed[1]).astype(BF), (kept[1] + passed[0]).astype(BF)
-    enc_grad = jnp.where(
-        first, jnp.concatenate([kept, far_half], 0), jnp.concatenate([far_half, kept], 0)
-    )
-    return context, query_grad, weight_grad, enc_grad[None]
+        got_z.append(rise(both, k))
+    got_z[0], weight_grad = lax.optimization_barrier((got_z[0], weight_grad))
+    kept, passed = whole(
+        ends_kernel, [VMEM] * 8, [((2, 64, 128), F32), ((2, 64, 128), BF)], [VMEM] * 2, []
+    )(pos, *got_z, *got, across)
+    passed = shift(passed, dc=1)
+    (enc_grad,) = whole(
+        result_kernel, [VMEM] * 2, [((1, 128, 128), BF)], [VMEM], []
+    )(pos, kept, passed)
+    return context, query_grad, weight_grad, enc_grad
 
 
 def solution(mesh):

time: 138 us -> 127 us (0.920)
  the two profiles are of different devices: /device:TPU:1 before, /device:TPU:8 now
where the time goes in v6:
time: 127 us; the launch traced here: 125 us
  starting transfers between devices  56.7 us (45%)
  Pallas kernels  29.6 us (23%)
  waiting for transfers between devices  28.8 us (23%)
  local copies, waits for them, and re-layouts  5.97 us (5%)
  other arithmetic  2.56 us (2%)
    ppermute x18, starting transfers between devices, cross(): return lax.ppermute(value, AXES, pairs)  31.7 us
    ppermute x18, waiting for transfers between devices, cross(): return lax.ppermute(value, AXES, pairs)  18.5 us
    ppermute x6, starting transfers between devices, rise(): return lax.ppermute(value, AXES, pairs)  15.4 us
    ppermute x10, starting transfers between devices, shift(): return lax.ppermute(value, AXES, pairs)  9.56 us
    ppermute x10, waiting for transfers between devices, shift(): return lax.ppermute(value, AXES, pairs)  8.91 us
    pallas_call x3, Pallas kernels, project(): whole(functools.partial(project_kernel, which, first, last), [VMEM] * (2...  7.53 us
    pallas_call x3, Pallas kernels, spread(): whole(functools.partial(spread_kernel, which, len(after)), [VMEM] * 4 + [...  7.42 us
    pallas_call x1, Pallas kernels, shards(): whole(weight_kernel, [VMEM] * 10 + [HBM], [((16, 256, 256), BF)] * 2, [VM...  6.51 us
  transfers between devices with their start and end apart: 34, of which 15 were waited for; matrix products, arithmetic and copies ran while one was open for 6% of the time, Pallas kernels for 14%

profile of v6, /device:TPU:8, one launch (start us, length us, event | category | flops | bytes accessed | tf_op | source)
XLA Modules:
  0.0 124.7 jit_solution(17410610854561164502)
XLA Ops:
  5.5 3.3 %collective-permute-start.2 = (bf16[2,64,256]{2,1,0:T(8,128)(2,1)S(1)}, bf16[2,64,256]{2,1,0:T(8,128)(2,1)S(1)}, u32[]{:S(2)}, u32[]{:S(2)}) collective-permute-start(bf16[2,64,256]{2,1,0:T(8,128)(2,1)S(1)} %get-tuple-element.29), channel_id=1, source_target_pairs={{0,2},{1,7},{2,4},{3,1},{4,6},{5,3},{6,0},{7,5},{8,10},{9,15},{10,... | collective-permute-start | bytes 196616 | tf_op jit(solution)/shard_map/ppermute | solution.py:51
  8.7 4.0 %collective-permute-start.1 = (bf16[2,64,256]{2,1,0:T(8,128)(2,1)S(1)}, bf16[2,64,256]{2,1,0:T(8,128)(2,1)S(1)}, u32[]{:S(2)}, u32[]{:S(2)}) collective-permute-start(bf16[2,64,256]{2,1,0:T(8,128)(2,1)S(1)} %get-tuple-element.29), channel_id=1, source_target_pairs={{0,34},{1,37},{2,36},{3,39},{4,38},{5,33},{6,32},{7,35},{8,42},{9,... | collective-permute-start | bytes 196616 | tf_op jit(solution)/shard_map/ppermute | solution.py:51
  12.8 3.2 %reshape.57.refs_2_.refs_4_.wo = bf16[16,256,256]{2,1,0:T(8,128)(2,1)S(1)} reshape(bf16[1,4096,2,128]{3,2,1,0:T(2,128)(2,1)} %param.7) | data formatting | bytes 4194304 | tf_op jit(solution)/shard_map/reshape | solution.py:383
  17.1 4.4 %collective-permute-start.4 = (bf16[64,256]{1,0:T(8,128)(2,1)S(1)}, bf16[64,256]{1,0:T(8,128)(2,1)S(1)}, u32[]{:S(2)}, u32[]{:S(2)}) collective-permute-start(bf16[64,256]{1,0:T(8,128)(2,1)S(1)} %get-tuple-element.28), channel_id=1, source_target_pairs={{0,4},{1,5},{2,6},{3,7},{4,0},{5,1},{6,2},{7,3},{8,12},{9,13},{10,... | collective-permute-start | bytes 98312 | tf_op jit(solution)/shard_map/ppermute | solution.py:34
  21.5 3.5 %collective-permute-done.4 = bf16[64,256]{1,0:T(8,128)(2,1)S(1)} collective-permute-done((bf16[64,256]{1,0:T(8,128)(2,1)S(1)}, bf16[64,256]{1,0:T(8,128)(2,1)S(1)}, u32[]{:S(2)}, u32[]{:S(2)}) %collective-permute-start.4) | collective-permute-done | bytes 32800 | tf_op jit(solution)/shard_map/ppermute | solution.py:34
  33.1 3.5 %collective-permute-done.9 = bf16[8,64,256]{2,1,0:T(8,128)(2,1)S(1)} collective-permute-done((bf16[8,64,256]{2,1,0:T(8,128)(2,1)S(1)}, bf16[8,64,256]{2,1,0:T(8,128)(2,1)S(1)}, u32[]{:S(2)}, u32[]{:S(2)}) %collective-permute-start.9) | collective-permute-done | bytes 262176 | tf_op jit(solution)/shard_map/ppermute | solution.py:43
  36.6 2.8 %collective-permute-start.11 = (bf16[2,8,64,256]{3,2,1,0:T(8,128)(2,1)S(1)}, bf16[2,8,64,256]{3,2,1,0:T(8,128)(2,1)S(1)}, u32[]{:S(2)}, u32[]{:S(2)}) collective-permute-start(bf16[2,8,64,256]{3,2,1,0:T(8,128)(2,1)S(1)} %pad_maximum_fusion.1.refs_1_), channel_id=1, source_target_pairs={{0,192},{1,25},{2,194},{3,27},{4,196},{5,29},{6,198},{7,31},{8,200... | collective-permute-start | bytes 1572872 | tf_op jit(solution)/shard_map/ppermute | solution.py:43
  39.5 3.2 %collective-permute-start.15 = (bf16[2,8,64,256]{3,2,1,0:T(8,128)(2,1)S(1)}, bf16[2,8,64,256]{3,2,1,0:T(8,128)(2,1)S(1)}, u32[]{:S(2)}, u32[]{:S(2)}) collective-permute-start(bf16[2,8,64,256]{3,2,1,0:T(8,128)(2,1)S(1)} %pad_maximum_fusion.refs_0_), channel_id=1, source_target_pairs={{0,192},{1,25},{2,194},{3,27},{4,196},{5,29},{6,198},{7,31},{8,200... | collective-permute-start | bytes 1572872 | tf_op jit(solution)/shard_map/ppermute | solution.py:43
  42.7 3.5 %collective-permute-done.11.refs_3_.refs_7_ = bf16[2,8,64,256]{3,2,1,0:T(8,128)(2,1)S(1)} collective-permute-done((bf16[2,8,64,256]{3,2,1,0:T(8,128)(2,1)S(1)}, bf16[2,8,64,256]{3,2,1,0:T(8,128)(2,1)S(1)}, u32[]{:S(2)}, u32[]{:S(2)}) %collective-permute-start.11) | collective-permute-done | bytes 524320 | tf_op jit(solution)/shard_map/ppermute | solution.py:43
  46.2 3.7 %collective-permute-start.12 = (bf16[2,8,64,256]{3,2,1,0:T(8,128)(2,1)S(1)}, bf16[2,8,64,256]{3,2,1,0:T(8,128)(2,1)S(1)}, u32[]{:S(2)}, u32[]{:S(2)}) collective-permute-start(bf16[2,8,64,256]{3,2,1,0:T(8,128)(2,1)S(1)} %collective-permute-done.11.refs_3_.refs_7_), channel_id=1, source_target_pairs={{0,192},{1,25},{2,194},{3,27},{4,196},{5,29},{6,198},{7,31},{8,200... | collective-permute-start | bytes 1572872 | tf_op jit(solution)/shard_map/ppermute | solution.py:43
  49.9 3.2 %shard_map.85 = (bf16[16,256,256]{2,1,0:T(8,128)(2,1)S(1)}, f32[512,512]{1,0:T(8,128)S(1)}) custom-call(s32[4]{0:T(128)S(1)} %pad_add_fusion.pos, bf16[2,8,64,256]{3,2,1,0:T(8,128)(2,1)S(1)} %pad_maximum_fusion.refs_0_, bf16[2,8,64,256]{3,2,1,0:T(8,128)(2,1)S(1)} %pad_maximum_fusion.1.refs_1_, bf16[16,256,256]{2,1,0:T(8,128)(2,1)S(1)} %reshape.57.refs_2_.refs_4_.wo, ...), custom_call_target="tpu_custom_call" | custom-call | tf_op jit(solution)/shard_map/pallas_call | solution.py:318
  61.0 5.8 %attend.1 = (bf16[1,8,512,128]{3,2,1,0:T(8,128)(2,1)}, bf16[1,8,512,128]{3,2,1,0:T(8,128)(2,1)}, bf16[8,64,256]{2,1,0:T(8,128)(2,1)S(1)}, bf16[8,64,256]{2,1,0:T(8,128)(2,1)S(1)}) custom-call(s32[4]{0:T(128)S(1)} %pad_add_fusion.pos, s32[8]{0:T(128)S(1)} %copy-done.3, bf16[1,8,512,128]{3,2,1,0:T(8,128)(2,1)S(1)} %copy-done, ...), custom_call_target="tpu_custom_call" | custom-call | tf_op jit(solution)/shard_map/attend/pallas_call | solution.py:340
  68.3 2.5 %shard_map.88 = (bf16[2,8,64,256]{3,2,1,0:T(8,128)(2,1)S(1)}, bf16[2,8,64,256]{3,2,1,0:T(8,128)(2,1)S(1)}) custom-call(s32[4]{0:T(128)S(1)} %pad_add_fusion.pos, bf16[8,64,256]{2,1,0:T(8,128)(2,1)S(1)} %get-tuple-element.36.g_own.refs_8_, bf16[8,64,256]{2,1,0:T(8,128)(2,1)S(1)} %collective-permute-done.17.g_par.refs_9_, ...), custom_call_target="tpu_custom_call" | custom-call | tf_op jit(solution)/shard_map/pallas_call | solution.py:328
  70.8 3.8 %collective-permute-start.23 = (bf16[2,8,64,256]{3,2,1,0:T(8,128)(2,1)S(1)}, bf16[2,8,64,256]{3,2,1,0:T(8,128)(2,1)S(1)}, u32[]{:S(2)}, u32[]{:S(2)}) collective-permute-start(bf16[2,8,64,256]{3,2,1,0:T(8,128)(2,1)S(1)} %get-tuple-element.45), channel_id=1, source_target_pairs={{0,192},{1,25},{2,194},{3,27},{4,196},{5,29},{6,198},{7,31},{8,200... | collective-permute-start | bytes 1572872 | tf_op jit(solution)/shard_map/ppermute | solution.py:43
  74.6 2.5 %shard_map.89 = (bf16[2,8,64,256]{3,2,1,0:T(8,128)(2,1)S(1)}, bf16[2,8,64,256]{3,2,1,0:T(8,128)(2,1)S(1)}, bf16[2,8,64,256]{3,2,1,0:T(8,128)(2,1)S(1)}, bf16[2,8,64,256]{3,2,1,0:T(8,128)(2,1)S(1)}) custom-call(s32[4]{0:T(128)S(1)} %pad_add_fusion.pos, bf16[8,64,256]{2,1,0:T(8,128)(2,1)S(1)} %get-tuple-element.36.g_own.refs_8_, ...), custom_call_target="tpu_custom_call" | custom-call | tf_op jit(solution)/shard_map/pallas_call | solution.py:328
  77.1 3.3 %collective-permute-start.20 = (bf16[2,8,64,256]{3,2,1,0:T(8,128)(2,1)S(1)}, bf16[2,8,64,256]{3,2,1,0:T(8,128)(2,1)S(1)}, u32[]{:S(2)}, u32[]{:S(2)}) collective-permute-start(bf16[2,8,64,256]{3,2,1,0:T(8,128)(2,1)S(1)} %get-tuple-element.41), channel_id=1, source_target_pairs={{0,192},{1,25},{2,194},{3,27},{4,196},{5,29},{6,198},{7,31},{8,200... | collective-permute-start | bytes 1572872 | tf_op jit(solution)/shard_map/ppermute | solution.py:43
  81.4 4.0 %collective-permute-start.24 = (bf16[2,8,64,256]{3,2,1,0:T(8,128)(2,1)S(1)}, bf16[2,8,64,256]{3,2,1,0:T(8,128)(2,1)S(1)}, u32[]{:S(2)}, u32[]{:S(2)}) collective-permute-start(bf16[2,8,64,256]{3,2,1,0:T(8,128)(2,1)S(1)} %add_convert_fusion.1), channel_id=1, source_target_pairs={{0,192},{1,25},{2,194},{3,27},{4,196},{5,29},{6,198},{7,31},{8,200... | collective-permute-start | bytes 1572872 | tf_op jit(solution)/shard_map/ppermute | solution.py:43
  85.7 2.5 %shard_map.90 = (bf16[2,8,64,256]{3,2,1,0:T(8,128)(2,1)S(1)}, bf16[2,8,64,256]{3,2,1,0:T(8,128)(2,1)S(1)}) custom-call(s32[4]{0:T(128)S(1)} %pad_add_fusion.pos, bf16[8,64,256]{2,1,0:T(8,128)(2,1)S(1)} %get-tuple-element.36.g_own.refs_8_, bf16[8,64,256]{2,1,0:T(8,128)(2,1)S(1)} %collective-permute-done.17.g_par.refs_9_, ...), custom_call_target="tpu_custom_call" | custom-call | tf_op jit(solution)/shard_map/pallas_call | solution.py:328
  88.2 6.5 %shard_map.91 = (bf16[16,256,256]{2,1,0:T(8,128)(2,1)S(1)}, bf16[16,256,256]{2,1,0:T(8,128)(2,1)S(1)}) custom-call(s32[4]{0:T(128)S(1)} %pad_add_fusion.pos, bf16[2,8,64,256]{3,2,1,0:T(8,128)(2,1)S(1)} %pad_maximum_fusion.refs_0_, bf16[2,8,64,256]{3,2,1,0:T(8,128)(2,1)S(1)} %pad_maximum_fusion.1.refs_1_, ...), custom_call_target="tpu_custom_call" | custom-call | tf_op jit(solution)/shard_map/pallas_call | solution.py:420
  96.6 3.2 %collective-permute-start.25 = (bf16[8,64,256]{2,1,0:T(8,128)(2,1)S(1)}, bf16[8,64,256]{2,1,0:T(8,128)(2,1)S(1)}, u32[]{:S(2)}, u32[]{:S(2)}) collective-permute-start(bf16[8,64,256]{2,1,0:T(8,128)(2,1)S(1)} %get-tuple-element.54), channel_id=1, source_target_pairs={{0,24},{1,193},{2,26},{3,195},{4,28},{5,197},{6,30},{7,199},{8,0},... | collective-permute-start | bytes 786440 | tf_op jit(solution)/shard_map/ppermute | solution.py:43
  100.1 3.0 %collective-permute-done.26.p3 = bf16[8,64,256]{2,1,0:T(8,128)(2,1)S(1)} collective-permute-done((bf16[8,64,256]{2,1,0:T(8,128)(2,1)S(1)}, bf16[8,64,256]{2,1,0:T(8,128)(2,1)S(1)}, u32[]{:S(2)}, u32[]{:S(2)}) %collective-permute-start.26) | collective-permute-done | bytes 262176 | tf_op jit(solution)/shard_map/ppermute | solution.py:43
  103.1 2.7 %collective-permute-done.25.p2 = bf16[8,64,256]{2,1,0:T(8,128)(2,1)S(1)} collective-permute-done((bf16[8,64,256]{2,1,0:T(8,128)(2,1)S(1)}, bf16[8,64,256]{2,1,0:T(8,128)(2,1)S(1)}, u32[]{:S(2)}, u32[]{:S(2)}) %collective-permute-start.25) | collective-permute-done | bytes 262176 | tf_op jit(solution)/shard_map/ppermute | solution.py:43
  107.2 4.4 %collective-permute-start.32 = (bf16[64,256]{1,0:T(8,128)(2,1)S(1)}, bf16[64,256]{1,0:T(8,128)(2,1)S(1)}, u32[]{:S(2)}, u32[]{:S(2)}) collective-permute-start(bf16[64,256]{1,0:T(8,128)(2,1)S(1)} %get-tuple-element.56), channel_id=1, source_target_pairs={{0,4},{1,5},{2,6},{3,7},{4,0},{5,1},{6,2},{7,3},{8,12},{9,13},{10,... | collective-permute-start | bytes 98312 | tf_op jit(solution)/shard_map/ppermute | solution.py:34
  112.6 2.7 %collective-permute-start.30 = (bf16[2,64,256]{2,1,0:T(8,128)(2,1)S(1)}, bf16[2,64,256]{2,1,0:T(8,128)(2,1)S(1)}, u32[]{:S(2)}, u32[]{:S(2)}) collective-permute-start(bf16[2,64,256]{2,1,0:T(8,128)(2,1)S(1)} %pad_maximum_fusion.6), channel_id=1, source_target_pairs={{0,2},{1,7},{2,4},{3,1},{4,6},{5,3},{6,0},{7,5},{8,10},{9,15},{10,... | collective-permute-start | bytes 196616 | tf_op jit(solution)/shard_map/ppermute | solution.py:51
  (84 shorter events, 38.6 us)
Async XLA Ops:
  3.5 12.6 %collective-permute-start.3 = (bf16[2,64,256]{2,1,0:T(8,128)(2,1)S(1)}, bf16[2,64,256]{2,1,0:T(8,128)(2,1)S(1)}, u32[]{:S(2)}, u32[]{:S(2)}) collective-permute-start(bf16[2,64,256]{2,1,0:T(8,128)(2,1)S(1)} %get-tuple-element.29), channel_id=1, source_target_pairs={{0,32},{1,39},{2,34},{3,33},{4,36},{5,35},{6,38},{7,37},{8,40},{9,... | collective-permute-start | bytes 196616 | tf_op jit(solution)/shard_map/ppermute | solution.py:51
  5.5 10.6 %collective-permute-start.2 = (bf16[2,64,256]{2,1,0:T(8,128)(2,1)S(1)}, bf16[2,64,256]{2,1,0:T(8,128)(2,1)S(1)}, u32[]{:S(2)}, u32[]{:S(2)}) collective-permute-start(bf16[2,64,256]{2,1,0:T(8,128)(2,1)S(1)} %get-tuple-element.29), channel_id=1, source_target_pairs={{0,2},{1,7},{2,4},{3,1},{4,6},{5,3},{6,0},{7,5},{8,10},{9,15},{10,... | collective-permute-start | bytes 196616 | tf_op jit(solution)/shard_map/ppermute | solution.py:51
  8.7 8.2 %collective-permute-start.1 = (bf16[2,64,256]{2,1,0:T(8,128)(2,1)S(1)}, bf16[2,64,256]{2,1,0:T(8,128)(2,1)S(1)}, u32[]{:S(2)}, u32[]{:S(2)}) collective-permute-start(bf16[2,64,256]{2,1,0:T(8,128)(2,1)S(1)} %get-tuple-element.29), channel_id=1, source_target_pairs={{0,34},{1,37},{2,36},{3,39},{4,38},{5,33},{6,32},{7,35},{8,42},{9,... | collective-permute-start | bytes 196616 | tf_op jit(solution)/shard_map/ppermute | solution.py:51
  15.9 33.9 %collective-permute-start.13 = (bf16[16,256,256]{2,1,0:T(8,128)(2,1)S(1)}, bf16[16,256,256]{2,1,0:T(8,128)(2,1)}, u32[]{:S(2)}, u32[]{:S(2)}) collective-permute-start(bf16[16,256,256]{2,1,0:T(8,128)(2,1)S(1)} %reshape.57.refs_2_.refs_4_.wo), channel_id=1, source_target_pairs={{0,1},{1,0},{2,3},{3,2},{4,5},{5,4},{6,7},{7,6},{8,9},{9,8},{10,11... | collective-permute-start | bytes 6291464 | tf_op jit(solution)/shard_map/ppermute | solution.py:34
  17.0 8.0 %collective-permute-start.5 = (bf16[3,64,256]{2,1,0:T(8,128)(2,1)S(1)}, bf16[3,64,256]{2,1,0:T(8,128)(2,1)S(1)}, u32[]{:S(2)}, u32[]{:S(2)}) collective-permute-start(bf16[3,64,256]{2,1,0:T(8,128)(2,1)S(1)} %get-tuple-element.66), channel_id=1, source_target_pairs={{0,1},{1,0},{2,3},{3,2},{4,5},{5,4},{6,7},{7,6},{8,9},{9,8},{10,11... | collective-permute-start | bytes 294920 | tf_op jit(solution)/shard_map/ppermute | solution.py:34
  27.1 9.4 %collective-permute-start.9 = (bf16[8,64,256]{2,1,0:T(8,128)(2,1)S(1)}, bf16[8,64,256]{2,1,0:T(8,128)(2,1)S(1)}, u32[]{:S(2)}, u32[]{:S(2)}) collective-permute-start(bf16[8,64,256]{2,1,0:T(8,128)(2,1)S(1)} %get-tuple-element.64), channel_id=1, source_target_pairs={{0,16},{1,129},{2,18},{3,131},{4,20},{5,133},{6,22},{7,135},{8,24}... | collective-permute-start | bytes 786440 | tf_op jit(solution)/shard_map/ppermute | solution.py:43
  31.5 11.2 %collective-permute-start.7 = (bf16[2,8,64,256]{3,2,1,0:T(8,128)(2,1)S(1)}, bf16[2,8,64,256]{3,2,1,0:T(8,128)(2,1)S(1)}, u32[]{:S(2)}, u32[]{:S(2)}) collective-permute-start(bf16[2,8,64,256]{3,2,1,0:T(8,128)(2,1)S(1)} %pad_maximum_fusion.refs_0_), channel_id=1, source_target_pairs={{0,64},{1,9},{2,66},{3,11},{4,68},{5,13},{6,70},{7,15},{8,72},{9,1... | collective-permute-start | bytes 1572872 | tf_op jit(solution)/shard_map/ppermute | solution.py:43
  36.6 9.5 %collective-permute-start.11 = (bf16[2,8,64,256]{3,2,1,0:T(8,128)(2,1)S(1)}, bf16[2,8,64,256]{3,2,1,0:T(8,128)(2,1)S(1)}, u32[]{:S(2)}, u32[]{:S(2)}) collective-permute-start(bf16[2,8,64,256]{3,2,1,0:T(8,128)(2,1)S(1)} %pad_maximum_fusion.1.refs_1_), channel_id=1, source_target_pairs={{0,192},{1,25},{2,194},{3,27},{4,196},{5,29},{6,198},{7,31},{8,200... | collective-permute-start | bytes 1572872 | tf_op jit(solution)/shard_map/ppermute | solution.py:43
  39.5 13.6 %collective-permute-start.14 = (bf16[2,8,64,256]{3,2,1,0:T(8,128)(2,1)S(1)}, bf16[2,8,64,256]{3,2,1,0:T(8,128)(2,1)S(1)}, u32[]{:S(2)}, u32[]{:S(2)}) collective-permute-start(bf16[2,8,64,256]{3,2,1,0:T(8,128)(2,1)S(1)} %pad_maximum_fusion.1.refs_1_), channel_id=1, source_target_pairs={{0,64},{1,9},{2,66},{3,11},{4,68},{5,13},{6,70},{7,15},{8,72},{9,1... | collective-permute-start | bytes 1572872 | tf_op jit(solution)/shard_map/ppermute | solution.py:43
  39.5 13.6 %collective-permute-start.15 = (bf16[2,8,64,256]{3,2,1,0:T(8,128)(2,1)S(1)}, bf16[2,8,64,256]{3,2,1,0:T(8,128)(2,1)S(1)}, u32[]{:S(2)}, u32[]{:S(2)}) collective-permute-start(bf16[2,8,64,256]{3,2,1,0:T(8,128)(2,1)S(1)} %pad_maximum_fusion.refs_0_), channel_id=1, source_target_pairs={{0,192},{1,25},{2,194},{3,27},{4,196},{5,29},{6,198},{7,31},{8,200... | collective-permute-start | bytes 1572872 | tf_op jit(solution)/shard_map/ppermute | solution.py:43
  42.7 12.8 %collective-permute-start.8 = (bf16[2,8,64,256]{3,2,1,0:T(8,128)(2,1)S(1)}, bf16[2,8,64,256]{3,2,1,0:T(8,128)(2,1)S(1)}, u32[]{:S(2)}, u32[]{:S(2)}) collective-permute-start(bf16[2,8,64,256]{3,2,1,0:T(8,128)(2,1)S(1)} %collective-permute-done.7.refs_0_.refs_2_), channel_id=1, source_target_pairs={{0,64},{1,9},{2,66},{3,11},{4,68},{5,13},{6,70},{7,15},{8,72},{9,1... | collective-permute-start | bytes 1572872 | tf_op jit(solution)/shard_map/ppermute | solution.py:43
  46.2 11.2 %collective-permute-start.12 = (bf16[2,8,64,256]{3,2,1,0:T(8,128)(2,1)S(1)}, bf16[2,8,64,256]{3,2,1,0:T(8,128)(2,1)S(1)}, u32[]{:S(2)}, u32[]{:S(2)}) collective-permute-start(bf16[2,8,64,256]{3,2,1,0:T(8,128)(2,1)S(1)} %collective-permute-done.11.refs_3_.refs_7_), channel_id=1, source_target_pairs={{0,192},{1,25},{2,194},{3,27},{4,196},{5,29},{6,198},{7,31},{8,200... | collective-permute-start | bytes 1572872 | tf_op jit(solution)/shard_map/ppermute | solution.py:43
  70.8 10.5 %collective-permute-start.23 = (bf16[2,8,64,256]{3,2,1,0:T(8,128)(2,1)S(1)}, bf16[2,8,64,256]{3,2,1,0:T(8,128)(2,1)S(1)}, u32[]{:S(2)}, u32[]{:S(2)}) collective-permute-start(bf16[2,8,64,256]{3,2,1,0:T(8,128)(2,1)S(1)} %get-tuple-element.45), channel_id=1, source_target_pairs={{0,192},{1,25},{2,194},{3,27},{4,196},{5,29},{6,198},{7,31},{8,200... | collective-permute-start | bytes 1572872 | tf_op jit(solution)/shard_map/ppermute | solution.py:43
  74.6 10.9 %collective-permute-start.18 = (bf16[2,8,64,256]{3,2,1,0:T(8,128)(2,1)S(1)}, bf16[2,8,64,256]{3,2,1,0:T(8,128)(2,1)S(1)}, u32[]{:S(2)}, u32[]{:S(2)}) collective-permute-start(bf16[2,8,64,256]{3,2,1,0:T(8,128)(2,1)S(1)} %get-tuple-element.38.refs_0_), channel_id=1, source_target_pairs={{0,64},{1,9},{2,66},{3,11},{4,68},{5,13},{6,70},{7,15},{8,72},{9,1... | collective-permute-start | bytes 1572872 | tf_op jit(solution)/shard_map/ppermute | solution.py:43
  77.1 17.7 %collective-permute-start.22 = (bf16[2,8,64,256]{3,2,1,0:T(8,128)(2,1)S(1)}, bf16[2,8,64,256]{3,2,1,0:T(8,128)(2,1)S(1)}, u32[]{:S(2)}, u32[]{:S(2)}) collective-permute-start(bf16[2,8,64,256]{3,2,1,0:T(8,128)(2,1)S(1)} %get-tuple-element.43), channel_id=1, source_target_pairs={{0,64},{1,9},{2,66},{3,11},{4,68},{5,13},{6,70},{7,15},{8,72},{9,1... | collective-permute-start | bytes 1572872 | tf_op jit(solution)/shard_map/ppermute | solution.py:43
  77.1 22.6 %collective-permute-start.20 = (bf16[2,8,64,256]{3,2,1,0:T(8,128)(2,1)S(1)}, bf16[2,8,64,256]{3,2,1,0:T(8,128)(2,1)S(1)}, u32[]{:S(2)}, u32[]{:S(2)}) collective-permute-start(bf16[2,8,64,256]{3,2,1,0:T(8,128)(2,1)S(1)} %get-tuple-element.41), channel_id=1, source_target_pairs={{0,192},{1,25},{2,194},{3,27},{4,196},{5,29},{6,198},{7,31},{8,200... | collective-permute-start | bytes 1572872 | tf_op jit(solution)/shard_map/ppermute | solution.py:43
  81.4 13.4 %collective-permute-start.24 = (bf16[2,8,64,256]{3,2,1,0:T(8,128)(2,1)S(1)}, bf16[2,8,64,256]{3,2,1,0:T(8,128)(2,1)S(1)}, u32[]{:S(2)}, u32[]{:S(2)}) collective-permute-start(bf16[2,8,64,256]{3,2,1,0:T(8,128)(2,1)S(1)} %add_convert_fusion.1), channel_id=1, source_target_pairs={{0,192},{1,25},{2,194},{3,27},{4,196},{5,29},{6,198},{7,31},{8,200... | collective-permute-start | bytes 1572872 | tf_op jit(solution)/shard_map/ppermute | solution.py:43
  85.6 14.1 %collective-permute-start.19 = (bf16[2,8,64,256]{3,2,1,0:T(8,128)(2,1)S(1)}, bf16[2,8,64,256]{3,2,1,0:T(8,128)(2,1)S(1)}, u32[]{:S(2)}, u32[]{:S(2)}) collective-permute-start(bf16[2,8,64,256]{3,2,1,0:T(8,128)(2,1)S(1)} %add_convert_fusion.2), channel_id=1, source_target_pairs={{0,64},{1,9},{2,66},{3,11},{4,68},{5,13},{6,70},{7,15},{8,72},{9,1... | collective-permute-start | bytes 1572872 | tf_op jit(solution)/shard_map/ppermute | solution.py:43
  94.7 23.6 %collective-permute-start.29 = (bf16[16,256,256]{2,1,0:T(8,128)(2,1)S(1)}, bf16[16,256,256]{2,1,0:T(8,128)(2,1)S(1)}, u32[]{:S(2)}, u32[]{:S(2)}) collective-permute-start(bf16[16,256,256]{2,1,0:T(8,128)(2,1)S(1)} %get-tuple-element.47), channel_id=1, source_target_pairs={{0,1},{1,0},{2,3},{3,2},{4,5},{5,4},{6,7},{7,6},{8,9},{9,8},{10,11... | collective-permute-start | bytes 6291464 | tf_op jit(solution)/shard_map/ppermute | solution.py:34
  95.1 8.1 %collective-permute-start.26 = (bf16[8,64,256]{2,1,0:T(8,128)(2,1)S(1)}, bf16[8,64,256]{2,1,0:T(8,128)(2,1)S(1)}, u32[]{:S(2)}, u32[]{:S(2)}) collective-permute-start(bf16[8,64,256]{2,1,0:T(8,128)(2,1)S(1)} %get-tuple-element.55), channel_id=1, source_target_pairs={{0,16},{1,129},{2,18},{3,131},{4,20},{5,133},{6,22},{7,135},{8,24}... | collective-permute-start | bytes 786440 | tf_op jit(solution)/shard_map/ppermute | solution.py:43
  96.6 9.2 %collective-permute-start.25 = (bf16[8,64,256]{2,1,0:T(8,128)(2,1)S(1)}, bf16[8,64,256]{2,1,0:T(8,128)(2,1)S(1)}, u32[]{:S(2)}, u32[]{:S(2)}) collective-permute-start(bf16[8,64,256]{2,1,0:T(8,128)(2,1)S(1)} %get-tuple-element.54), channel_id=1, source_target_pairs={{0,24},{1,193},{2,26},{3,195},{4,28},{5,197},{6,30},{7,199},{8,0},... | collective-permute-start | bytes 786440 | tf_op jit(solution)/shard_map/ppermute | solution.py:43
  107.2 13.9 %collective-permute-start.32 = (bf16[64,256]{1,0:T(8,128)(2,1)S(1)}, bf16[64,256]{1,0:T(8,128)(2,1)S(1)}, u32[]{:S(2)}, u32[]{:S(2)}) collective-permute-start(bf16[64,256]{1,0:T(8,128)(2,1)S(1)} %get-tuple-element.56), channel_id=1, source_target_pairs={{0,4},{1,5},{2,6},{3,7},{4,0},{5,1},{6,2},{7,3},{8,12},{9,13},{10,... | collective-permute-start | bytes 98312 | tf_op jit(solution)/shard_map/ppermute | solution.py:34
  111.6 9.4 %collective-permute-start.28 = (bf16[2,64,256]{2,1,0:T(8,128)(2,1)S(1)}, bf16[2,64,256]{2,1,0:T(8,128)(2,1)S(1)}, u32[]{:S(2)}, u32[]{:S(2)}) collective-permute-start(bf16[2,64,256]{2,1,0:T(8,128)(2,1)S(1)} %pad_maximum_fusion.5), channel_id=1, source_target_pairs={{0,34},{1,37},{2,36},{3,39},{4,38},{5,33},{6,32},{7,35},{8,42},{9,... | collective-permute-start | bytes 196616 | tf_op jit(solution)/shard_map/ppermute | solution.py:51
  112.6 8.5 %collective-permute-start.30 = (bf16[2,64,256]{2,1,0:T(8,128)(2,1)S(1)}, bf16[2,64,256]{2,1,0:T(8,128)(2,1)S(1)}, u32[]{:S(2)}, u32[]{:S(2)}) collective-permute-start(bf16[2,64,256]{2,1,0:T(8,128)(2,1)S(1)} %pad_maximum_fusion.6), channel_id=1, source_target_pairs={{0,2},{1,7},{2,4},{3,1},{4,6},{5,3},{6,0},{7,5},{8,10},{9,15},{10,... | collective-permute-start | bytes 196616 | tf_op jit(solution)/shard_map/ppermute | solution.py:51
  (14 other events, 60.9 us)
